TPU v7x, 32 devices: a whole 2x2x4 slice. The times are simulated.
32 devices in a mesh: groups: 2 (over y), gx: 4 (over z), gy: 2 (over x), gz: 2 (over core).
Axes of the slice: x: 2, y: 2, z: 4, core: 2. Of those that a mesh axis runs over, the one named last changes fastest.
Arguments:
- features: bfloat16 [32, 8, 32, 128], P(('groups', 'gx'), 'gy', 'gz'), parts along dimension 0, may hold values from -6 to 6
- scales: bfloat16 [32, 8, 32, 128], P(('groups', 'gx'), 'gy', 'gz'), parts along dimension 0, may hold values from 0.29882812 to 3
- occupancy: int32 [8, 2, 8], P(('groups', 'gx'), 'gy', 'gz'), parts along dimension 0, may hold values 0 or 1
- kernel: bfloat16 [62, 128, 128], replicated, may hold values from -0.0625 to 0.0625
- gamma: float32 [128, 128], replicated, may hold values from 0 to 0.015625
- beta: float32 [128], replicated, may hold values from 0.5 to 2
Outputs:
- grad_features: bfloat16 [32, 8, 32, 128], P(('groups', 'gx'), 'gy', 'gz'), parts along dimension 0
- grad_kernel: float32 [2031616], P(('groups', 'gx', 'gy', 'gz')), parts along dimension 0
- grad_gamma: float32 [256, 128], P('groups'), parts along dimension 0
- grad_beta: float32 [256], P('groups'), parts along dimension 0
There are 2 independent parts, one for each index of `groups`. A program takes and returns all parts, laid end to end along the dimension named above; an argument that names none is the same for every part. Nothing has to cross between parts.
All inputs are finite; a program needn't handle non-finite values. No bound on the sum of `occupancy` on one device may be relied on, other than what follows from the above.
Results may differ from a plain program's by a relative error of at most 0.0039.
The roundings to bfloat16 on the way count: a program that leaves them out, or rounds other values in their place, can miss the bound.
Values may be sent and summed in bfloat16 or wider, within the bound.
No kernel may reach another device: no remote copies, remote signals or barrier semaphores. Data moves between devices by JAX's collectives and lax.ppermute only.
A program may use at most 64 MiB of HBM per device.

v0:
```python
import math

import jax
import jax.numpy as jnp
from jax import lax
from jax.sharding import PartitionSpec as P

OB = 4


def padded_2(shard, sides, width):
    for axis, dim in sides:
        size, length = (lax.axis_size(axis), shard.shape[dim])
        up = [(i, (i + 1) % size) for i in range(size - 1)]
        down = [(j, i) for i, j in up]
        last = lax.slice_in_dim(shard, length - width, length, axis=dim)
        leading = lax.slice_in_dim(shard, 0, width, axis=dim)
        before = lax.ppermute(last, axis, up)
        after = lax.ppermute(leading, axis, down)
        shard = jnp.concatenate([before, shard, after], axis=dim)
    return shard


def from_behind(value, axis, steps):
    count = lax.axis_size(axis)
    leading, last = (max(0, -steps), min(count, count - steps))
    return lax.ppermute(value, axis, [(source, source + steps) for source in range(leading, last)])


def causal_offsets():
    result = []
    for along_x in range(-2, 3):
        for along_y in range(-2, 3):
            for along_z in range(-2, 3):
                if (along_x, along_y, along_z) < (0, 0, 0):
                    result.append((along_x, along_y, along_z))
    return result


def tap_groups():
    groups = []
    for number, offset in enumerate(causal_offsets()):
        if groups and groups[-1][0] == offset[0] and (groups[-1][1] == offset[1]):
            groups[-1][3] += 1
        else:
            groups.append([offset[0], offset[1], offset[2], 1, number])
    return groups


def expand_blocks(occupancy, edge):
    blocks_x, blocks_y, blocks_z = occupancy.shape
    grown = jnp.broadcast_to(
        occupancy[:, None, :, None, :, None], (blocks_x, edge, blocks_y, edge, blocks_z, edge)
    )
    return grown.reshape(-1, 1).astype(jnp.float32)


def forward_patch(padded, along_x, along_y, start_z, count, extent):
    size_x, size_y, size_z = extent
    pieces = [
        padded[
            2 + along_x : 2 + along_x + size_x,
            2 + along_y : 2 + along_y + size_y,
            2 + along_z : 2 + along_z + size_z,
        ]
        for along_z in range(start_z, start_z + count)
    ]
    return jnp.concatenate(pieces, axis=3).reshape(size_x * size_y * size_z, -1)


def context_mean(padded, kernel, extent):
    channels = kernel.shape[1]
    total = jnp.zeros((extent[0] * extent[1] * extent[2], channels), jnp.float32)
    for along_x, along_y, start_z, count, first_tap in tap_groups():
        patch = forward_patch(padded, along_x, along_y, start_z, count, extent)
        weights = kernel[first_tap : first_tap + count].reshape(count * channels, channels)
        total = total + jnp.dot(patch, weights, preferred_element_type=jnp.float32)
    return total


def context_transposed(padded, kernel, extent):
    size_x, size_y, size_z = extent
    channels = kernel.shape[1]
    total = jnp.zeros((size_x * size_y * size_z, channels), jnp.float32)
    for along_x, along_y, start_z, count, first_tap in tap_groups():
        pieces = [
            padded[
                -along_x : -along_x + size_x,
                2 - along_y : 2 - along_y + size_y,
                2 - along_z : 2 - along_z + size_z,
            ]
            for along_z in range(start_z, start_z + count)
        ]
        patch = jnp.concatenate(pieces, axis=3).reshape(size_x * size_y * size_z, -1)
        weights = jnp.transpose(kernel[first_tap : first_tap + count], (0, 2, 1)).reshape(
            count * channels, channels
        )
        total = total + jnp.dot(patch, weights, preferred_element_type=jnp.float32)
    return total


def kernel_terms(padded, mean_grad, extent):
    terms = []
    for along_x, along_y, start_z, count, first_tap in tap_groups():
        patch = forward_patch(padded, along_x, along_y, start_z, count, extent)
        terms.append(
            lax.dot_general(
                patch, mean_grad, (((0,), (0,)), ((), ())), preferred_element_type=jnp.float32
            )
        )
    return jnp.concatenate(terms, axis=0).reshape(-1)


def lower_sides_first(latent):
    widened = padded_2(latent, (("gy", 1), ("gz", 2)), 2)
    below = from_behind(widened[-2:], "gx", 1)
    return jnp.concatenate([below, widened], axis=0)


def upper_sides_first(grads):
    widened = padded_2(grads, (("gy", 1), ("gz", 2)), 2)
    above = from_behind(widened[:2], "gx", -1)
    return jnp.concatenate([widened, above], axis=0)


def local(features, scales, occupancy, kernel, gamma, beta):
    size_x, size_y, size_z, channels = features.shape
    extent = (size_x, size_y, size_z)
    voxels = size_x * size_y * size_z
    feats = features.astype(jnp.float32).reshape(voxels, channels)
    occupied = expand_blocks(occupancy, OB)
    energy = beta[None, :] + jnp.dot(
        feats * feats, gamma, precision=lax.Precision.HIGHEST, preferred_element_type=jnp.float32
    )
    inv_root = lax.rsqrt(energy)
    latent = (occupied * feats * inv_root).astype(jnp.bfloat16)
    latent_grid = latent.reshape(size_x, size_y, size_z, channels)
    padded = lower_sides_first(latent_grid)
    mean = context_mean(padded, kernel, extent)
    latent_f = latent.astype(jnp.float32)
    scale_f = scales.astype(jnp.float32).reshape(voxels, channels)
    inverse = 1.0 / (scale_f * scale_f)
    mean_grad = (occupied * (mean - latent_f) * inverse).astype(jnp.bfloat16)
    grad_grid = mean_grad.reshape(size_x, size_y, size_z, channels)
    grad_pad = upper_sides_first(grad_grid)
    context_grad = context_transposed(grad_pad, kernel, extent)
    latent_grad = occupied * (context_grad + (latent_f - mean) * inverse)
    weighted = latent_grad * feats * inv_root * inv_root * inv_root
    coupled = jnp.dot(
        weighted, gamma.T, precision=lax.Precision.HIGHEST, preferred_element_type=jnp.float32
    )
    grad_features = (
        (latent_grad * inv_root - feats * coupled)
        .astype(jnp.bfloat16)
        .reshape(size_x, size_y, size_z, channels)
    )
    kernel_local = kernel_terms(padded, mean_grad, extent) / voxels
    grad_kernel = lax.psum_scatter(
        kernel_local, ("gx", "gy", "gz"), scatter_dimension=0, tiled=True
    )
    factor = 0.5 / math.sqrt(voxels)
    gamma_local = -factor * jnp.dot(
        (feats * feats).T,
        weighted,
        precision=lax.Precision.HIGHEST,
        preferred_element_type=jnp.float32,
    )
    beta_local = -factor * jnp.sum(weighted, axis=0)
    grad_gamma, grad_beta = lax.psum((gamma_local, beta_local), ("gx", "gy", "gz"))
    return (grad_features, grad_kernel, grad_gamma, grad_beta)


def solution(mesh):
    return jax.shard_map(
        local,
        mesh=mesh,
        in_specs=(
            P(("groups", "gx"), "gy", "gz", None),
            P(("groups", "gx"), "gy", "gz", None),
            P(("groups", "gx"), "gy", "gz"),
            P(),
            P(),
            P(),
        ),
        out_specs=(
            P(("groups", "gx"), "gy", "gz", None),
            P(("groups", "gx", "gy", "gz")),
            P("groups", None),
            P("groups"),
        ),
        check_vma=False,
    )
```

profile of v0, /device:TPU:0, one launch (start us, length us, event | category | flops | bytes accessed | tf_op | source)
XLA Modules:
  0.0 195.3 jit_solution(11821745433101948663)
XLA Ops:
  8.1 1.2 fusion.12
  9.3 4.9 %collective-permute-start = (bf16[4,2,16,128]{3,2,1,0:T(8,128)(2,1)S(1)}, bf16[4,2,16,128]{3,2,1,0:T(8,128)(2,1)S(1)}, u32[]{:S(2)}, u32[]{:S(2)}) collective-permute-start(bf16[4,2,16,128]{3,2,1,0:T(8,128)(2,1)S(1)} %get-tuple-element.160), channel_id=1, source_target_pairs={{0,2},{1,3},{4,6},{5,7},{8,10},{9,11},{12,14},{13,15},{16,18},{17,... | collective-permute-start | bytes 98312 | tf_op jit(solution)/shard_map/ppermute | solution.py:18
  14.2 1.3 collective-permute-start.1
  15.5 2.1 %fusion.16 = (bf16[5,128,128]{2,1,0:T(8,128)(2,1)}, bf16[5,128,128]{2,1,0:T(8,128)(2,1)}, bf16[5,128,128]{2,1,0:T(8,128)(2,1)}, bf16[5,128,128]{2,1,0:T(8,128)(2,1)}, bf16[5,128,128]{2,1,0:T(8,128)(2,1)}) fusion(bf16[62,128,128]{2,1,0:T(8,128)(2,1)} %param.9), kind=kLoop, calls=%fused_computation.225 | loop fusion | bytes 1638400 | tf_op jit(solution)/shard_map/slice | solution.py:76
  17.7 3.0 %slice_bitcast_fusion.1 = (bf16[5,128,128]{1,2,0:T(8,128)(2,1)S(1)}, bf16[5,128,128]{1,2,0:T(8,128)(2,1)S(1)}, bf16[5,128,128]{1,2,0:T(8,128)(2,1)S(1)}, bf16[5,...) fusion(bf16[62,128,128]{2,1,0:T(8,128)(2,1)} %param.9), kind=kLoop, calls=%fused_computation.212 | loop fusion | bytes 5079040 | tf_op jit(solution)/shard_map/transpose | solution.py:95
  20.6 0.9 slice_bitcast_fusion
  22.2 1.3 collective-permute-start.3
  23.5 3.6 %collective-permute-start.2 = (bf16[4,8,2,128]{3,2,1,0:T(2,128)(2,1)}, bf16[4,8,2,128]{3,2,1,0:T(2,128)(2,1)}, u32[]{:S(2)}, u32[]{:S(2)}) collective-permute-start(bf16[4,8,2,128]{3,2,1,0:T(2,128)(2,1)} %get-tuple-element.153), channel_id=1, source_target_pairs={{0,1},{2,3},{4,5},{6,7},{8,9},{10,11},{12,13},{14,15},{16,17},{18,... | collective-permute-start | bytes 49160 | tf_op jit(solution)/shard_map/ppermute | solution.py:18
  27.9 0.8 copy.47
  28.7 0.8 copy.36
  29.5 0.8 copy.37
  30.3 0.8 copy.38
  31.2 0.8 copy.39
  33.2 0.7 pad_maximum_fusion.9
  34.0 3.5 %collective-permute-start.4 = (bf16[2,8,20,128]{3,2,1,0:T(8,128)(2,1)S(1)}, bf16[2,8,20,128]{3,2,1,0:T(8,128)(2,1)S(1)}, u32[]{:S(2)}, u32[]{:S(2)}) collective-permute-start(bf16[2,8,20,128]{3,2,1,0:T(8,128)(2,1)S(1)} %pad_maximum_fusion.9), channel_id=1, source_target_pairs={{0,4},{4,8},{8,12},{1,5},{5,9},{9,13},{2,6},{6,10},{10,14},{3,7},{... | collective-permute-start | bytes 245768 | tf_op jit(solution)/shard_map/ppermute | solution.py:27
  37.5 0.8 pad_maximum_fusion.1
  38.8 0.9 collective-permute-done.4
  39.7 0.8 maximum_maximum_fusion
  44.9 4.5 %collective-permute-start.5 = (bf16[4,2,16,128]{3,2,1,0:T(8,128)(2,1)S(1)}, bf16[4,2,16,128]{3,2,1,0:T(8,128)(2,1)S(1)}, u32[]{:S(2)}, u32[]{:S(2)}) collective-permute-start(bf16[4,2,16,128]{3,2,1,0:T(8,128)(2,1)S(1)} %get-tuple-element.158), channel_id=1, source_target_pairs={{0,2},{1,3},{4,6},{5,7},{8,10},{9,11},{12,14},{13,15},{16,18},{17,... | collective-permute-start | bytes 98312 | tf_op jit(solution)/shard_map/ppermute | solution.py:18
  49.4 1.3 collective-permute-start.6
  54.3 0.9 collective-permute-done.6
  55.3 1.3 collective-permute-start.7
  56.6 1.4 collective-permute-start.8
  58.0 2.2 %multiply_bitcast_fusion = f32[1015808]{0:T(1024)} fusion(f32[7936,128]{1,0:T(8,128)S(1)} %convolution_dynamic-update-slice_fusion.12), kind=kLoop, calls=%fused_computation | loop fusion | flops 1015808 | bytes 8126464 | tf_op jit(solution)/shard_map/div | solution.py:157
  60.3 1.5 collective-permute-start.9
  62.4 5.4 %collective-permute-done.9 = bf16[2,8,20,128]{3,2,1,0:T(8,128)(2,1)S(1)} collective-permute-done((bf16[2,8,20,128]{3,2,1,0:T(8,128)(2,1)S(1)}, bf16[2,8,20,128]{3,2,1,0:T(8,128)(2,1)S(1)}, u32[]{:S(2)}, u32[]{:S(2)}) %collective-permute-start.9) | collective-permute-done | bytes 81952 | tf_op jit(solution)/shard_map/ppermute | solution.py:27
  72.1 1.0 convolution_multiply_fusion.1
  74.4 34.5 %psum.15 = f32[128]{0:T(128)} all-reduce(f32[128]{0:T(128)S(1)} %broadcast_multiply_fusion), channel_id=1, replica_groups=mesh['groups'=2,'gx'=4,'gy'=2,'gz'=2] {'gx','gy','gz'}, use_global_device_ids=true, to_apply=%region_3.0 | all-reduce | flops 128 | bytes 1024 | tf_op jit(solution)/shard_map/psum | solution.py:169
  108.9 0.9 fusion.6
  109.8 75.5 %all-reduce.4.cloned.1.call-done = (f32[1015808]{0:T(1024)}, f32[128,128]{1,0:T(8,128)}) async-done(((f32[1015808]{0:T(1024)}, f32[128,128]{1,0:T(8,128)}), (f32[1015808]{0:T(1024)}, f32[128,128]{1,0:T(8,128)})) %all-reduce.4.cloned.1.call-update) | async-done | bytes 4128784
  185.3 1.7 dynamic-slice.1
  186.9 1.5 copy.159
  (135 shorter events, 16.9 us)
Async XLA Ops:
  7.2 0.9 copy-start
  7.2 178.1 %all-reduce.4.cloned.1.call-start = ((), (), s32[]{:S(2)}) async-start(), calls=%async_computation | async-start | bytes 8257536
  8.1 1.2 copy-start.15
  8.1 19.0 %copy-start.14 = (bf16[4,4,16,128]{3,2,1,0:T(8,128)(2,1)S(1)}, bf16[4,4,16,128]{3,2,1,0:T(8,128)(2,1)}, u32[]{:S(2)}) copy-start(bf16[4,4,16,128]{3,2,1,0:T(8,128)(2,1)} %param.7) | copy-start | bytes 196612
  9.3 12.2 %collective-permute-start = (bf16[4,2,16,128]{3,2,1,0:T(8,128)(2,1)S(1)}, bf16[4,2,16,128]{3,2,1,0:T(8,128)(2,1)S(1)}, u32[]{:S(2)}, u32[]{:S(2)}) collective-permute-start(bf16[4,2,16,128]{3,2,1,0:T(8,128)(2,1)S(1)} %get-tuple-element.160), channel_id=1, source_target_pairs={{0,2},{1,3},{4,6},{5,7},{8,10},{9,11},{12,14},{13,15},{16,18},{17,... | collective-permute-start | bytes 98312 | tf_op jit(solution)/shard_map/ppermute | solution.py:18
  14.2 7.3 %collective-permute-start.1 = (bf16[4,2,16,128]{3,2,1,0:T(8,128)(2,1)S(1)}, bf16[4,2,16,128]{3,2,1,0:T(8,128)(2,1)S(1)}, u32[]{:S(2)}, u32[]{:S(2)}) collective-permute-start(bf16[4,2,16,128]{3,2,1,0:T(8,128)(2,1)S(1)} %get-tuple-element.161), channel_id=1, source_target_pairs={{2,0},{3,1},{6,4},{7,5},{10,8},{11,9},{14,12},{15,13},{18,16},{19,... | collective-permute-start | bytes 98312 | tf_op jit(solution)/shard_map/ppermute | solution.py:19
  22.2 11.1 %collective-permute-start.3 = (bf16[4,8,2,128]{3,2,1,0:T(2,128)(2,1)}, bf16[4,8,2,128]{3,2,1,0:T(2,128)(2,1)S(1)}, u32[]{:S(2)}, u32[]{:S(2)}) collective-permute-start(bf16[4,8,2,128]{3,2,1,0:T(2,128)(2,1)} %get-tuple-element.152), channel_id=1, source_target_pairs={{1,0},{3,2},{5,4},{7,6},{9,8},{11,10},{13,12},{15,14},{17,16},{19,... | collective-permute-start | bytes 49160 | tf_op jit(solution)/shard_map/ppermute | solution.py:19
  23.5 9.8 %collective-permute-start.2 = (bf16[4,8,2,128]{3,2,1,0:T(2,128)(2,1)}, bf16[4,8,2,128]{3,2,1,0:T(2,128)(2,1)}, u32[]{:S(2)}, u32[]{:S(2)}) collective-permute-start(bf16[4,8,2,128]{3,2,1,0:T(2,128)(2,1)} %get-tuple-element.153), channel_id=1, source_target_pairs={{0,1},{2,3},{4,5},{6,7},{8,9},{10,11},{12,13},{14,15},{16,17},{18,... | collective-permute-start | bytes 49160 | tf_op jit(solution)/shard_map/ppermute | solution.py:18
  34.0 5.7 %collective-permute-start.4 = (bf16[2,8,20,128]{3,2,1,0:T(8,128)(2,1)S(1)}, bf16[2,8,20,128]{3,2,1,0:T(8,128)(2,1)S(1)}, u32[]{:S(2)}, u32[]{:S(2)}) collective-permute-start(bf16[2,8,20,128]{3,2,1,0:T(8,128)(2,1)S(1)} %pad_maximum_fusion.9), channel_id=1, source_target_pairs={{0,4},{4,8},{8,12},{1,5},{5,9},{9,13},{2,6},{6,10},{10,14},{3,7},{... | collective-permute-start | bytes 245768 | tf_op jit(solution)/shard_map/ppermute | solution.py:27
  38.4 3.2 %copy-start.7 = (bf16[5,128,128]{2,1,0:T(8,128)(2,1)S(1)}, bf16[5,128,128]{2,1,0:T(8,128)(2,1)}, u32[]{:S(2)}) copy-start(bf16[5,128,128]{2,1,0:T(8,128)(2,1)} %get-tuple-element.33) | copy-start | bytes 491524
  38.7 3.2 %copy-start.6 = (bf16[5,128,128]{2,1,0:T(8,128)(2,1)S(1)}, bf16[5,128,128]{2,1,0:T(8,128)(2,1)}, u32[]{:S(2)}) copy-start(bf16[5,128,128]{2,1,0:T(8,128)(2,1)} %get-tuple-element.32) | copy-start | bytes 491524
  40.5 1.6 copy-start.5
  40.6 1.8 copy-start.4
  40.6 2.0 %copy-start.2 = (bf16[5,128,128]{2,1,0:T(8,128)(2,1)S(1)}, bf16[5,128,128]{2,1,0:T(8,128)(2,1)}, u32[]{:S(2)}) copy-start(bf16[5,128,128]{2,1,0:T(8,128)(2,1)} %get-tuple-element.26) | copy-start | bytes 491524
  41.6 2.7 %copy-start.12 = (bf16[5,128,128]{2,1,0:T(8,128)(2,1)S(1)}, bf16[5,128,128]{2,1,0:T(8,128)(2,1)}, u32[]{:S(2)}) copy-start(bf16[5,128,128]{2,1,0:T(8,128)(2,1)} %get-tuple-element.29) | copy-start | bytes 491524
  41.6 2.7 %copy-start.16 = (f32[256]{0:T(256)S(1)}, f32[256]{0:T(256)}, u32[]{:S(2)}) copy-start(f32[256]{0:T(256)} %copy-done.15) | copy-start | bytes 3076
  44.9 9.4 %collective-permute-start.5 = (bf16[4,2,16,128]{3,2,1,0:T(8,128)(2,1)S(1)}, bf16[4,2,16,128]{3,2,1,0:T(8,128)(2,1)S(1)}, u32[]{:S(2)}, u32[]{:S(2)}) collective-permute-start(bf16[4,2,16,128]{3,2,1,0:T(8,128)(2,1)S(1)} %get-tuple-element.158), channel_id=1, source_target_pairs={{0,2},{1,3},{4,6},{5,7},{8,10},{9,11},{12,14},{13,15},{16,18},{17,... | collective-permute-start | bytes 98312 | tf_op jit(solution)/shard_map/ppermute | solution.py:18
  49.4 5.8 %collective-permute-start.6 = (bf16[4,2,16,128]{3,2,1,0:T(8,128)(2,1)S(1)}, bf16[4,2,16,128]{3,2,1,0:T(8,128)(2,1)S(1)}, u32[]{:S(2)}, u32[]{:S(2)}) collective-permute-start(bf16[4,2,16,128]{3,2,1,0:T(8,128)(2,1)S(1)} %get-tuple-element.159), channel_id=1, source_target_pairs={{2,0},{3,1},{6,4},{7,5},{10,8},{11,9},{14,12},{15,13},{18,16},{19,... | collective-permute-start | bytes 98312 | tf_op jit(solution)/shard_map/ppermute | solution.py:19
  55.3 4.9 %collective-permute-start.7 = (bf16[4,8,2,128]{3,2,1,0:T(2,128)(2,1)S(1)}, bf16[4,8,2,128]{3,2,1,0:T(2,128)(2,1)S(1)}, u32[]{:S(2)}, u32[]{:S(2)}) collective-permute-start(bf16[4,8,2,128]{3,2,1,0:T(2,128)(2,1)S(1)} %get-tuple-element.148), channel_id=1, source_target_pairs={{0,1},{2,3},{4,5},{6,7},{8,9},{10,11},{12,13},{14,15},{16,17},{18,... | collective-permute-start | bytes 49160 | tf_op jit(solution)/shard_map/ppermute | solution.py:18
  56.6 5.4 %copy-start.13 = (bf16[2,128,128]{2,1,0:T(8,128)(2,1)S(1)}, bf16[2,128,128]{2,1,0:T(8,128)(2,1)}, u32[]{:S(2)}) copy-start(bf16[2,128,128]{2,1,0:T(8,128)(2,1)} %copy.48) | copy-start | bytes 196612
  56.6 3.6 %collective-permute-start.8 = (bf16[4,8,2,128]{3,2,1,0:T(2,128)(2,1)S(1)}, bf16[4,8,2,128]{3,2,1,0:T(2,128)(2,1)S(1)}, u32[]{:S(2)}, u32[]{:S(2)}) collective-permute-start(bf16[4,8,2,128]{3,2,1,0:T(2,128)(2,1)S(1)} %get-tuple-element.149), channel_id=1, source_target_pairs={{1,0},{3,2},{5,4},{7,6},{9,8},{11,10},{13,12},{15,14},{17,16},{19,... | collective-permute-start | bytes 49160 | tf_op jit(solution)/shard_map/ppermute | solution.py:19
  60.3 7.5 %collective-permute-start.9 = (bf16[2,8,20,128]{3,2,1,0:T(8,128)(2,1)S(1)}, bf16[2,8,20,128]{3,2,1,0:T(8,128)(2,1)S(1)}, u32[]{:S(2)}, u32[]{:S(2)}) collective-permute-start(bf16[2,8,20,128]{3,2,1,0:T(8,128)(2,1)S(1)} %pad_maximum_fusion.5), channel_id=1, source_target_pairs={{4,0},{8,4},{12,8},{5,1},{9,5},{13,9},{6,2},{10,6},{14,10},{7,3},{... | collective-permute-start | bytes 245768 | tf_op jit(solution)/shard_map/ppermute | solution.py:27
  62.0 7.0 %copy-start.11 = (bf16[5,128,128]{2,1,0:T(8,128)(2,1)S(1)}, bf16[5,128,128]{2,1,0:T(8,128)(2,1)}, u32[]{:S(2)}) copy-start(bf16[5,128,128]{2,1,0:T(8,128)(2,1)} %copy.36) | copy-start | bytes 491524
  62.3 7.0 %copy-start.10 = (bf16[5,128,128]{2,1,0:T(8,128)(2,1)S(1)}, bf16[5,128,128]{2,1,0:T(8,128)(2,1)}, u32[]{:S(2)}) copy-start(bf16[5,128,128]{2,1,0:T(8,128)(2,1)} %copy.37) | copy-start | bytes 491524
  67.9 1.6 copy-start.9
  68.0 1.7 copy-start.8
  69.0 2.8 %copy-start.1 = (bf16[4,4,16,128]{3,2,1,0:T(8,128)(2,1)S(1)}, bf16[4,4,16,128]{3,2,1,0:T(8,128)(2,1)}, u32[]{:S(2)}) copy-start(bf16[4,4,16,128]{3,2,1,0:T(8,128)(2,1)} %param.6) | copy-start | bytes 196612
  69.0 2.8 %copy-start.3 = (bf16[5,128,128]{2,1,0:T(8,128)(2,1)S(1)}, bf16[5,128,128]{2,1,0:T(8,128)(2,1)}, u32[]{:S(2)}) copy-start(bf16[5,128,128]{2,1,0:T(8,128)(2,1)} %copy.47) | copy-start | bytes 491524
  71.0 2.1 %copy-start.17 = (u32[32]{0:T(128)S(1)}, u32[32]{0:T(128)}, u32[]{:S(2)}) copy-start(u32[32]{0:T(128)} %constant.15) | copy-start | bytes 388
Sparse Core Ops, SparseCore 0:
  73.2 111.9 all-reduce.3
where the time goes:
time: 196 us; the launch traced here: 195 us
  waiting for transfers between devices  82.8 us (42%)
  blocking collectives  34.5 us (18%)
  starting transfers between devices  24.6 us (13%)
  local copies, waits for them, and re-layouts  18.6 us (9%)
  between operations  15.6 us (8%)
  matrix products  12.9 us (7%)
  other arithmetic  6.33 us (3%)
    unnamed x2, waiting for transfers between devices  75.5 us
    psum x1, blocking collectives, local(): lax.psum((gamma_local, beta_local), ('gx', 'gy', 'gz'))  34.5 us
    ppermute x4, starting transfers between devices, padded_2(): before = lax.ppermute(last, axis, up)  14.3 us
    transpose x15, local copies, waits for them, and re-layouts, context_transposed(): jnp.transpose(kernel[first_tap:first_tap + count], (0, 2, 1))  9.94 us
    ppermute x2, waiting for transfers between devices, from_behind(): lax.ppermute(value, axis, [(source, source + steps) for source in range(l...  6.32 us
    unnamed x59, local copies, waits for them, and re-layouts  5.71 us
    ppermute x4, starting transfers between devices, padded_2(): after = lax.ppermute(leading, axis, down)  5.29 us
    ppermute x2, starting transfers between devices, from_behind(): lax.ppermute(value, axis, [(source, source + steps) for source in range(l...  4.96 us
  transfers between devices with their start and end apart: 11, of which 4 were waited for; matrix products, arithmetic and copies ran while one was open for 11% of the time, Pallas kernels for 0%

commit v1 on v0

--- a/solution.py
+++ b/solution.py
@@ -123,6 +123,81 @@
     return jnp.concatenate([widened, above], axis=0)
 
 
+def swapped(value, axis, partner):
+    count = lax.axis_size(axis)
+    return lax.ppermute(value, axis, [(i, partner(i)) for i in range(count)])
+
+
+def gathered(shard, axis, dim):
+    count = lax.axis_size(axis)
+    place = lax.axis_index(axis)
+    if count == 2:
+        other = swapped(shard, axis, lambda i: 1 - i)
+        orders = ((shard, other), (other, shard))
+    elif count == 4:
+        mirror = swapped(shard, axis, lambda i: 3 - i)
+        pair = swapped(jnp.stack([shard, mirror]), axis, lambda i: i ^ 1)
+        near, far = pair[0], pair[1]
+        orders = (
+            (shard, near, far, mirror),
+            (near, shard, mirror, far),
+            (far, mirror, shard, near),
+            (mirror, far, near, shard),
+        )
+    else:
+        return lax.all_gather(shard, axis, axis=dim, tiled=True)
+    return lax.select_n(place, *[jnp.concatenate(order, axis=dim) for order in orders])
+
+
+def whole_slab(block):
+    for axis, dim in (("gx", 0), ("gy", 1), ("gz", 2)):
+        block = gathered(block, axis, dim)
+    return block
+
+
+def summed(value):
+    for axis in ("gz", "gy", "gx"):
+        count = lax.axis_size(axis)
+        if count & (count - 1):
+            value = lax.psum(value, axis)
+            continue
+        step = 1
+        while step < count:
+            value = value + swapped(value, axis, lambda i: i ^ step)
+            step *= 2
+    return value
+
+
+def own_kernel_rows(latent_grid, grad_grid):
+    slab, grads = whole_slab(latent_grid), whole_slab(grad_grid)
+    size_x, size_y, size_z, channels = slab.shape
+    offsets = causal_offsets()
+    devices = lax.axis_size(("gx", "gy", "gz"))
+    rows = len(offsets) * channels // devices
+    spanned = max(-(-((d * rows) % channels + rows) // channels) for d in range(devices))
+    first_row = lax.axis_index(("gx", "gy", "gz")) * rows
+    first_tap = jnp.minimum(first_row // channels, len(offsets) - spanned)
+    table = jnp.array(offsets, jnp.int32)
+    padded = jnp.pad(slab, ((2, 0), (2, 2), (2, 2), (0, 0)))
+    pieces = []
+    for number in range(spanned):
+        shift = lax.dynamic_index_in_dim(table, first_tap + number, keepdims=False)
+        pieces.append(
+            lax.dynamic_slice(
+                padded, (2 + shift[0], 2 + shift[1], 2 + shift[2], 0), (size_x, size_y, size_z, channels)
+            ).reshape(-1, channels)
+        )
+    product = lax.dot_general(
+        jnp.concatenate(pieces, axis=1),
+        grads.reshape(-1, channels),
+        (((0,), (0,)), ((), ())),
+        preferred_element_type=jnp.float32,
+    )
+    return lax.dynamic_slice(
+        product, (first_row - first_tap * channels, 0), (rows, channels)
+    ).reshape(-1)
+
+
 def local(features, scales, occupancy, kernel, gamma, beta):
     size_x, size_y, size_z, channels = features.shape
     extent = (size_x, size_y, size_z)
@@ -154,10 +229,17 @@
         .astype(jnp.bfloat16)
         .reshape(size_x, size_y, size_z, channels)
     )
-    kernel_local = kernel_terms(padded, mean_grad, extent) / voxels
-    grad_kernel = lax.psum_scatter(
-        kernel_local, ("gx", "gy", "gz"), scatter_dimension=0, tiled=True
-    )
+    devices = lax.axis_size(("gx", "gy", "gz"))
+    fits = devices * voxels <= 16384 and (62 * channels) % devices == 0
+    if fits:
+        grad_kernel = own_kernel_rows(latent_grid, grad_grid) / voxels
+    else:
+        grad_kernel = lax.psum_scatter(
+            kernel_terms(padded, mean_grad, extent) / voxels,
+            ("gx", "gy", "gz"),
+            scatter_dimension=0,
+            tiled=True,
+        )
     factor = 0.5 / math.sqrt(voxels)
     gamma_local = -factor * jnp.dot(
         (feats * feats).T,
@@ -166,7 +248,8 @@
         preferred_element_type=jnp.float32,
     )
     beta_local = -factor * jnp.sum(weighted, axis=0)
-    grad_gamma, grad_beta = lax.psum((gamma_local, beta_local), ("gx", "gy", "gz"))
+    both = summed(jnp.concatenate([gamma_local, jnp.broadcast_to(beta_local, (8, channels))], axis=0))
+    grad_gamma, grad_beta = both[:channels], both[channels]
     return (grad_features, grad_kernel, grad_gamma, grad_beta)
 
 

time: 196 us -> 120 us (0.61)
  waiting for transfers between devices: 82.8 us -> 18.1 us
  blocking collectives: 34.5 us -> 0 us
  starting transfers between devices: 24.6 us -> 35.1 us
  between operations: 15.6 us -> 20.9 us
  matrix products: 12.9 us -> 17.8 us
  local copies, waits for them, and re-layouts: 18.6 us -> 21.5 us
    unnamed x2 -> x0, waiting for transfers between devices: 75.5 us -> none
    psum x1 -> x0, blocking collectives: 34.5 us -> none  [local(): lax.psum((gamma_local, beta_local), ('gx', 'gy', 'gz'))]
    ppermute x0 -> x12, waiting for transfers between devices: none -> 14.1 us  [swapped(): return lax.ppermute(value, axis, [(i, partner(i)) for i in range(count)])]
    ppermute x0 -> x12, starting transfers between devices: none -> 13.6 us  [swapped(): return lax.ppermute(value, axis, [(i, partner(i)) for i in range(count)])]
    dot_general x13, matrix products: 2.96 us -> 10.6 us  [context_mean(): total = total + jnp.dot(patch, weights, preferred_element_type=jnp.float32)]
    dynamic_slice x0 -> x3, local copies, waits for them, and re-layouts: none -> 3.7 us  [the longest x2 2.81 us: own_kernel_rows(): lax.dynamic_slice(padded, (2 + shift[0], 2 + shift[1], 2 + shift[2], 0),...]
    unnamed x59 -> x92, local copies, waits for them, and re-layouts: 5.71 us -> 3.09 us
    slice x0 -> x4, local copies, waits for them, and re-layouts: none -> 2.55 us  [the longest x3 1.91 us: own_kernel_rows(): shift[2]]
  transfers between devices with their start and end apart: 11 -> 22, of which waited for: 4 -> 9; matrix products, arithmetic and copies ran while one was open for 11% -> 34% of each run, Pallas kernels for 0% -> 0%
where the time goes in v1:
time: 120 us; the launch traced here: 119 us
  starting transfers between devices  35.1 us (29%)
  local copies, waits for them, and re-layouts  21.5 us (18%)
  between operations  20.9 us (17%)
  waiting for transfers between devices  18.1 us (15%)
  matrix products  17.8 us (15%)
  other arithmetic  5.94 us (5%)
    ppermute x12, waiting for transfers between devices, swapped(): return lax.ppermute(value, axis, [(i, partner(i)) for i in range(count)])  14.1 us
    ppermute x12, starting transfers between devices, swapped(): return lax.ppermute(value, axis, [(i, partner(i)) for i in range(count)])  13.6 us
    ppermute x4, starting transfers between devices, padded_2(): before = lax.ppermute(last, axis, up)  13.4 us
    dot_general x13, matrix products, context_mean(): total = total + jnp.dot(patch, weights, preferred_element_type=jnp.float32)  10.6 us
    transpose x15, local copies, waits for them, and re-layouts, context_transposed(): jnp.transpose(kernel[first_tap:first_tap + count], (0, 2, 1))  7.86 us
    ppermute x4, starting transfers between devices, padded_2(): after = lax.ppermute(leading, axis, down)  5.14 us
    ppermute x2, waiting for transfers between devices, from_behind(): lax.ppermute(value, axis, [(source, source + steps) for source in range(l...  3.84 us
    unnamed x92, local copies, waits for them, and re-layouts  3.09 us
  transfers between devices with their start and end apart: 22, of which 9 were waited for; matrix products, arithmetic and copies ran while one was open for 34% of the time, Pallas kernels for 0%

profile of v1, /device:TPU:0, one launch (start us, length us, event | category | flops | bytes accessed | tf_op | source)
XLA Modules:
  0.0 119.4 jit_solution(9417999318335833035)
XLA Ops:
  2.9 5.1 %collective-permute-start.10 = (bf16[4,4,16,128]{3,2,1,0:T(8,128)(2,1)S(1)}, bf16[4,4,16,128]{3,2,1,0:T(8,128)(2,1)}, u32[]{:S(2)}, u32[]{:S(2)}) collective-permute-start(bf16[4,4,16,128]{3,2,1,0:T(8,128)(2,1)S(1)} %bitcast.200), channel_id=1, source_target_pairs={{0,12},{4,8},{8,4},{12,0},{1,13},{5,9},{9,5},{13,1},{2,14},{6,10},... | collective-permute-start | bytes 196616 | tf_op jit(solution)/shard_map/ppermute | solution.py:128
  8.6 1.3 %collective-permute-start.1 = (bf16[4,2,16,128]{3,2,1,0:T(8,128)(2,1)}, bf16[4,2,16,128]{3,2,1,0:T(8,128)(2,1)S(1)}, u32[]{:S(2)}, u32[]{:S(2)}) collective-permute-start(bf16[4,2,16,128]{3,2,1,0:T(8,128)(2,1)} %get-tuple-element.167), channel_id=1, source_target_pairs={{2,0},{3,1},{6,4},{7,5},{10,8},{11,9},{14,12},{15,13},{18,16},{19,... | collective-permute-start | bytes 98312 | tf_op jit(solution)/shard_map/ppermute | solution.py:19
  9.9 4.5 %collective-permute-start = (bf16[4,2,16,128]{3,2,1,0:T(8,128)(2,1)S(1)}, bf16[4,2,16,128]{3,2,1,0:T(8,128)(2,1)S(1)}, u32[]{:S(2)}, u32[]{:S(2)}) collective-permute-start(bf16[4,2,16,128]{3,2,1,0:T(8,128)(2,1)S(1)} %get-tuple-element.166), channel_id=1, source_target_pairs={{0,2},{1,3},{4,6},{5,7},{8,10},{9,11},{12,14},{13,15},{16,18},{17,... | collective-permute-start | bytes 98312 | tf_op jit(solution)/shard_map/ppermute | solution.py:18
  14.5 1.5 %slice_bitcast_fusion.5 = (bf16[2,128,128]{1,2,0:T(8,128)(2,1)}, bf16[2,128,128]{2,1,0:T(8,128)(2,1)}) fusion(bf16[62,128,128]{2,1,0:T(8,128)(2,1)} %param.10), kind=kLoop, calls=%fused_computation.231 | loop fusion | bytes 196608 | tf_op jit(solution)/shard_map/transpose | solution.py:95
  16.0 2.1 %fusion.19 = (bf16[5,128,128]{2,1,0:T(8,128)(2,1)}, bf16[5,128,128]{2,1,0:T(8,128)(2,1)}, bf16[5,128,128]{2,1,0:T(8,128)(2,1)}, bf16[5,128,128]{2,1,0:T(8,128)(2,1)}, bf16[5,128,128]{2,1,0:T(8,128)(2,1)}) fusion(bf16[62,128,128]{2,1,0:T(8,128)(2,1)} %param.10), kind=kLoop, calls=%fused_computation.246 | loop fusion | bytes 1638400 | tf_op jit(solution)/shard_map/slice | solution.py:76
  18.1 1.6 %slice_bitcast_fusion.6 = (bf16[5,128,128]{1,2,0:T(8,128)(2,1)S(1)}, bf16[5,128,128]{1,2,0:T(8,128)(2,1)}, bf16[5,128,128]{1,2,0:T(8,128)(2,1)}, bf16[5,128,128]...) fusion(bf16[62,128,128]{2,1,0:T(8,128)(2,1)S(1)} %copy-done.1), kind=kLoop, calls=%fused_computation.233 | loop fusion | bytes 5079040 | tf_op jit(solution)/shard_map/transpose | solution.py:95
  22.2 1.3 %collective-permute-start.3 = (bf16[4,8,2,128]{3,2,1,0:T(2,128)(2,1)S(1)}, bf16[4,8,2,128]{3,2,1,0:T(2,128)(2,1)S(1)}, u32[]{:S(2)}, u32[]{:S(2)}) collective-permute-start(bf16[4,8,2,128]{3,2,1,0:T(2,128)(2,1)S(1)} %get-tuple-element.158), channel_id=1, source_target_pairs={{1,0},{3,2},{5,4},{7,6},{9,8},{11,10},{13,12},{15,14},{17,16},{19,... | collective-permute-start | bytes 49160 | tf_op jit(solution)/shard_map/ppermute | solution.py:19
  23.5 3.0 %collective-permute-start.2 = (bf16[4,8,2,128]{3,2,1,0:T(2,128)(2,1)S(1)}, bf16[4,8,2,128]{3,2,1,0:T(2,128)(2,1)S(1)}, u32[]{:S(2)}, u32[]{:S(2)}) collective-permute-start(bf16[4,8,2,128]{3,2,1,0:T(2,128)(2,1)S(1)} %get-tuple-element.159), channel_id=1, source_target_pairs={{0,1},{2,3},{4,5},{6,7},{8,9},{10,11},{12,13},{14,15},{16,17},{18,... | collective-permute-start | bytes 49160 | tf_op jit(solution)/shard_map/ppermute | solution.py:18
  27.6 1.4 %collective-permute-start.4 = (bf16[2,8,20,128]{3,2,1,0:T(8,128)(2,1)S(1)}, bf16[2,8,20,128]{3,2,1,0:T(8,128)(2,1)S(1)}, u32[]{:S(2)}, u32[]{:S(2)}) collective-permute-start(bf16[2,8,20,128]{3,2,1,0:T(8,128)(2,1)S(1)} %pad_maximum_fusion.11), channel_id=1, source_target_pairs={{0,4},{4,8},{8,12},{1,5},{5,9},{9,13},{2,6},{6,10},{10,14},{3,7},{... | collective-permute-start | bytes 245768 | tf_op jit(solution)/shard_map/ppermute | solution.py:27
  29.4 2.3 %collective-permute-done.4 = bf16[2,8,20,128]{3,2,1,0:T(8,128)(2,1)S(1)} collective-permute-done((bf16[2,8,20,128]{3,2,1,0:T(8,128)(2,1)S(1)}, bf16[2,8,20,128]{3,2,1,0:T(8,128)(2,1)S(1)}, u32[]{:S(2)}, u32[]{:S(2)}) %collective-permute-start.4) | collective-permute-done | bytes 81952 | tf_op jit(solution)/shard_map/ppermute | solution.py:27
  33.8 1.2 %convolution_add_fusion.19 = f32[256,128]{1,0:T(8,128)S(1)} fusion(f32[256,128]{1,0:T(8,128)S(1)} %convolution_add_fusion.20, bf16[256,640]{1,0:T(8,128)(2,1)} %bitcast.262, bf16[640,128]{1,0:T(8,128)(2,1)S(1)} %bitcast.236), kind=kOutput, calls=%fused_computation.28 | convolution fusion | flops 41975808 | bytes 753664 | tf_op jit(solution)/shard_map/dot_general | solution.py:77
  35.1 1.2 %convolution_add_fusion.18 = f32[256,128]{1,0:T(8,128)S(1)} fusion(f32[256,128]{1,0:T(8,128)S(1)} %convolution_add_fusion.19, bf16[256,640]{1,0:T(8,128)(2,1)} %bitcast.261, bf16[640,128]{1,0:T(8,128)(2,1)S(1)} %bitcast.234), kind=kOutput, calls=%fused_computation.27 | convolution fusion | flops 41975808 | bytes 753664 | tf_op jit(solution)/shard_map/dot_general | solution.py:77
  36.4 1.2 %convolution_add_fusion.17 = f32[256,128]{1,0:T(8,128)S(1)} fusion(f32[256,128]{1,0:T(8,128)S(1)} %convolution_add_fusion.18, bf16[256,640]{1,0:T(8,128)(2,1)} %bitcast.260, bf16[640,128]{1,0:T(8,128)(2,1)S(1)} %bitcast.233), kind=kOutput, calls=%fused_computation.26 | convolution fusion | flops 41975808 | bytes 753664 | tf_op jit(solution)/shard_map/dot_general | solution.py:77
  37.7 1.2 %convolution_add_fusion.16 = f32[256,128]{1,0:T(8,128)S(1)} fusion(f32[256,128]{1,0:T(8,128)S(1)} %convolution_add_fusion.17, bf16[256,640]{1,0:T(8,128)(2,1)} %bitcast.259, bf16[640,128]{1,0:T(8,128)(2,1)S(1)} %bitcast.232), kind=kOutput, calls=%fused_computation.25 | convolution fusion | flops 41975808 | bytes 753664 | tf_op jit(solution)/shard_map/dot_general | solution.py:77
  38.9 1.2 %convolution_add_fusion.15 = f32[256,128]{1,0:T(8,128)S(1)} fusion(f32[256,128]{1,0:T(8,128)S(1)} %convolution_add_fusion.16, bf16[256,640]{1,0:T(8,128)(2,1)} %bitcast.258, bf16[640,128]{1,0:T(8,128)(2,1)S(1)} %bitcast.231), kind=kOutput, calls=%fused_computation.24 | convolution fusion | flops 41975808 | bytes 753664 | tf_op jit(solution)/shard_map/dot_general | solution.py:77
  40.2 1.3 %convolution_add_fusion.14 = f32[256,128]{1,0:T(8,128)S(1)} fusion(f32[256,128]{1,0:T(8,128)S(1)} %convolution_add_fusion.15, bf16[256,640]{1,0:T(8,128)(2,1)} %bitcast.257, bf16[640,128]{1,0:T(8,128)(2,1)S(1)} %bitcast.230), kind=kOutput, calls=%fused_computation.23 | convolution fusion | flops 41975808 | bytes 753664 | tf_op jit(solution)/shard_map/dot_general | solution.py:77
  41.5 1.2 %convolution_add_fusion.13 = f32[256,128]{1,0:T(8,128)S(1)} fusion(f32[256,128]{1,0:T(8,128)S(1)} %convolution_add_fusion.14, bf16[256,640]{1,0:T(8,128)(2,1)} %bitcast.256, bf16[640,128]{1,0:T(8,128)(2,1)S(1)} %bitcast.229), kind=kOutput, calls=%fused_computation.22 | convolution fusion | flops 41975808 | bytes 753664 | tf_op jit(solution)/shard_map/dot_general | solution.py:77
  43.9 1.3 %collective-permute-start.6 = (bf16[4,2,16,128]{3,2,1,0:T(8,128)(2,1)S(1)}, bf16[4,2,16,128]{3,2,1,0:T(8,128)(2,1)S(1)}, u32[]{:S(2)}, u32[]{:S(2)}) collective-permute-start(bf16[4,2,16,128]{3,2,1,0:T(8,128)(2,1)S(1)} %get-tuple-element.165), channel_id=1, source_target_pairs={{2,0},{3,1},{6,4},{7,5},{10,8},{11,9},{14,12},{15,13},{18,16},{19,... | collective-permute-start | bytes 98312 | tf_op jit(solution)/shard_map/ppermute | solution.py:19
  45.2 4.5 %collective-permute-start.5 = (bf16[4,2,16,128]{3,2,1,0:T(8,128)(2,1)S(1)}, bf16[4,2,16,128]{3,2,1,0:T(8,128)(2,1)S(1)}, u32[]{:S(2)}, u32[]{:S(2)}) collective-permute-start(bf16[4,2,16,128]{3,2,1,0:T(8,128)(2,1)S(1)} %get-tuple-element.164), channel_id=1, source_target_pairs={{0,2},{1,3},{4,6},{5,7},{8,10},{9,11},{12,14},{13,15},{16,18},{17,... | collective-permute-start | bytes 98312 | tf_op jit(solution)/shard_map/ppermute | solution.py:18
  74.3 1.3 %collective-permute-start.7 = (bf16[4,8,2,128]{3,2,1,0:T(2,128)(2,1)S(1)}, bf16[4,8,2,128]{3,2,1,0:T(2,128)(2,1)S(1)}, u32[]{:S(2)}, u32[]{:S(2)}) collective-permute-start(bf16[4,8,2,128]{3,2,1,0:T(2,128)(2,1)S(1)} %get-tuple-element.154), channel_id=1, source_target_pairs={{0,1},{2,3},{4,5},{6,7},{8,9},{10,11},{12,13},{14,15},{16,17},{18,... | collective-permute-start | bytes 49160 | tf_op jit(solution)/shard_map/ppermute | solution.py:18
  75.6 1.3 %collective-permute-start.8 = (bf16[4,8,2,128]{3,2,1,0:T(2,128)(2,1)S(1)}, bf16[4,8,2,128]{3,2,1,0:T(2,128)(2,1)S(1)}, u32[]{:S(2)}, u32[]{:S(2)}) collective-permute-start(bf16[4,8,2,128]{3,2,1,0:T(2,128)(2,1)S(1)} %get-tuple-element.155), channel_id=1, source_target_pairs={{1,0},{3,2},{5,4},{7,6},{9,8},{11,10},{13,12},{15,14},{17,16},{19,... | collective-permute-start | bytes 49160 | tf_op jit(solution)/shard_map/ppermute | solution.py:19
  77.8 2.5 %collective-permute-start.11 = (bf16[2,4,4,16,128]{4,3,2,1,0:T(8,128)(2,1)S(1)}, bf16[2,4,4,16,128]{4,3,2,1,0:T(8,128)(2,1)S(1)}, u32[]{:S(2)}, u32[]{:S(2)}) collective-permute-start(bf16[2,4,4,16,128]{4,3,2,1,0:T(8,128)(2,1)S(1)} %pad_maximum_fusion.5), channel_id=1, source_target_pairs={{0,4},{4,0},{8,12},{12,8},{1,5},{5,1},{9,13},{13,9},{2,6},{6,2},{1... | collective-permute-start | bytes 393224 | tf_op jit(solution)/shard_map/ppermute | solution.py:128
  80.3 1.2 %collective-permute-start.14 = (bf16[4,4,16,128]{3,2,1,0:T(8,128)(2,1)S(1)}, bf16[4,4,16,128]{3,2,1,0:T(8,128)(2,1)S(1)}, u32[]{:S(2)}, u32[]{:S(2)}) collective-permute-start(bf16[4,4,16,128]{3,2,1,0:T(8,128)(2,1)S(1)} %bitcast.211), channel_id=1, source_target_pairs={{0,12},{4,8},{8,4},{12,0},{1,13},{5,9},{9,5},{13,1},{2,14},{6,10},... | collective-permute-start | bytes 196616 | tf_op jit(solution)/shard_map/ppermute | solution.py:128
  81.7 1.5 %collective-permute-start.9 = (bf16[2,8,20,128]{3,2,1,0:T(8,128)(2,1)S(1)}, bf16[2,8,20,128]{3,2,1,0:T(8,128)(2,1)S(1)}, u32[]{:S(2)}, u32[]{:S(2)}) collective-permute-start(bf16[2,8,20,128]{3,2,1,0:T(8,128)(2,1)S(1)} %pad_maximum_fusion.7), channel_id=1, source_target_pairs={{4,0},{8,4},{12,8},{5,1},{9,5},{13,9},{6,2},{10,6},{14,10},{7,3},{... | collective-permute-start | bytes 245768 | tf_op jit(solution)/shard_map/ppermute | solution.py:27
  85.4 1.8 %collective-permute-done.14 = bf16[4,4,16,128]{3,2,1,0:T(8,128)(2,1)S(1)} collective-permute-done((bf16[4,4,16,128]{3,2,1,0:T(8,128)(2,1)S(1)}, bf16[4,4,16,128]{3,2,1,0:T(8,128)(2,1)S(1)}, u32[]{:S(2)}, u32[]{:S(2)}) %collective-permute-start.14) | collective-permute-done | bytes 65568 | tf_op jit(solution)/shard_map/ppermute | solution.py:128
  87.8 1.6 %collective-permute-done.9 = bf16[2,8,20,128]{3,2,1,0:T(8,128)(2,1)S(1)} collective-permute-done((bf16[2,8,20,128]{3,2,1,0:T(8,128)(2,1)S(1)}, bf16[2,8,20,128]{3,2,1,0:T(8,128)(2,1)S(1)}, u32[]{:S(2)}, u32[]{:S(2)}) %collective-permute-start.9) | collective-permute-done | bytes 81952 | tf_op jit(solution)/shard_map/ppermute | solution.py:27
  96.1 1.7 %collective-permute-start.16 = (bf16[16,4,16,128]{3,2,1,0:T(8,128)(2,1)S(1)}, bf16[16,4,16,128]{3,2,1,0:T(8,128)(2,1)S(1)}, u32[]{:S(2)}, u32[]{:S(2)}) collective-permute-start(bf16[16,4,16,128]{3,2,1,0:T(8,128)(2,1)S(1)} %fusion.8), channel_id=1, source_target_pairs={{0,2},{2,0},{1,3},{3,1},{4,6},{6,4},{5,7},{7,5},{8,10},{10,8},{9,1... | collective-permute-start | bytes 786440 | tf_op jit(solution)/shard_map/ppermute | solution.py:128
  97.8 2.9 %collective-permute-done.19 = f32[136,128]{1,0:T(8,128)S(1)} collective-permute-done((f32[136,128]{1,0:T(8,128)S(1)}, f32[136,128]{1,0:T(8,128)S(1)}, u32[]{:S(2)}, u32[]{:S(2)}) %collective-permute-start.19) | collective-permute-done | bytes 69664 | tf_op jit(solution)/shard_map/ppermute | solution.py:128
  101.4 3.6 %collective-permute-done.20 = f32[136,128]{1,0:T(8,128)S(1)} collective-permute-done((f32[136,128]{1,0:T(8,128)S(1)}, f32[136,128]{1,0:T(8,128)S(1)}, u32[]{:S(2)}, u32[]{:S(2)}) %collective-permute-start.20) | collective-permute-done | bytes 69664 | tf_op jit(solution)/shard_map/ppermute | solution.py:128
  107.0 4.0 %collective-permute-done.21 = f32[136,128]{1,0:T(8,128)S(1)} collective-permute-done((f32[136,128]{1,0:T(8,128)S(1)}, f32[136,128]{1,0:T(8,128)S(1)}, u32[]{:S(2)}, u32[]{:S(2)}) %collective-permute-start.21) | collective-permute-done | bytes 69664 | tf_op jit(solution)/shard_map/ppermute | solution.py:128
  113.4 2.3 %pad_dynamic-slice_fusion = (bf16[16,8,32,128]{3,2,1,0:T(8,128)(2,1)S(1)}, bf16[16,8,32,128]{3,2,1,0:T(8,128)(2,1)S(1)}, bf16[16,8,32,128]{3,2,1,0:T(8,128)(2,1)S(1)}, bf16[16,8,32,128]{3,2,1,0:T(8,128)(2,1)S(1)}) fusion(s32[]{:T(128)S(6)} %select_n.176, s32[]{:T(128)S(6)} %select_n.177, s32[]{:T(128)S(6)} %select_n.178, ...), kind=kLoop, calls=%fused_computation | loop fusion | bytes 5242928 | tf_op jit(solution)/shard_map/dynamic_slice | solution.py:186
  117.0 1.6 %fusion.31 = f32[640,128]{1,0:T(8,128)S(1)} fusion(bf16[4096,640]{1,0:T(8,128)(2,1)S(1)} %constant_dynamic-update-slice_fusion.120, bf16[4096,128]{1,0:T(8,128)(2,1)S(1)} %bitcast.227), kind=kOutput, calls=%fused_computation.258 | convolution fusion | flops 671088640 | bytes 6619136 | tf_op jit(solution)/shard_map/dot_general | solution.py:190
  (201 shorter events, 32.5 us)
Async XLA Ops:
  0.6 17.5 %copy-start.1 = (bf16[62,128,128]{2,1,0:T(8,128)(2,1)S(1)}, bf16[62,128,128]{2,1,0:T(8,128)(2,1)}, u32[]{:S(2)}) copy-start(bf16[62,128,128]{2,1,0:T(8,128)(2,1)} %param.10) | copy-start | bytes 6094852
  2.9 74.0 %collective-permute-start.10 = (bf16[4,4,16,128]{3,2,1,0:T(8,128)(2,1)S(1)}, bf16[4,4,16,128]{3,2,1,0:T(8,128)(2,1)}, u32[]{:S(2)}, u32[]{:S(2)}) collective-permute-start(bf16[4,4,16,128]{3,2,1,0:T(8,128)(2,1)S(1)} %bitcast.200), channel_id=1, source_target_pairs={{0,12},{4,8},{8,4},{12,0},{1,13},{5,9},{9,5},{13,1},{2,14},{6,10},... | collective-permute-start | bytes 196616 | tf_op jit(solution)/shard_map/ppermute | solution.py:128
  8.6 13.5 %collective-permute-start.1 = (bf16[4,2,16,128]{3,2,1,0:T(8,128)(2,1)}, bf16[4,2,16,128]{3,2,1,0:T(8,128)(2,1)S(1)}, u32[]{:S(2)}, u32[]{:S(2)}) collective-permute-start(bf16[4,2,16,128]{3,2,1,0:T(8,128)(2,1)} %get-tuple-element.167), channel_id=1, source_target_pairs={{2,0},{3,1},{6,4},{7,5},{10,8},{11,9},{14,12},{15,13},{18,16},{19,... | collective-permute-start | bytes 98312 | tf_op jit(solution)/shard_map/ppermute | solution.py:19
  9.9 12.3 %collective-permute-start = (bf16[4,2,16,128]{3,2,1,0:T(8,128)(2,1)S(1)}, bf16[4,2,16,128]{3,2,1,0:T(8,128)(2,1)S(1)}, u32[]{:S(2)}, u32[]{:S(2)}) collective-permute-start(bf16[4,2,16,128]{3,2,1,0:T(8,128)(2,1)S(1)} %get-tuple-element.166), channel_id=1, source_target_pairs={{0,2},{1,3},{4,6},{5,7},{8,10},{9,11},{12,14},{13,15},{16,18},{17,... | collective-permute-start | bytes 98312 | tf_op jit(solution)/shard_map/ppermute | solution.py:18
  19.7 9.4 %copy-start.32 = (bf16[2,128,128]{2,1,0:T(8,128)(2,1)S(1)}, bf16[2,128,128]{2,1,0:T(8,128)(2,1)}, u32[]{:S(2)}) copy-start(bf16[2,128,128]{2,1,0:T(8,128)(2,1)} %get-tuple-element.26) | copy-start | bytes 196612
  22.2 5.0 %collective-permute-start.3 = (bf16[4,8,2,128]{3,2,1,0:T(2,128)(2,1)S(1)}, bf16[4,8,2,128]{3,2,1,0:T(2,128)(2,1)S(1)}, u32[]{:S(2)}, u32[]{:S(2)}) collective-permute-start(bf16[4,8,2,128]{3,2,1,0:T(2,128)(2,1)S(1)} %get-tuple-element.158), channel_id=1, source_target_pairs={{1,0},{3,2},{5,4},{7,6},{9,8},{11,10},{13,12},{15,14},{17,16},{19,... | collective-permute-start | bytes 49160 | tf_op jit(solution)/shard_map/ppermute | solution.py:19
  23.5 3.9 %collective-permute-start.2 = (bf16[4,8,2,128]{3,2,1,0:T(2,128)(2,1)S(1)}, bf16[4,8,2,128]{3,2,1,0:T(2,128)(2,1)S(1)}, u32[]{:S(2)}, u32[]{:S(2)}) collective-permute-start(bf16[4,8,2,128]{3,2,1,0:T(2,128)(2,1)S(1)} %get-tuple-element.159), channel_id=1, source_target_pairs={{0,1},{2,3},{4,5},{6,7},{8,9},{10,11},{12,13},{14,15},{16,17},{18,... | collective-permute-start | bytes 49160 | tf_op jit(solution)/shard_map/ppermute | solution.py:18
  27.6 4.1 %collective-permute-start.4 = (bf16[2,8,20,128]{3,2,1,0:T(8,128)(2,1)S(1)}, bf16[2,8,20,128]{3,2,1,0:T(8,128)(2,1)S(1)}, u32[]{:S(2)}, u32[]{:S(2)}) collective-permute-start(bf16[2,8,20,128]{3,2,1,0:T(8,128)(2,1)S(1)} %pad_maximum_fusion.11), channel_id=1, source_target_pairs={{0,4},{4,8},{8,12},{1,5},{5,9},{9,13},{2,6},{6,10},{10,14},{3,7},{... | collective-permute-start | bytes 245768 | tf_op jit(solution)/shard_map/ppermute | solution.py:27
  33.8 7.7 %copy-start.9 = (bf16[5,128,128]{2,1,0:T(8,128)(2,1)S(1)}, bf16[5,128,128]{2,1,0:T(8,128)(2,1)}, u32[]{:S(2)}) copy-start(bf16[5,128,128]{2,1,0:T(8,128)(2,1)} %get-tuple-element.19) | copy-start | bytes 491524
  35.1 7.6 %copy-start.8 = (bf16[5,128,128]{2,1,0:T(8,128)(2,1)S(1)}, bf16[5,128,128]{2,1,0:T(8,128)(2,1)}, u32[]{:S(2)}) copy-start(bf16[5,128,128]{2,1,0:T(8,128)(2,1)} %get-tuple-element.18) | copy-start | bytes 491524
  38.9 30.4 %copy-start.33 = (bf16[2,128,128]{1,2,0:T(8,128)(2,1)S(1)}, bf16[2,128,128]{1,2,0:T(8,128)(2,1)}, u32[]{:S(2)}) copy-start(bf16[2,128,128]{1,2,0:T(8,128)(2,1)} %get-tuple-element.25) | copy-start | bytes 196612
  38.9 30.5 %copy-start.7 = (bf16[5,128,128]{1,2,0:T(8,128)(2,1)S(1)}, bf16[5,128,128]{1,2,0:T(8,128)(2,1)}, u32[]{:S(2)}) copy-start(bf16[5,128,128]{1,2,0:T(8,128)(2,1)} %get-tuple-element.7) | copy-start | bytes 491524
  40.2 30.0 %copy-start.6 = (bf16[5,128,128]{1,2,0:T(8,128)(2,1)S(1)}, bf16[5,128,128]{1,2,0:T(8,128)(2,1)}, u32[]{:S(2)}) copy-start(bf16[5,128,128]{1,2,0:T(8,128)(2,1)} %get-tuple-element.8) | copy-start | bytes 491524
  40.2 30.8 %copy-start.5 = (bf16[5,128,128]{1,2,0:T(8,128)(2,1)S(1)}, bf16[5,128,128]{1,2,0:T(8,128)(2,1)}, u32[]{:S(2)}) copy-start(bf16[5,128,128]{1,2,0:T(8,128)(2,1)} %get-tuple-element.9) | copy-start | bytes 491524
  40.2 31.6 %copy-start.4 = (bf16[5,128,128]{1,2,0:T(8,128)(2,1)S(1)}, bf16[5,128,128]{1,2,0:T(8,128)(2,1)}, u32[]{:S(2)}) copy-start(bf16[5,128,128]{1,2,0:T(8,128)(2,1)} %get-tuple-element.10) | copy-start | bytes 491524
  41.5 31.2 %copy-start.3 = (bf16[5,128,128]{1,2,0:T(8,128)(2,1)S(1)}, bf16[5,128,128]{1,2,0:T(8,128)(2,1)}, u32[]{:S(2)}) copy-start(bf16[5,128,128]{1,2,0:T(8,128)(2,1)} %get-tuple-element.11) | copy-start | bytes 491524
  43.9 30.4 %collective-permute-start.6 = (bf16[4,2,16,128]{3,2,1,0:T(8,128)(2,1)S(1)}, bf16[4,2,16,128]{3,2,1,0:T(8,128)(2,1)S(1)}, u32[]{:S(2)}, u32[]{:S(2)}) collective-permute-start(bf16[4,2,16,128]{3,2,1,0:T(8,128)(2,1)S(1)} %get-tuple-element.165), channel_id=1, source_target_pairs={{2,0},{3,1},{6,4},{7,5},{10,8},{11,9},{14,12},{15,13},{18,16},{19,... | collective-permute-start | bytes 98312 | tf_op jit(solution)/shard_map/ppermute | solution.py:19
  45.2 29.1 %collective-permute-start.5 = (bf16[4,2,16,128]{3,2,1,0:T(8,128)(2,1)S(1)}, bf16[4,2,16,128]{3,2,1,0:T(8,128)(2,1)S(1)}, u32[]{:S(2)}, u32[]{:S(2)}) collective-permute-start(bf16[4,2,16,128]{3,2,1,0:T(8,128)(2,1)S(1)} %get-tuple-element.164), channel_id=1, source_target_pairs={{0,2},{1,3},{4,6},{5,7},{8,10},{9,11},{12,14},{13,15},{16,18},{17,... | collective-permute-start | bytes 98312 | tf_op jit(solution)/shard_map/ppermute | solution.py:18
  74.3 7.2 %collective-permute-start.7 = (bf16[4,8,2,128]{3,2,1,0:T(2,128)(2,1)S(1)}, bf16[4,8,2,128]{3,2,1,0:T(2,128)(2,1)S(1)}, u32[]{:S(2)}, u32[]{:S(2)}) collective-permute-start(bf16[4,8,2,128]{3,2,1,0:T(2,128)(2,1)S(1)} %get-tuple-element.154), channel_id=1, source_target_pairs={{0,1},{2,3},{4,5},{6,7},{8,9},{10,11},{12,13},{14,15},{16,17},{18,... | collective-permute-start | bytes 49160 | tf_op jit(solution)/shard_map/ppermute | solution.py:18
  75.6 5.9 %collective-permute-start.8 = (bf16[4,8,2,128]{3,2,1,0:T(2,128)(2,1)S(1)}, bf16[4,8,2,128]{3,2,1,0:T(2,128)(2,1)S(1)}, u32[]{:S(2)}, u32[]{:S(2)}) collective-permute-start(bf16[4,8,2,128]{3,2,1,0:T(2,128)(2,1)S(1)} %get-tuple-element.155), channel_id=1, source_target_pairs={{1,0},{3,2},{5,4},{7,6},{9,8},{11,10},{13,12},{15,14},{17,16},{19,... | collective-permute-start | bytes 49160 | tf_op jit(solution)/shard_map/ppermute | solution.py:19
  77.8 6.5 %collective-permute-start.11 = (bf16[2,4,4,16,128]{4,3,2,1,0:T(8,128)(2,1)S(1)}, bf16[2,4,4,16,128]{4,3,2,1,0:T(8,128)(2,1)S(1)}, u32[]{:S(2)}, u32[]{:S(2)}) collective-permute-start(bf16[2,4,4,16,128]{4,3,2,1,0:T(8,128)(2,1)S(1)} %pad_maximum_fusion.5), channel_id=1, source_target_pairs={{0,4},{4,0},{8,12},{12,8},{1,5},{5,1},{9,13},{13,9},{2,6},{6,2},{1... | collective-permute-start | bytes 393224 | tf_op jit(solution)/shard_map/ppermute | solution.py:128
  80.3 6.9 %collective-permute-start.14 = (bf16[4,4,16,128]{3,2,1,0:T(8,128)(2,1)S(1)}, bf16[4,4,16,128]{3,2,1,0:T(8,128)(2,1)S(1)}, u32[]{:S(2)}, u32[]{:S(2)}) collective-permute-start(bf16[4,4,16,128]{3,2,1,0:T(8,128)(2,1)S(1)} %bitcast.211), channel_id=1, source_target_pairs={{0,12},{4,8},{8,4},{12,0},{1,13},{5,9},{9,5},{13,1},{2,14},{6,10},... | collective-permute-start | bytes 196616 | tf_op jit(solution)/shard_map/ppermute | solution.py:128
  81.7 7.7 %collective-permute-start.9 = (bf16[2,8,20,128]{3,2,1,0:T(8,128)(2,1)S(1)}, bf16[2,8,20,128]{3,2,1,0:T(8,128)(2,1)S(1)}, u32[]{:S(2)}, u32[]{:S(2)}) collective-permute-start(bf16[2,8,20,128]{3,2,1,0:T(8,128)(2,1)S(1)} %pad_maximum_fusion.7), channel_id=1, source_target_pairs={{4,0},{8,4},{12,8},{5,1},{9,5},{13,9},{6,2},{10,6},{14,10},{7,3},{... | collective-permute-start | bytes 245768 | tf_op jit(solution)/shard_map/ppermute | solution.py:27
  85.3 16.0 %collective-permute-start.12 = (bf16[16,4,16,128]{3,2,1,0:T(8,128)(2,1)S(1)}, bf16[16,4,16,128]{3,2,1,0:T(8,128)(2,1)S(1)}, u32[]{:S(2)}, u32[]{:S(2)}) collective-permute-start(bf16[16,4,16,128]{3,2,1,0:T(8,128)(2,1)S(1)} %fusion.7), channel_id=1, source_target_pairs={{0,2},{2,0},{1,3},{3,1},{4,6},{6,4},{5,7},{7,5},{8,10},{10,8},{9,1... | collective-permute-start | bytes 786440 | tf_op jit(solution)/shard_map/ppermute | solution.py:128
  87.2 7.2 %collective-permute-start.15 = (bf16[2,4,4,16,128]{4,3,2,1,0:T(8,128)(2,1)S(1)}, bf16[2,4,4,16,128]{4,3,2,1,0:T(8,128)(2,1)S(1)}, u32[]{:S(2)}, u32[]{:S(2)}) collective-permute-start(bf16[2,4,4,16,128]{4,3,2,1,0:T(8,128)(2,1)S(1)} %pad_maximum_fusion.6), channel_id=1, source_target_pairs={{0,4},{4,0},{8,12},{12,8},{1,5},{5,1},{9,13},{13,9},{2,6},{6,2},{1... | collective-permute-start | bytes 393224 | tf_op jit(solution)/shard_map/ppermute | solution.py:128
  94.2 1.3 %collective-permute-start.18 = (f32[136,128]{1,0:T(8,128)S(1)}, f32[136,128]{1,0:T(8,128)S(1)}, u32[]{:S(2)}, u32[]{:S(2)}) collective-permute-start(f32[136,128]{1,0:T(8,128)S(1)} %pad_maximum_fusion.15), channel_id=1, source_target_pairs={{0,1},{1,0},{2,3},{3,2},{4,5},{5,4},{6,7},{7,6},{8,9},{9,8},{10,11... | collective-permute-start | bytes 208904 | tf_op jit(solution)/shard_map/ppermute | solution.py:128
  95.6 5.1 %collective-permute-start.19 = (f32[136,128]{1,0:T(8,128)S(1)}, f32[136,128]{1,0:T(8,128)S(1)}, u32[]{:S(2)}, u32[]{:S(2)}) collective-permute-start(f32[136,128]{1,0:T(8,128)S(1)} %fusion.17), channel_id=1, source_target_pairs={{0,2},{2,0},{1,3},{3,1},{4,6},{6,4},{5,7},{7,5},{8,10},{10,8},{9,1... | collective-permute-start | bytes 208904 | tf_op jit(solution)/shard_map/ppermute | solution.py:128
  96.1 16.1 %collective-permute-start.16 = (bf16[16,4,16,128]{3,2,1,0:T(8,128)(2,1)S(1)}, bf16[16,4,16,128]{3,2,1,0:T(8,128)(2,1)S(1)}, u32[]{:S(2)}, u32[]{:S(2)}) collective-permute-start(bf16[16,4,16,128]{3,2,1,0:T(8,128)(2,1)S(1)} %fusion.8), channel_id=1, source_target_pairs={{0,2},{2,0},{1,3},{3,1},{4,6},{6,4},{5,7},{7,5},{8,10},{10,8},{9,1... | collective-permute-start | bytes 786440 | tf_op jit(solution)/shard_map/ppermute | solution.py:128
  100.7 4.4 %collective-permute-start.20 = (f32[136,128]{1,0:T(8,128)S(1)}, f32[136,128]{1,0:T(8,128)S(1)}, u32[]{:S(2)}, u32[]{:S(2)}) collective-permute-start(f32[136,128]{1,0:T(8,128)S(1)} %add.453), channel_id=1, source_target_pairs={{0,4},{4,0},{8,12},{12,8},{1,5},{5,1},{9,13},{13,9},{2,6},{6,2},{1... | collective-permute-start | bytes 208904 | tf_op jit(solution)/shard_map/ppermute | solution.py:128
  101.4 11.0 %collective-permute-start.13 = (bf16[16,8,16,128]{3,2,1,0:T(8,128)(2,1)S(1)}, bf16[16,8,16,128]{3,2,1,0:T(8,128)(2,1)S(1)}, u32[]{:S(2)}, u32[]{:S(2)}) collective-permute-start(bf16[16,8,16,128]{3,2,1,0:T(8,128)(2,1)S(1)} %maximum_select_fusion.2), channel_id=1, source_target_pairs={{0,1},{1,0},{2,3},{3,2},{4,5},{5,4},{6,7},{7,6},{8,9},{9,8},{10,11... | collective-permute-start | bytes 1572872 | tf_op jit(solution)/shard_map/ppermute | solution.py:128
  105.1 6.0 %collective-permute-start.21 = (f32[136,128]{1,0:T(8,128)S(1)}, f32[136,128]{1,0:T(8,128)S(1)}, u32[]{:S(2)}, u32[]{:S(2)}) collective-permute-start(f32[136,128]{1,0:T(8,128)S(1)} %add.454), channel_id=1, source_target_pairs={{0,8},{4,12},{8,0},{12,4},{1,9},{5,13},{9,1},{13,5},{2,10},{6,14},... | collective-permute-start | bytes 208904 | tf_op jit(solution)/shard_map/ppermute | solution.py:128
  112.3 4.4 %collective-permute-start.17 = (bf16[16,8,16,128]{3,2,1,0:T(8,128)(2,1)S(1)}, bf16[16,8,16,128]{3,2,1,0:T(8,128)(2,1)S(1)}, u32[]{:S(2)}, u32[]{:S(2)}) collective-permute-start(bf16[16,8,16,128]{3,2,1,0:T(8,128)(2,1)S(1)} %maximum_select_fusion.3), channel_id=1, source_target_pairs={{0,1},{1,0},{2,3},{3,2},{4,5},{5,4},{6,7},{7,6},{8,9},{9,8},{10,11... | collective-permute-start | bytes 1572872 | tf_op jit(solution)/shard_map/ppermute | solution.py:128
  (24 other events, 68.6 us)

commit v2 on v0

--- a/solution.py
+++ b/solution.py
@@ -1,8 +1,11 @@
+import functools
 import math
 
 import jax
 import jax.numpy as jnp
 from jax import lax
+from jax.experimental import pallas as pl
+from jax.experimental.pallas import tpu as pltpu
 from jax.sharding import PartitionSpec as P
 
 OB = 4
@@ -170,9 +173,303 @@
     return (grad_features, grad_kernel, grad_gamma, grad_beta)
 
 
+HIGHEST = lax.Precision.HIGHEST
+F32 = jnp.float32
+BF16 = jnp.bfloat16
+EDGE = 8
+
+
+def exchanged(value, axes, target):
+    names = (axes,) if isinstance(axes, str) else axes
+    sizes = [lax.axis_size(name) for name in names]
+    places = [()]
+    for size in sizes:
+        places = [place + (i,) for place in places for i in range(size)]
+    pairs = []
+    for number, place in enumerate(places):
+        goal = target(*place)
+        if all(0 <= spot < size for spot, size in zip(goal, sizes)):
+            flat = 0
+            for spot, size in zip(goal, sizes):
+                flat = flat * size + spot
+            pairs.append((number, flat))
+    return lax.ppermute(value, names if len(names) > 1 else names[0], pairs)
+
+
+def sum_over(value):
+    value = value + exchanged(value, "gz", lambda z: (1 - z,))
+    value = value + exchanged(value, "gy", lambda y: (1 - y,))
+    value = value + exchanged(value, "gx", lambda x: (x ^ 1,))
+    return value + exchanged(value, "gx", lambda x: (3 - x,))
+
+
+def occupied_rows(occupancy, extent, channels):
+    size_x, size_y, size_z = extent
+    level = lax.broadcasted_iota(jnp.int32, (size_z, channels), 0) // OB
+    layers = []
+    for bx in range(size_x // OB):
+        lines = []
+        for by in range(size_y // OB):
+            column = jnp.zeros((size_z, channels), F32)
+            for bz in range(size_z // OB):
+                value = occupancy[bx, by, bz].astype(F32)
+                column = jnp.where(level == bz, value, column)
+            lines.append(jnp.broadcast_to(column[None, None], (OB, OB, size_z, channels)))
+        layers.append(jnp.concatenate(lines, axis=1) if len(lines) > 1 else lines[0])
+    mask = jnp.concatenate(layers, axis=0) if len(layers) > 1 else layers[0]
+    return mask.reshape(size_x * size_y * size_z, channels)
+
+
+def latent_kernel(features, occupancy, gamma, beta, latent, top, root):
+    size_x, size_y, size_z, channels = features.shape
+    feats = features[...].astype(F32).reshape(-1, channels)
+    energy = beta[...] + jnp.dot(
+        feats * feats, gamma[...], precision=HIGHEST, preferred_element_type=F32
+    )
+    inv_root = lax.rsqrt(energy)
+    root[...] = inv_root
+    occupied = occupied_rows(occupancy, features.shape[:3], channels)
+    rounded = (occupied * feats * inv_root).astype(BF16).reshape(features.shape)
+    latent[...] = rounded
+    top[...] = rounded[size_x - 2 :]
+
+
+def fill_wide(wide, own, side, layers, corner, own_z, side_z, layers_z, corner_z, at_own, at_layers):
+    size_x, size_y, size_z, _ = own.shape
+    first_y = lax.axis_index("gy") == 0
+    first_z = lax.axis_index("gz") == 0
+    to_y = jnp.where(first_y, 2 + size_y, 0)
+    no_y = jnp.where(first_y, 0, 2 + size_y)
+    from_y = jnp.where(first_y, 0, size_y - 2)
+    after = EDGE + size_z
+
+    def put(at_x, at_y, main, across):
+        span = (pl.ds(at_x, main.shape[0]), pl.ds(at_y, main.shape[1]))
+        wide[span + (pl.ds(EDGE, size_z),)] = main.astype(F32)
+        across = across.astype(F32)
+        wide[span + (pl.ds(0, EDGE),)] = jnp.where(first_z, 0.0, across[:, :, size_z - EDGE :])
+        wide[span + (pl.ds(after, EDGE),)] = jnp.where(first_z, across[:, :, :EDGE], 0.0)
+
+    put(at_own, 2, own[...], own_z[...])
+    put(at_layers, 2, layers[...], layers_z[...])
+    two = pl.ds(from_y, 2)
+    put(at_own, to_y, side[:, two], side_z[:, two])
+    put(at_layers, to_y, corner[:, two], corner_z[:, two])
+    blank = (size_x + 2, 2) + wide.shape[2:]
+    wide[:, pl.ds(no_y, 2)] = jnp.zeros(blank, F32)
+
+
+def spread_shifts(wide, shifted, size_z, sign):
+    channels = wide.shape[3]
+    for number in range(5):
+        start = EDGE + sign * (number - 2)
+        shifted[:, :, :, number * channels : (number + 1) * channels] = wide[
+            :, :, start : start + size_z, :
+        ].astype(BF16)
+
+
+def mean_kernel(
+    own, side, layers, corner, own_z, side_z, layers_z, corner_z,
+    kernel, scales, occupancy, grad, bottom, rest, wide, shifted,
+):
+    size_x, size_y, size_z, channels = own.shape
+    fill_wide(wide, own, side, layers, corner, own_z, side_z, layers_z, corner_z, 2, 0)
+    spread_shifts(wide, shifted, size_z, 1)
+    total = jnp.zeros((size_x * size_y * size_z, channels), F32)
+    for along_x, along_y, _, count, first_tap in tap_groups():
+        patch = shifted[
+            2 + along_x : 2 + along_x + size_x,
+            2 + along_y : 2 + along_y + size_y,
+            :,
+            : count * channels,
+        ].reshape(-1, count * channels)
+        weights = kernel[first_tap : first_tap + count].reshape(count * channels, channels)
+        total = total + jnp.dot(patch, weights, preferred_element_type=F32)
+    scale = scales[...].astype(F32).reshape(-1, channels)
+    inverse = 1.0 / (scale * scale)
+    latent = own[...].astype(F32).reshape(-1, channels)
+    difference = (total - latent) * inverse
+    occupied = occupied_rows(occupancy, own.shape[:3], channels)
+    rounded = (occupied * difference).astype(BF16).reshape(own.shape)
+    grad[...] = rounded
+    bottom[...] = rounded[:2]
+    rest[...] = -difference
+
+
+def feature_kernel(
+    own, side, layers, corner, own_z, side_z, layers_z, corner_z,
+    kernel, rest, root, features, gamma, occupancy, grad_features, sums, wide, shifted,
+):
+    size_x, size_y, size_z, channels = own.shape
+    voxels = size_x * size_y * size_z
+    fill_wide(wide, own, side, layers, corner, own_z, side_z, layers_z, corner_z, 0, size_x)
+    spread_shifts(wide, shifted, size_z, -1)
+    total = jnp.zeros((voxels, channels), F32)
+    for along_x, along_y, _, count, first_tap in tap_groups():
+        patch = shifted[
+            -along_x : -along_x + size_x,
+            2 - along_y : 2 - along_y + size_y,
+            :,
+            : count * channels,
+        ].reshape(-1, count * channels)
+        weights = jnp.concatenate([kernel[first_tap + k] for k in range(count)], axis=1)
+        total = total + lax.dot_general(
+            patch, weights, (((1,), (1,)), ((), ())), preferred_element_type=F32
+        )
+    occupied = occupied_rows(occupancy, own.shape[:3], channels)
+    latent_grad = occupied * (total + rest[...])
+    inv_root = root[...]
+    feats = features[...].astype(F32).reshape(voxels, channels)
+    weighted = latent_grad * feats * inv_root * inv_root * inv_root
+    coupled = lax.dot_general(
+        weighted, gamma[...], (((1,), (1,)), ((), ())), precision=HIGHEST, preferred_element_type=F32
+    )
+    grad_features[...] = (latent_grad * inv_root - feats * coupled).astype(BF16).reshape(features.shape)
+    factor = 0.5 / math.sqrt(voxels)
+    sums[:channels] = -factor * jnp.dot(
+        (feats * feats).T, weighted, precision=HIGHEST, preferred_element_type=F32
+    )
+    ones = jnp.sum(weighted, axis=0, keepdims=True)
+    sums[channels:] = -factor * jnp.broadcast_to(ones, (8, channels))
+
+
+def share_kernel(spanned, rows, voxels, *refs):
+    latent_parts, grad_parts = refs[:8], refs[8:16]
+    share, wide, flat, turned, product = refs[16:]
+    size_x, size_y, size_z, channels = latent_parts[0].shape
+    gx, gy, gz = lax.axis_index("gx"), lax.axis_index("gy"), lax.axis_index("gz")
+    all_x, all_y, all_z = wide.shape[0] - 2, wide.shape[1] - 4, wide.shape[2] - 2 * EDGE
+    lines = (wide.shape[1], wide.shape[2], channels)
+    for layer in range(2):
+        wide[layer] = jnp.zeros(lines, F32)
+    for start in (0, 2 + all_y):
+        wide[2:, start : start + 2] = jnp.zeros((all_x, 2, wide.shape[2], channels), F32)
+    for start in (0, EDGE + all_z):
+        wide[2:, 2 : 2 + all_y, start : start + EDGE] = jnp.zeros((all_x, all_y, EDGE, channels), F32)
+
+    def place(parts, store):
+        for across_z in range(2):
+            at_z = pl.multiple_of((gz if across_z == 0 else 1 - gz) * size_z, size_z)
+            for across_y in range(2):
+                at_y = (gy if across_y == 0 else 1 - gy) * size_y
+                single, triple = parts[4 * across_z + 2 * across_y], parts[4 * across_z + 2 * across_y + 1]
+                store(gx * size_x, at_y, at_z, single[...])
+                for other in range(1, 4):
+                    store((gx ^ other) * size_x, at_y, at_z, triple[other - 1])
+
+    def store_latent(at_x, at_y, at_z, value):
+        wide[
+            pl.ds(2 + at_x, size_x), pl.ds(2 + at_y, size_y), pl.ds(pl.multiple_of(EDGE + at_z, EDGE), size_z)
+        ] = value.astype(F32)
+
+    def store_grad(at_x, at_y, at_z, value):
+        flat[pl.ds(at_x, size_x), pl.ds(at_y, size_y), pl.ds(at_z, size_z)] = value
+
+    place(latent_parts, store_latent)
+    place(grad_parts, store_grad)
+    turned[...] = flat[...].reshape(-1, channels).T
+    first_row = ((gx * 2 + gy) * 2 + gz) * rows
+    first_tap = jnp.minimum(first_row // channels, 62 - spanned)
+    for level in range(5):
+        number = lax.rem(level + 5 - lax.rem(first_tap, 5), 5)
+        group = (first_tap + number) // 5
+        along_x, along_y = group // 5, lax.rem(group, 5)
+        start = EDGE + level - 2
+        patch = wide[pl.ds(along_x, all_x), pl.ds(along_y, all_y), start : start + all_z]
+        result = jnp.dot(
+            turned[...], patch.astype(BF16).reshape(-1, channels), preferred_element_type=F32
+        )
+        product[pl.ds(pl.multiple_of(number * channels, channels), channels)] = result.T * (1.0 / voxels)
+    offset = pl.multiple_of(first_row - first_tap * channels, 16)
+    share[...] = product[pl.ds(offset, rows)]
+
+
+def call(body, outs, scratch, smem, args):
+    in_specs = [
+        pl.BlockSpec(memory_space=pltpu.SMEM if n in smem else pltpu.VMEM) for n in range(len(args))
+    ]
+    return pl.pallas_call(
+        body,
+        out_shape=outs,
+        in_specs=in_specs,
+        out_specs=[pl.BlockSpec(memory_space=pltpu.VMEM)] * len(outs),
+        scratch_shapes=scratch,
+    )(*args)
+
+
+def with_neighbours(block, layers, step):
+    flip = lambda i: 1 - i
+    side = exchanged(block, "gy", lambda y: (flip(y),))
+    near = exchanged(layers, "gx", lambda x: (x + step,))
+    corner = exchanged(layers, ("gx", "gy"), lambda x, y: (x + step, flip(y)))
+    mine = (block, side, near, corner)
+    return mine + tuple(exchanged(part, "gz", lambda z: (flip(z),)) for part in mine)
+
+
+def whole_parts(parts):
+    block, side, side_z, block_z = parts[0], parts[1], parts[5], parts[4]
+    others = jnp.stack([exchanged(block, "gx", lambda x, k=k: (x ^ k,)) for k in (1, 2, 3)])
+    others_y = exchanged(others, "gy", lambda y: (1 - y,))
+    others_z = exchanged(others, "gz", lambda z: (1 - z,))
+    others_yz = exchanged(others_y, "gz", lambda z: (1 - z,))
+    return (block, others, side, others_y, block_z, others_z, side_z, others_yz)
+
+
+def fast_local(features, scales, occupancy, kernel, gamma, beta):
+    shape = features.shape
+    size_x, size_y, size_z, channels = shape
+    voxels = size_x * size_y * size_z
+    struct = jax.ShapeDtypeStruct
+    layers = struct((2,) + shape[1:], BF16)
+    rows_f32 = struct((voxels, channels), F32)
+    wide = pltpu.VMEM((size_x + 2, size_y + 4, size_z + 2 * EDGE, channels), F32)
+    shifted = pltpu.VMEM((size_x + 2, size_y + 4, size_z, 5 * channels), BF16)
+    latent, top, root = call(
+        latent_kernel, [struct(shape, BF16), layers, rows_f32], [], (1,),
+        (features, occupancy, gamma, beta.reshape(1, channels)),
+    )
+    latents = with_neighbours(latent, top, 1)
+    grad, bottom, rest = call(
+        mean_kernel, [struct(shape, BF16), layers, rows_f32], [wide, shifted], (10,),
+        latents + (kernel, scales, occupancy),
+    )
+    grads = with_neighbours(grad, bottom, -1)
+    grad_features, sums = call(
+        feature_kernel, [struct(shape, BF16), struct((channels + 8, channels), F32)], [wide, shifted], (13,),
+        grads + (kernel, rest, root, features, gamma, occupancy),
+    )
+    sums = sum_over(sums)
+    devices = 16
+    rows = 62 * channels // devices
+    spanned = 5
+    all_x, all_y, all_z = 4 * size_x, 2 * size_y, 2 * size_z
+    share, = call(
+        functools.partial(share_kernel, spanned, rows, voxels),
+        [struct((rows, channels), F32)],
+        [
+            pltpu.VMEM((all_x + 2, all_y + 4, all_z + 2 * EDGE, channels), F32),
+            pltpu.VMEM((all_x, all_y, all_z, channels), BF16),
+            pltpu.VMEM((channels, all_x * all_y * all_z), BF16),
+            pltpu.VMEM((spanned * channels, channels), F32),
+        ],
+        (),
+        whole_parts(latents) + whole_parts(grads),
+    )
+    return grad_features, share.reshape(-1), sums[:channels], sums[channels]
+
+
+def chosen(features, scales, occupancy, kernel, gamma, beta):
+    sizes = tuple(lax.axis_size(axis) for axis in ("gx", "gy", "gz"))
+    size_x, size_y, size_z, channels = features.shape
+    small = size_x >= 2 and size_y >= 2 and size_z % 16 == 0 and size_x * size_y * size_z <= 1024
+    if sizes == (4, 2, 2) and small and channels == 128:
+        return fast_local(features, scales, occupancy, kernel, gamma, beta)
+    return local(features, scales, occupancy, kernel, gamma, beta)
+
+
 def solution(mesh):
     return jax.shard_map(
-        local,
+        chosen,
         mesh=mesh,
         in_specs=(
             P(("groups", "gx"), "gy", "gz", None),

time: 196 us -> 71.3 us (0.36)
  waiting for transfers between devices: 82.8 us -> 19.1 us
  blocking collectives: 34.5 us -> 0 us
  local copies, waits for them, and re-layouts: 18.6 us -> 3.85 us
  between operations: 15.6 us -> 0.93 us
  Pallas kernels: 0 us -> 14.3 us
  matrix products: 12.9 us -> 0 us
  starting transfers between devices: 24.6 us -> 31.8 us
  other arithmetic: 6.33 us -> 0.97 us
    unnamed x2 -> x0, waiting for transfers between devices: 75.5 us -> none
    psum x1 -> x0, blocking collectives: 34.5 us -> none  [local(): lax.psum((gamma_local, beta_local), ('gx', 'gy', 'gz'))]
    pallas_call x0 -> x4, Pallas kernels: none -> 14.3 us  [call(): pl.pallas_call(body, out_shape=outs, in_specs=in_specs, out_specs=[pl.Blo...]
    dot_general x42 -> x0, matrix products: 12.9 us -> none  [the longest x13 3.77 us: kernel_terms(): lax.dot_general(patch, mean_grad, (((0,), (0,)), ((), ())), preferred_ele...]
    ppermute x10 -> x30, waiting for transfers between devices: 7.27 us -> 19.1 us  [exchanged(): return lax.ppermute(value, names if len(names) > 1 else names[0], pairs)]
    transpose x15 -> x0, local copies, waits for them, and re-layouts: 9.94 us -> none  [context_transposed(): jnp.transpose(kernel[first_tap:first_tap + count], (0, 2, 1))]
    ppermute x10 -> x30, starting transfers between devices: 24.6 us -> 31.8 us  [exchanged(): return lax.ppermute(value, names if len(names) > 1 else names[0], pairs)]
    concatenate x9 -> x0, other arithmetic: 3.34 us -> none  [the longest x5 2.35 us: padded_2(): shard = jnp.concatenate([before, shard, after], axis=dim)]
  transfers between devices with their start and end apart: 11 -> 30, of which waited for: 4 -> 7; matrix products, arithmetic and copies ran while one was open for 11% -> 3% of each run, Pallas kernels for 0% -> 6%
where the time goes in v2:
time: 71.3 us; the launch traced here: 70.9 us
  starting transfers between devices  31.8 us (45%)
  waiting for transfers between devices  19.1 us (27%)
  Pallas kernels  14.3 us (20%)
  local copies, waits for them, and re-layouts  3.85 us (5%)
  other arithmetic  0.97 us (1%)
  between operations  0.93 us (1%)
    ppermute x30, starting transfers between devices, exchanged(): return lax.ppermute(value, names if len(names) > 1 else names[0], pairs)  31.8 us
    ppermute x30, waiting for transfers between devices, exchanged(): return lax.ppermute(value, names if len(names) > 1 else names[0], pairs)  19.1 us
    pallas_call x4, Pallas kernels, call(): pl.pallas_call(body, out_shape=outs, in_specs=in_specs, out_specs=[pl.Blo...  14.3 us
    unnamed x48, local copies, waits for them, and re-layouts  2.7 us
  transfers between devices with their start and end apart: 30, of which 7 were waited for; matrix products, arithmetic and copies ran while one was open for 3% of the time, Pallas kernels for 6%

profile of v2, /device:TPU:0, one launch (start us, length us, event | category | flops | bytes accessed | tf_op | source)
XLA Modules:
  0.0 70.9 jit_solution(13980616158883496669)
XLA Ops:
  0.6 1.8 %shard_map.93 = (bf16[4,4,16,128]{3,2,1,0:T(8,128)(2,1)}, bf16[2,4,16,128]{3,2,1,0:T(8,128)(2,1)}, f32[256,128]{1,0:T(8,128)}) custom-call(bf16[4,4,16,128]{3,2,1,0:T(8,128)(2,1)} %features.3, s32[1,1,4]{2,1,0:T(1,128)} %occupancy.5, f32[128,128]{1,0:T(8,128)} %gamma.3, f32[1,128]{1,0:T(1,128)} %bitcast.17), custom_call_target="tpu_custom_call" | custom-call | tf_op jit(solution)/shard_map/pallas_call | solution.py:391
  2.5 3.0 %collective-permute-start = (bf16[4,4,16,128]{3,2,1,0:T(8,128)(2,1)}, bf16[4,4,16,128]{3,2,1,0:T(8,128)(2,1)S(1)}, u32[]{:S(2)}, u32[]{:S(2)}) collective-permute-start(bf16[4,4,16,128]{3,2,1,0:T(8,128)(2,1)} %get-tuple-element.12.own.refs_0_), channel_id=1, source_target_pairs={{0,2},{2,0},{1,3},{3,1},{4,6},{6,4},{5,7},{7,5},{8,10},{10,8},{9,1... | collective-permute-start | bytes 196616 | tf_op jit(solution)/shard_map/ppermute | solution.py:196
  5.4 3.4 %collective-permute-start.2 = (bf16[2,4,16,128]{3,2,1,0:T(8,128)(2,1)}, bf16[2,4,16,128]{3,2,1,0:T(8,128)(2,1)S(1)}, u32[]{:S(2)}, u32[]{:S(2)}) collective-permute-start(bf16[2,4,16,128]{3,2,1,0:T(8,128)(2,1)} %get-tuple-element.13), channel_id=1, source_target_pairs={{0,6},{2,4},{4,10},{6,8},{8,14},{10,12},{1,7},{3,5},{5,11},{7,9},{... | collective-permute-start | bytes 98312 | tf_op jit(solution)/shard_map/ppermute | solution.py:196
  8.9 3.5 %collective-permute-start.1 = (bf16[2,4,16,128]{3,2,1,0:T(8,128)(2,1)}, bf16[2,4,16,128]{3,2,1,0:T(8,128)(2,1)S(1)}, u32[]{:S(2)}, u32[]{:S(2)}) collective-permute-start(bf16[2,4,16,128]{3,2,1,0:T(8,128)(2,1)} %get-tuple-element.13), channel_id=1, source_target_pairs={{0,4},{4,8},{8,12},{1,5},{5,9},{9,13},{2,6},{6,10},{10,14},{3,7},{... | collective-permute-start | bytes 98312 | tf_op jit(solution)/shard_map/ppermute | solution.py:196
  13.1 1.2 %collective-permute-done.1.layers = bf16[2,4,16,128]{3,2,1,0:T(8,128)(2,1)S(1)} collective-permute-done((bf16[2,4,16,128]{3,2,1,0:T(8,128)(2,1)}, bf16[2,4,16,128]{3,2,1,0:T(8,128)(2,1)S(1)}, u32[]{:S(2)}, u32[]{:S(2)}) %collective-permute-start.1) | collective-permute-done | bytes 32800 | tf_op jit(solution)/shard_map/ppermute | solution.py:196
  14.3 1.2 %collective-permute-done.5.layers_z = bf16[2,4,16,128]{3,2,1,0:T(8,128)(2,1)S(1)} collective-permute-done((bf16[2,4,16,128]{3,2,1,0:T(8,128)(2,1)S(1)}, bf16[2,4,16,128]{3,2,1,0:T(8,128)(2,1)S(1)}, u32[]{:S(2)}, u32[]{:S(2)}) %collective-permute-start.5) | collective-permute-done | bytes 32800 | tf_op jit(solution)/shard_map/ppermute | solution.py:196
  16.1 0.6 copy-done.5
  16.7 3.8 %shard_map.94 = (bf16[4,4,16,128]{3,2,1,0:T(8,128)(2,1)}, bf16[2,4,16,128]{3,2,1,0:T(8,128)(2,1)}, f32[256,128]{1,0:T(8,128)}) custom-call(bf16[4,4,16,128]{3,2,1,0:T(8,128)(2,1)} %get-tuple-element.12.own.refs_0_, bf16[4,4,16,128]{3,2,1,0:T(8,128)(2,1)} %copy-done.3, bf16[2,4,16,128]{3,2,1,0:T(8,128)(2,1)} %copy-done.20, ...), custom_call_target="tpu_custom_call" | custom-call | tf_op jit(solution)/shard_map/pallas_call | solution.py:391
  20.5 1.5 %collective-permute-start.7 = (bf16[4,4,16,128]{3,2,1,0:T(8,128)(2,1)}, bf16[4,4,16,128]{3,2,1,0:T(8,128)(2,1)S(1)}, u32[]{:S(2)}, u32[]{:S(2)}) collective-permute-start(bf16[4,4,16,128]{3,2,1,0:T(8,128)(2,1)} %get-tuple-element.14.own.refs_8_), channel_id=1, source_target_pairs={{0,2},{2,0},{1,3},{3,1},{4,6},{6,4},{5,7},{7,5},{8,10},{10,8},{9,1... | collective-permute-start | bytes 196616 | tf_op jit(solution)/shard_map/ppermute | solution.py:196
  22.0 1.3 %collective-permute-start.9 = (bf16[2,4,16,128]{3,2,1,0:T(8,128)(2,1)}, bf16[2,4,16,128]{3,2,1,0:T(8,128)(2,1)S(1)}, u32[]{:S(2)}, u32[]{:S(2)}) collective-permute-start(bf16[2,4,16,128]{3,2,1,0:T(8,128)(2,1)} %get-tuple-element.15), channel_id=1, source_target_pairs={{4,2},{6,0},{8,6},{10,4},{12,10},{14,8},{5,3},{7,1},{9,7},{11,5},{... | collective-permute-start | bytes 98312 | tf_op jit(solution)/shard_map/ppermute | solution.py:196
  23.3 1.3 %collective-permute-start.8 = (bf16[2,4,16,128]{3,2,1,0:T(8,128)(2,1)}, bf16[2,4,16,128]{3,2,1,0:T(8,128)(2,1)S(1)}, u32[]{:S(2)}, u32[]{:S(2)}) collective-permute-start(bf16[2,4,16,128]{3,2,1,0:T(8,128)(2,1)} %get-tuple-element.15), channel_id=1, source_target_pairs={{4,0},{8,4},{12,8},{5,1},{9,5},{13,9},{6,2},{10,6},{14,10},{7,3},{... | collective-permute-start | bytes 98312 | tf_op jit(solution)/shard_map/ppermute | solution.py:196
  24.6 4.3 %collective-permute-done.9.corner = bf16[2,4,16,128]{3,2,1,0:T(8,128)(2,1)S(1)} collective-permute-done((bf16[2,4,16,128]{3,2,1,0:T(8,128)(2,1)}, bf16[2,4,16,128]{3,2,1,0:T(8,128)(2,1)S(1)}, u32[]{:S(2)}, u32[]{:S(2)}) %collective-permute-start.9) | collective-permute-done | bytes 32800 | tf_op jit(solution)/shard_map/ppermute | solution.py:196
  29.5 2.1 %collective-permute-start.16 = (bf16[4,4,16,128]{3,2,1,0:T(8,128)(2,1)S(1)}, bf16[4,4,16,128]{3,2,1,0:T(8,128)(2,1)S(1)}, u32[]{:S(2)}, u32[]{:S(2)}) collective-permute-start(bf16[4,4,16,128]{3,2,1,0:T(8,128)(2,1)S(1)} %copy-done.2), channel_id=1, source_target_pairs={{0,12},{4,8},{8,4},{12,0},{1,13},{5,9},{9,5},{13,1},{2,14},{6,10},... | collective-permute-start | bytes 196616 | tf_op jit(solution)/shard_map/ppermute | solution.py:196
  31.6 2.0 %collective-permute-start.15 = (bf16[4,4,16,128]{3,2,1,0:T(8,128)(2,1)S(1)}, bf16[4,4,16,128]{3,2,1,0:T(8,128)(2,1)S(1)}, u32[]{:S(2)}, u32[]{:S(2)}) collective-permute-start(bf16[4,4,16,128]{3,2,1,0:T(8,128)(2,1)S(1)} %copy-done.2), channel_id=1, source_target_pairs={{0,8},{4,12},{8,0},{12,4},{1,9},{5,13},{9,1},{13,5},{2,10},{6,14},... | collective-permute-start | bytes 196616 | tf_op jit(solution)/shard_map/ppermute | solution.py:196
  33.9 1.2 %collective-permute-done.12.layers_z = bf16[2,4,16,128]{3,2,1,0:T(8,128)(2,1)S(1)} collective-permute-done((bf16[2,4,16,128]{3,2,1,0:T(8,128)(2,1)S(1)}, bf16[2,4,16,128]{3,2,1,0:T(8,128)(2,1)S(1)}, u32[]{:S(2)}, u32[]{:S(2)}) %collective-permute-start.12) | collective-permute-done | bytes 32800 | tf_op jit(solution)/shard_map/ppermute | solution.py:196
  35.1 2.1 %collective-permute-start.22 = (bf16[4,4,16,128]{3,2,1,0:T(8,128)(2,1)}, bf16[4,4,16,128]{3,2,1,0:T(8,128)(2,1)S(1)}, u32[]{:S(2)}, u32[]{:S(2)}) collective-permute-start(bf16[4,4,16,128]{3,2,1,0:T(8,128)(2,1)} %get-tuple-element.14.own.refs_8_), channel_id=1, source_target_pairs={{0,12},{4,8},{8,4},{12,0},{1,13},{5,9},{9,5},{13,1},{2,14},{6,10},... | collective-permute-start | bytes 196616 | tf_op jit(solution)/shard_map/ppermute | solution.py:196
  37.2 1.1 %collective-permute-start.21 = (bf16[4,4,16,128]{3,2,1,0:T(8,128)(2,1)}, bf16[4,4,16,128]{3,2,1,0:T(8,128)(2,1)S(1)}, u32[]{:S(2)}, u32[]{:S(2)}) collective-permute-start(bf16[4,4,16,128]{3,2,1,0:T(8,128)(2,1)} %get-tuple-element.14.own.refs_8_), channel_id=1, source_target_pairs={{0,8},{4,12},{8,0},{12,4},{1,9},{5,13},{9,1},{13,5},{2,10},{6,14},... | collective-permute-start | bytes 196616 | tf_op jit(solution)/shard_map/ppermute | solution.py:196
  38.4 4.2 %shard_map.95 = (bf16[4,4,16,128]{3,2,1,0:T(8,128)(2,1)}, f32[136,128]{1,0:T(8,128)}) custom-call(bf16[4,4,16,128]{3,2,1,0:T(8,128)(2,1)} %get-tuple-element.14.own.refs_8_, bf16[4,4,16,128]{3,2,1,0:T(8,128)(2,1)} %copy-done.7, bf16[2,4,16,128]{3,2,1,0:T(8,128)(2,1)} %copy-done.17, bf16[2,4,16,128]{3,2,1,0:T(8,128)(2,1)} %copy-done.16, ...), custom_call_target="tpu_custom_call" | custom-call | tf_op jit(solution)/shard_map/pallas_call | solution.py:391
  42.6 1.2 %collective-permute-start.20 = (bf16[4,4,16,128]{3,2,1,0:T(8,128)(2,1)S(1)}, bf16[4,4,16,128]{3,2,1,0:T(8,128)(2,1)S(1)}, u32[]{:S(2)}, u32[]{:S(2)}) collective-permute-start(bf16[4,4,16,128]{3,2,1,0:T(8,128)(2,1)S(1)} %copy-done.6), channel_id=1, source_target_pairs={{0,4},{4,0},{8,12},{12,8},{1,5},{5,1},{9,13},{13,9},{2,6},{6,2},{1... | collective-permute-start | bytes 196616 | tf_op jit(solution)/shard_map/ppermute | solution.py:196
  43.9 1.4 %collective-permute-start.17 = (bf16[3,4,4,16,128]{4,3,2,1,0:T(8,128)(2,1)S(1)}, bf16[3,4,4,16,128]{4,3,2,1,0:T(8,128)(2,1)S(1)}, u32[]{:S(2)}, u32[]{:S(2)}) collective-permute-start(bf16[3,4,4,16,128]{4,3,2,1,0:T(8,128)(2,1)S(1)} %pad_maximum_fusion.refs_1_), channel_id=1, source_target_pairs={{0,2},{2,0},{1,3},{3,1},{4,6},{6,4},{5,7},{7,5},{8,10},{10,8},{9,1... | collective-permute-start | bytes 589832 | tf_op jit(solution)/shard_map/ppermute | solution.py:196
  45.3 0.9 %add.12 = f32[136,128]{1,0:T(8,128)S(1)} add(f32[136,128]{1,0:T(8,128)} %get-tuple-element.19, f32[136,128]{1,0:T(8,128)S(1)} %collective-permute-done.26) | non-fusion elementwise | flops 17408 | bytes 208896 | tf_op jit(solution)/shard_map/add | solution.py:200
  46.2 1.4 %collective-permute-start.27 = (f32[136,128]{1,0:T(8,128)S(1)}, f32[136,128]{1,0:T(8,128)S(1)}, u32[]{:S(2)}, u32[]{:S(2)}) collective-permute-start(f32[136,128]{1,0:T(8,128)S(1)} %add.12), channel_id=1, source_target_pairs={{0,2},{2,0},{1,3},{3,1},{4,6},{6,4},{5,7},{7,5},{8,10},{10,8},{9,1... | collective-permute-start | bytes 208904 | tf_op jit(solution)/shard_map/ppermute | solution.py:196
  47.7 0.9 %collective-permute-start.23 = (bf16[3,4,4,16,128]{4,3,2,1,0:T(8,128)(2,1)S(1)}, bf16[3,4,4,16,128]{4,3,2,1,0:T(8,128)(2,1)S(1)}, u32[]{:S(2)}, u32[]{:S(2)}) collective-permute-start(bf16[3,4,4,16,128]{4,3,2,1,0:T(8,128)(2,1)S(1)} %pad_maximum_fusion.1.refs_9_), channel_id=1, source_target_pairs={{0,2},{2,0},{1,3},{3,1},{4,6},{6,4},{5,7},{7,5},{8,10},{10,8},{9,1... | collective-permute-start | bytes 589832 | tf_op jit(solution)/shard_map/ppermute | solution.py:196
  48.6 4.7 %collective-permute-done.27 = f32[136,128]{1,0:T(8,128)S(1)} collective-permute-done((f32[136,128]{1,0:T(8,128)S(1)}, f32[136,128]{1,0:T(8,128)S(1)}, u32[]{:S(2)}, u32[]{:S(2)}) %collective-permute-start.27) | collective-permute-done | bytes 69664 | tf_op jit(solution)/shard_map/ppermute | solution.py:196
  53.2 0.9 %collective-permute-start.28 = (f32[136,128]{1,0:T(8,128)S(1)}, f32[136,128]{1,0:T(8,128)S(1)}, u32[]{:S(2)}, u32[]{:S(2)}) collective-permute-start(f32[136,128]{1,0:T(8,128)S(1)} %add.13), channel_id=1, source_target_pairs={{0,4},{4,0},{8,12},{12,8},{1,5},{5,1},{9,13},{13,9},{2,6},{6,2},{1... | collective-permute-start | bytes 208904 | tf_op jit(solution)/shard_map/ppermute | solution.py:196
  54.2 3.4 %collective-permute-done.28 = f32[136,128]{1,0:T(8,128)S(1)} collective-permute-done((f32[136,128]{1,0:T(8,128)S(1)}, f32[136,128]{1,0:T(8,128)S(1)}, u32[]{:S(2)}, u32[]{:S(2)}) %collective-permute-start.28) | collective-permute-done | bytes 69664 | tf_op jit(solution)/shard_map/ppermute | solution.py:196
  57.6 2.2 %collective-permute-start.29 = (f32[136,128]{1,0:T(8,128)S(1)}, f32[136,128]{1,0:T(8,128)S(1)}, u32[]{:S(2)}, u32[]{:S(2)}) collective-permute-start(f32[136,128]{1,0:T(8,128)S(1)} %add.14), channel_id=1, source_target_pairs={{0,12},{4,8},{8,4},{12,0},{1,13},{5,9},{9,5},{13,1},{2,14},{6,10},... | collective-permute-start | bytes 208904 | tf_op jit(solution)/shard_map/ppermute | solution.py:196
  60.8 3.0 %collective-permute-done.29 = f32[136,128]{1,0:T(8,128)S(1)} collective-permute-done((f32[136,128]{1,0:T(8,128)S(1)}, f32[136,128]{1,0:T(8,128)S(1)}, u32[]{:S(2)}, u32[]{:S(2)}) %collective-permute-start.29) | collective-permute-done | bytes 69664 | tf_op jit(solution)/shard_map/ppermute | solution.py:196
  63.8 0.6 slice.8
  65.1 0.6 copy-done.12
  65.8 0.7 copy-done.15
  66.5 4.4 %shard_map.96 = f32[496,128]{1,0:T(8,128)} custom-call(bf16[4,4,16,128]{3,2,1,0:T(8,128)(2,1)} %get-tuple-element.12.own.refs_0_, bf16[3,4,4,16,128]{4,3,2,1,0:T(8,128)(2,1)} %copy-done, bf16[4,4,16,128]{3,2,1,0:T(8,128)(2,1)} %copy-done.3, bf16[3,4,4,16,128]{4,3,2,1,0:T(8,128)(2,1)} %copy-done.10, bf16[4,4,16,128]{3,2,1,0:T(8,128)(2,1)} %copy-done.4, ...), custom_call_target="tpu_custom_call" | custom-call | tf_op jit(solution)/shard_map/pallas_call | solution.py:391
  (88 shorter events, 3.9 us)
Async XLA Ops:
  2.5 27.0 %copy-start.2 = (bf16[4,4,16,128]{3,2,1,0:T(8,128)(2,1)S(1)}, bf16[4,4,16,128]{3,2,1,0:T(8,128)(2,1)}, u32[]{:S(2)}) copy-start(bf16[4,4,16,128]{3,2,1,0:T(8,128)(2,1)} %get-tuple-element.12.own.refs_0_) | copy-start | bytes 196612
  2.5 10.0 %collective-permute-start = (bf16[4,4,16,128]{3,2,1,0:T(8,128)(2,1)}, bf16[4,4,16,128]{3,2,1,0:T(8,128)(2,1)S(1)}, u32[]{:S(2)}, u32[]{:S(2)}) collective-permute-start(bf16[4,4,16,128]{3,2,1,0:T(8,128)(2,1)} %get-tuple-element.12.own.refs_0_), channel_id=1, source_target_pairs={{0,2},{2,0},{1,3},{3,1},{4,6},{6,4},{5,7},{7,5},{8,10},{10,8},{9,1... | collective-permute-start | bytes 196616 | tf_op jit(solution)/shard_map/ppermute | solution.py:196
  5.4 7.5 %collective-permute-start.2 = (bf16[2,4,16,128]{3,2,1,0:T(8,128)(2,1)}, bf16[2,4,16,128]{3,2,1,0:T(8,128)(2,1)S(1)}, u32[]{:S(2)}, u32[]{:S(2)}) collective-permute-start(bf16[2,4,16,128]{3,2,1,0:T(8,128)(2,1)} %get-tuple-element.13), channel_id=1, source_target_pairs={{0,6},{2,4},{4,10},{6,8},{8,14},{10,12},{1,7},{3,5},{5,11},{7,9},{... | collective-permute-start | bytes 98312 | tf_op jit(solution)/shard_map/ppermute | solution.py:196
  8.9 5.4 %collective-permute-start.1 = (bf16[2,4,16,128]{3,2,1,0:T(8,128)(2,1)}, bf16[2,4,16,128]{3,2,1,0:T(8,128)(2,1)S(1)}, u32[]{:S(2)}, u32[]{:S(2)}) collective-permute-start(bf16[2,4,16,128]{3,2,1,0:T(8,128)(2,1)} %get-tuple-element.13), channel_id=1, source_target_pairs={{0,4},{4,8},{8,12},{1,5},{5,9},{9,13},{2,6},{6,10},{10,14},{3,7},{... | collective-permute-start | bytes 98312 | tf_op jit(solution)/shard_map/ppermute | solution.py:196
  12.4 3.1 %collective-permute-start.3 = (bf16[4,4,16,128]{3,2,1,0:T(8,128)(2,1)}, bf16[4,4,16,128]{3,2,1,0:T(8,128)(2,1)S(1)}, u32[]{:S(2)}, u32[]{:S(2)}) collective-permute-start(bf16[4,4,16,128]{3,2,1,0:T(8,128)(2,1)} %get-tuple-element.12.own.refs_0_), channel_id=1, source_target_pairs={{0,1},{1,0},{2,3},{3,2},{4,5},{5,4},{6,7},{7,6},{8,9},{9,8},{10,11... | collective-permute-start | bytes 196616 | tf_op jit(solution)/shard_map/ppermute | solution.py:196
  12.5 3.0 %collective-permute-start.4 = (bf16[4,4,16,128]{3,2,1,0:T(8,128)(2,1)S(1)}, bf16[4,4,16,128]{3,2,1,0:T(8,128)(2,1)S(1)}, u32[]{:S(2)}, u32[]{:S(2)}) collective-permute-start(bf16[4,4,16,128]{3,2,1,0:T(8,128)(2,1)S(1)} %collective-permute-done.side.refs_2_), channel_id=1, source_target_pairs={{0,1},{1,0},{2,3},{3,2},{4,5},{5,4},{6,7},{7,6},{8,9},{9,8},{10,11... | collective-permute-start | bytes 196616 | tf_op jit(solution)/shard_map/ppermute | solution.py:196
  13.0 1.3 %collective-permute-start.6 = (bf16[2,4,16,128]{3,2,1,0:T(8,128)(2,1)S(1)}, bf16[2,4,16,128]{3,2,1,0:T(8,128)(2,1)S(1)}, u32[]{:S(2)}, u32[]{:S(2)}) collective-permute-start(bf16[2,4,16,128]{3,2,1,0:T(8,128)(2,1)S(1)} %collective-permute-done.2.corner), channel_id=1, source_target_pairs={{0,1},{1,0},{2,3},{3,2},{4,5},{5,4},{6,7},{7,6},{8,9},{9,8},{10,11... | collective-permute-start | bytes 98312 | tf_op jit(solution)/shard_map/ppermute | solution.py:196
  14.3 1.2 %collective-permute-start.5 = (bf16[2,4,16,128]{3,2,1,0:T(8,128)(2,1)S(1)}, bf16[2,4,16,128]{3,2,1,0:T(8,128)(2,1)S(1)}, u32[]{:S(2)}, u32[]{:S(2)}) collective-permute-start(bf16[2,4,16,128]{3,2,1,0:T(8,128)(2,1)S(1)} %collective-permute-done.1.layers), channel_id=1, source_target_pairs={{0,1},{1,0},{2,3},{3,2},{4,5},{5,4},{6,7},{7,6},{8,9},{9,8},{10,11... | collective-permute-start | bytes 98312 | tf_op jit(solution)/shard_map/ppermute | solution.py:196
  20.5 22.1 %copy-start.6 = (bf16[4,4,16,128]{3,2,1,0:T(8,128)(2,1)S(1)}, bf16[4,4,16,128]{3,2,1,0:T(8,128)(2,1)}, u32[]{:S(2)}) copy-start(bf16[4,4,16,128]{3,2,1,0:T(8,128)(2,1)} %get-tuple-element.14.own.refs_8_) | copy-start | bytes 196612
  20.5 8.4 %collective-permute-start.7 = (bf16[4,4,16,128]{3,2,1,0:T(8,128)(2,1)}, bf16[4,4,16,128]{3,2,1,0:T(8,128)(2,1)S(1)}, u32[]{:S(2)}, u32[]{:S(2)}) collective-permute-start(bf16[4,4,16,128]{3,2,1,0:T(8,128)(2,1)} %get-tuple-element.14.own.refs_8_), channel_id=1, source_target_pairs={{0,2},{2,0},{1,3},{3,1},{4,6},{6,4},{5,7},{7,5},{8,10},{10,8},{9,1... | collective-permute-start | bytes 196616 | tf_op jit(solution)/shard_map/ppermute | solution.py:196
  22.0 11.6 %collective-permute-start.10 = (bf16[4,4,16,128]{3,2,1,0:T(8,128)(2,1)}, bf16[4,4,16,128]{3,2,1,0:T(8,128)(2,1)S(1)}, u32[]{:S(2)}, u32[]{:S(2)}) collective-permute-start(bf16[4,4,16,128]{3,2,1,0:T(8,128)(2,1)} %get-tuple-element.14.own.refs_8_), channel_id=1, source_target_pairs={{0,1},{1,0},{2,3},{3,2},{4,5},{5,4},{6,7},{7,6},{8,9},{9,8},{10,11... | collective-permute-start | bytes 196616 | tf_op jit(solution)/shard_map/ppermute | solution.py:196
  22.0 6.9 %collective-permute-start.9 = (bf16[2,4,16,128]{3,2,1,0:T(8,128)(2,1)}, bf16[2,4,16,128]{3,2,1,0:T(8,128)(2,1)S(1)}, u32[]{:S(2)}, u32[]{:S(2)}) collective-permute-start(bf16[2,4,16,128]{3,2,1,0:T(8,128)(2,1)} %get-tuple-element.15), channel_id=1, source_target_pairs={{4,2},{6,0},{8,6},{10,4},{12,10},{14,8},{5,3},{7,1},{9,7},{11,5},{... | collective-permute-start | bytes 98312 | tf_op jit(solution)/shard_map/ppermute | solution.py:196
  23.3 8.2 %collective-permute-start.8 = (bf16[2,4,16,128]{3,2,1,0:T(8,128)(2,1)}, bf16[2,4,16,128]{3,2,1,0:T(8,128)(2,1)S(1)}, u32[]{:S(2)}, u32[]{:S(2)}) collective-permute-start(bf16[2,4,16,128]{3,2,1,0:T(8,128)(2,1)} %get-tuple-element.15), channel_id=1, source_target_pairs={{4,0},{8,4},{12,8},{5,1},{9,5},{13,9},{6,2},{10,6},{14,10},{7,3},{... | collective-permute-start | bytes 98312 | tf_op jit(solution)/shard_map/ppermute | solution.py:196
  29.0 4.9 %collective-permute-start.13 = (bf16[2,4,16,128]{3,2,1,0:T(8,128)(2,1)S(1)}, bf16[2,4,16,128]{3,2,1,0:T(8,128)(2,1)S(1)}, u32[]{:S(2)}, u32[]{:S(2)}) collective-permute-start(bf16[2,4,16,128]{3,2,1,0:T(8,128)(2,1)S(1)} %collective-permute-done.9.corner), channel_id=1, source_target_pairs={{0,1},{1,0},{2,3},{3,2},{4,5},{5,4},{6,7},{7,6},{8,9},{9,8},{10,11... | collective-permute-start | bytes 98312 | tf_op jit(solution)/shard_map/ppermute | solution.py:196
  29.0 8.2 %collective-permute-start.11 = (bf16[4,4,16,128]{3,2,1,0:T(8,128)(2,1)S(1)}, bf16[4,4,16,128]{3,2,1,0:T(8,128)(2,1)S(1)}, u32[]{:S(2)}, u32[]{:S(2)}) collective-permute-start(bf16[4,4,16,128]{3,2,1,0:T(8,128)(2,1)S(1)} %collective-permute-done.7.side.refs_10_), channel_id=1, source_target_pairs={{0,1},{1,0},{2,3},{3,2},{4,5},{5,4},{6,7},{7,6},{8,9},{9,8},{10,11... | collective-permute-start | bytes 196616 | tf_op jit(solution)/shard_map/ppermute | solution.py:196
  29.5 13.1 %collective-permute-start.16 = (bf16[4,4,16,128]{3,2,1,0:T(8,128)(2,1)S(1)}, bf16[4,4,16,128]{3,2,1,0:T(8,128)(2,1)S(1)}, u32[]{:S(2)}, u32[]{:S(2)}) collective-permute-start(bf16[4,4,16,128]{3,2,1,0:T(8,128)(2,1)S(1)} %copy-done.2), channel_id=1, source_target_pairs={{0,12},{4,8},{8,4},{12,0},{1,13},{5,9},{9,5},{13,1},{2,14},{6,10},... | collective-permute-start | bytes 196616 | tf_op jit(solution)/shard_map/ppermute | solution.py:196
  31.6 12.3 %collective-permute-start.15 = (bf16[4,4,16,128]{3,2,1,0:T(8,128)(2,1)S(1)}, bf16[4,4,16,128]{3,2,1,0:T(8,128)(2,1)S(1)}, u32[]{:S(2)}, u32[]{:S(2)}) collective-permute-start(bf16[4,4,16,128]{3,2,1,0:T(8,128)(2,1)S(1)} %copy-done.2), channel_id=1, source_target_pairs={{0,8},{4,12},{8,0},{12,4},{1,9},{5,13},{9,1},{13,5},{2,10},{6,14},... | collective-permute-start | bytes 196616 | tf_op jit(solution)/shard_map/ppermute | solution.py:196
  33.6 10.2 %collective-permute-start.14 = (bf16[4,4,16,128]{3,2,1,0:T(8,128)(2,1)S(1)}, bf16[4,4,16,128]{3,2,1,0:T(8,128)(2,1)S(1)}, u32[]{:S(2)}, u32[]{:S(2)}) collective-permute-start(bf16[4,4,16,128]{3,2,1,0:T(8,128)(2,1)S(1)} %copy-done.2), channel_id=1, source_target_pairs={{0,4},{4,0},{8,12},{12,8},{1,5},{5,1},{9,13},{13,9},{2,6},{6,2},{1... | collective-permute-start | bytes 196616 | tf_op jit(solution)/shard_map/ppermute | solution.py:196
  33.9 1.2 %collective-permute-start.12 = (bf16[2,4,16,128]{3,2,1,0:T(8,128)(2,1)S(1)}, bf16[2,4,16,128]{3,2,1,0:T(8,128)(2,1)S(1)}, u32[]{:S(2)}, u32[]{:S(2)}) collective-permute-start(bf16[2,4,16,128]{3,2,1,0:T(8,128)(2,1)S(1)} %collective-permute-done.8.layers), channel_id=1, source_target_pairs={{0,1},{1,0},{2,3},{3,2},{4,5},{5,4},{6,7},{7,6},{8,9},{9,8},{10,11... | collective-permute-start | bytes 98312 | tf_op jit(solution)/shard_map/ppermute | solution.py:196
  35.1 12.5 %collective-permute-start.22 = (bf16[4,4,16,128]{3,2,1,0:T(8,128)(2,1)}, bf16[4,4,16,128]{3,2,1,0:T(8,128)(2,1)S(1)}, u32[]{:S(2)}, u32[]{:S(2)}) collective-permute-start(bf16[4,4,16,128]{3,2,1,0:T(8,128)(2,1)} %get-tuple-element.14.own.refs_8_), channel_id=1, source_target_pairs={{0,12},{4,8},{8,4},{12,0},{1,13},{5,9},{9,5},{13,1},{2,14},{6,10},... | collective-permute-start | bytes 196616 | tf_op jit(solution)/shard_map/ppermute | solution.py:196
  37.2 10.4 %collective-permute-start.21 = (bf16[4,4,16,128]{3,2,1,0:T(8,128)(2,1)}, bf16[4,4,16,128]{3,2,1,0:T(8,128)(2,1)S(1)}, u32[]{:S(2)}, u32[]{:S(2)}) collective-permute-start(bf16[4,4,16,128]{3,2,1,0:T(8,128)(2,1)} %get-tuple-element.14.own.refs_8_), channel_id=1, source_target_pairs={{0,8},{4,12},{8,0},{12,4},{1,9},{5,13},{9,1},{13,5},{2,10},{6,14},... | collective-permute-start | bytes 196616 | tf_op jit(solution)/shard_map/ppermute | solution.py:196
  42.6 5.0 %collective-permute-start.20 = (bf16[4,4,16,128]{3,2,1,0:T(8,128)(2,1)S(1)}, bf16[4,4,16,128]{3,2,1,0:T(8,128)(2,1)S(1)}, u32[]{:S(2)}, u32[]{:S(2)}) collective-permute-start(bf16[4,4,16,128]{3,2,1,0:T(8,128)(2,1)S(1)} %copy-done.6), channel_id=1, source_target_pairs={{0,4},{4,0},{8,12},{12,8},{1,5},{5,1},{9,13},{13,9},{2,6},{6,2},{1... | collective-permute-start | bytes 196616 | tf_op jit(solution)/shard_map/ppermute | solution.py:196
  43.9 1.5 %collective-permute-start.26 = (f32[136,128]{1,0:T(8,128)}, f32[136,128]{1,0:T(8,128)S(1)}, u32[]{:S(2)}, u32[]{:S(2)}) collective-permute-start(f32[136,128]{1,0:T(8,128)} %get-tuple-element.19), channel_id=1, source_target_pairs={{0,1},{1,0},{2,3},{3,2},{4,5},{5,4},{6,7},{7,6},{8,9},{9,8},{10,11... | collective-permute-start | bytes 208904 | tf_op jit(solution)/shard_map/ppermute | solution.py:196
  43.9 16.4 %collective-permute-start.17 = (bf16[3,4,4,16,128]{4,3,2,1,0:T(8,128)(2,1)S(1)}, bf16[3,4,4,16,128]{4,3,2,1,0:T(8,128)(2,1)S(1)}, u32[]{:S(2)}, u32[]{:S(2)}) collective-permute-start(bf16[3,4,4,16,128]{4,3,2,1,0:T(8,128)(2,1)S(1)} %pad_maximum_fusion.refs_1_), channel_id=1, source_target_pairs={{0,2},{2,0},{1,3},{3,1},{4,6},{6,4},{5,7},{7,5},{8,10},{10,8},{9,1... | collective-permute-start | bytes 589832 | tf_op jit(solution)/shard_map/ppermute | solution.py:196
  46.2 7.0 %collective-permute-start.27 = (f32[136,128]{1,0:T(8,128)S(1)}, f32[136,128]{1,0:T(8,128)S(1)}, u32[]{:S(2)}, u32[]{:S(2)}) collective-permute-start(f32[136,128]{1,0:T(8,128)S(1)} %add.12), channel_id=1, source_target_pairs={{0,2},{2,0},{1,3},{3,1},{4,6},{6,4},{5,7},{7,5},{8,10},{10,8},{9,1... | collective-permute-start | bytes 208904 | tf_op jit(solution)/shard_map/ppermute | solution.py:196
  47.7 12.7 %collective-permute-start.23 = (bf16[3,4,4,16,128]{4,3,2,1,0:T(8,128)(2,1)S(1)}, bf16[3,4,4,16,128]{4,3,2,1,0:T(8,128)(2,1)S(1)}, u32[]{:S(2)}, u32[]{:S(2)}) collective-permute-start(bf16[3,4,4,16,128]{4,3,2,1,0:T(8,128)(2,1)S(1)} %pad_maximum_fusion.1.refs_9_), channel_id=1, source_target_pairs={{0,2},{2,0},{1,3},{3,1},{4,6},{6,4},{5,7},{7,5},{8,10},{10,8},{9,1... | collective-permute-start | bytes 589832 | tf_op jit(solution)/shard_map/ppermute | solution.py:196
  53.2 4.4 %collective-permute-start.28 = (f32[136,128]{1,0:T(8,128)S(1)}, f32[136,128]{1,0:T(8,128)S(1)}, u32[]{:S(2)}, u32[]{:S(2)}) collective-permute-start(f32[136,128]{1,0:T(8,128)S(1)} %add.13), channel_id=1, source_target_pairs={{0,4},{4,0},{8,12},{12,8},{1,5},{5,1},{9,13},{13,9},{2,6},{6,2},{1... | collective-permute-start | bytes 208904 | tf_op jit(solution)/shard_map/ppermute | solution.py:196
  57.6 6.2 %collective-permute-start.29 = (f32[136,128]{1,0:T(8,128)S(1)}, f32[136,128]{1,0:T(8,128)S(1)}, u32[]{:S(2)}, u32[]{:S(2)}) collective-permute-start(f32[136,128]{1,0:T(8,128)S(1)} %add.14), channel_id=1, source_target_pairs={{0,12},{4,8},{8,4},{12,0},{1,13},{5,9},{9,5},{13,1},{2,14},{6,10},... | collective-permute-start | bytes 208904 | tf_op jit(solution)/shard_map/ppermute | solution.py:196
  59.8 5.2 %collective-permute-start.18 = (bf16[3,4,4,16,128]{4,3,2,1,0:T(8,128)(2,1)S(1)}, bf16[3,4,4,16,128]{4,3,2,1,0:T(8,128)(2,1)S(1)}, u32[]{:S(2)}, u32[]{:S(2)}) collective-permute-start(bf16[3,4,4,16,128]{4,3,2,1,0:T(8,128)(2,1)S(1)} %pad_maximum_fusion.refs_1_), channel_id=1, source_target_pairs={{0,1},{1,0},{2,3},{3,2},{4,5},{5,4},{6,7},{7,6},{8,9},{9,8},{10,11... | collective-permute-start | bytes 589832 | tf_op jit(solution)/shard_map/ppermute | solution.py:196
  59.8 5.2 %collective-permute-start.24 = (bf16[3,4,4,16,128]{4,3,2,1,0:T(8,128)(2,1)S(1)}, bf16[3,4,4,16,128]{4,3,2,1,0:T(8,128)(2,1)S(1)}, u32[]{:S(2)}, u32[]{:S(2)}) collective-permute-start(bf16[3,4,4,16,128]{4,3,2,1,0:T(8,128)(2,1)S(1)} %pad_maximum_fusion.1.refs_9_), channel_id=1, source_target_pairs={{0,1},{1,0},{2,3},{3,2},{4,5},{5,4},{6,7},{7,6},{8,9},{9,8},{10,11... | collective-permute-start | bytes 589832 | tf_op jit(solution)/shard_map/ppermute | solution.py:196
  60.3 4.7 %collective-permute-start.19 = (bf16[3,4,4,16,128]{4,3,2,1,0:T(8,128)(2,1)S(1)}, bf16[3,4,4,16,128]{4,3,2,1,0:T(8,128)(2,1)S(1)}, u32[]{:S(2)}, u32[]{:S(2)}) collective-permute-start(bf16[3,4,4,16,128]{4,3,2,1,0:T(8,128)(2,1)S(1)} %collective-permute-done.17.refs_3_), channel_id=1, source_target_pairs={{0,1},{1,0},{2,3},{3,2},{4,5},{5,4},{6,7},{7,6},{8,9},{9,8},{10,11... | collective-permute-start | bytes 589832 | tf_op jit(solution)/shard_map/ppermute | solution.py:196
  60.4 4.6 %collective-permute-start.25 = (bf16[3,4,4,16,128]{4,3,2,1,0:T(8,128)(2,1)S(1)}, bf16[3,4,4,16,128]{4,3,2,1,0:T(8,128)(2,1)S(1)}, u32[]{:S(2)}, u32[]{:S(2)}) collective-permute-start(bf16[3,4,4,16,128]{4,3,2,1,0:T(8,128)(2,1)S(1)} %collective-permute-done.23.refs_11_), channel_id=1, source_target_pairs={{0,1},{1,0},{2,3},{3,2},{4,5},{5,4},{6,7},{7,6},{8,9},{9,8},{10,11... | collective-permute-start | bytes 589832 | tf_op jit(solution)/shard_map/ppermute | solution.py:196
  (22 other events, 100.0 us)

commit v3 on v0

--- a/solution.py
+++ b/solution.py
@@ -1,8 +1,11 @@
+import functools
 import math
 
 import jax
 import jax.numpy as jnp
 from jax import lax
+from jax.experimental import pallas as pl
+from jax.experimental.pallas import tpu as pltpu
 from jax.sharding import PartitionSpec as P
 
 OB = 4
@@ -170,9 +173,377 @@
     return (grad_features, grad_kernel, grad_gamma, grad_beta)
 
 
+HIGHEST = lax.Precision.HIGHEST
+F32 = jnp.float32
+BF16 = jnp.bfloat16
+EDGE = 8
+
+
+def exchanged(value, axes, target):
+    names = (axes,) if isinstance(axes, str) else axes
+    sizes = [lax.axis_size(name) for name in names]
+    places = [()]
+    for size in sizes:
+        places = [place + (i,) for place in places for i in range(size)]
+    pairs = []
+    for number, place in enumerate(places):
+        goal = target(*place)
+        if all(0 <= spot < size for spot, size in zip(goal, sizes)):
+            flat = 0
+            for spot, size in zip(goal, sizes):
+                flat = flat * size + spot
+            pairs.append((number, flat))
+    return lax.ppermute(value, names if len(names) > 1 else names[0], pairs)
+
+
+def flipped(value, axis):
+    return exchanged(value, axis, lambda i: (1 - i,))
+
+
+def occupied_rows(occupancy, extent, channels):
+    size_x, size_y, size_z = extent
+    level = lax.broadcasted_iota(jnp.int32, (size_z, channels), 0) // OB
+    layers = []
+    for bx in range(size_x // OB):
+        lines = []
+        for by in range(size_y // OB):
+            column = jnp.zeros((size_z, channels), F32)
+            for bz in range(size_z // OB):
+                value = occupancy[bx, by, bz].astype(F32)
+                column = jnp.where(level == bz, value, column)
+            lines.append(jnp.broadcast_to(column[None, None], (OB, OB, size_z, channels)))
+        layers.append(jnp.concatenate(lines, axis=1) if len(lines) > 1 else lines[0])
+    mask = jnp.concatenate(layers, axis=0) if len(layers) > 1 else layers[0]
+    return mask.reshape(size_x * size_y * size_z, channels)
+
+
+def latent_kernel(
+    far_features, far_scales, far_occupancy, far_gamma, far_beta,
+    latent, across_y, first_x, second_x, root, features, gamma,
+    scales, beta, occupancy, arrivals,
+):
+    loads = [
+        pltpu.make_async_copy(far, near, arrivals.at[n])
+        for n, (far, near) in enumerate(
+            (
+                (far_features, features),
+                (far_gamma, gamma),
+                (far_beta, beta),
+                (far_occupancy, occupancy),
+                (far_scales, scales),
+            )
+        )
+    ]
+    for load in loads:
+        load.start()
+    for load in loads:
+        load.wait()
+    size_x, _, _, channels = features.shape
+    feats = features[...].astype(F32).reshape(-1, channels)
+    energy = beta[...] + jnp.dot(
+        feats * feats, gamma[...], precision=HIGHEST, preferred_element_type=F32
+    )
+    inv_root = lax.rsqrt(energy)
+    root[...] = inv_root
+    occupied = occupied_rows(occupancy, features.shape[:3], channels)
+    rounded = (occupied * feats * inv_root).astype(BF16).reshape(features.shape)
+    latent[...] = rounded
+    scale = scales[...].astype(F32).reshape(-1, channels)
+    signed = jnp.where(occupied > 0.0, scale, -scale).astype(BF16).reshape(features.shape)
+    across_y[:size_x] = rounded
+    across_y[size_x:] = signed
+    upward = rounded[size_x - 2 :]
+    downward = rounded[:2]
+    odd = lax.rem(lax.axis_index("gx"), 2) == 1
+    first_x[:2] = jnp.where(odd, downward, upward)
+    second_x[:2] = jnp.where(odd, upward, downward)
+    first_x[2:] = signed[:2]
+    second_x[2:] = signed[:2]
+
+
+def below_and_above(first, second):
+    odd = lax.rem(lax.axis_index("gx"), 2) == 1
+    return jnp.where(odd, first, second), jnp.where(odd, second, first)
+
+
+def z_edges(wide, spot, across, size_z):
+    first_z = lax.axis_index("gz") == 0
+    across = across.astype(F32)
+    wide[spot + (pl.ds(0, EDGE),)] = jnp.where(first_z, 0.0, across[:, :, size_z - EDGE :])
+    wide[spot + (pl.ds(EDGE + size_z, EDGE),)] = jnp.where(first_z, across[:, :, :EDGE], 0.0)
+
+
+def mean_kernel(
+    own, side, first, corner, second, corner_2,
+    own_z, side_z, first_z, corner_z, second_z, corner_2z,
+    far_kernel, grad, rest, kernel, wide, shifted, level, held, arrival,
+):
+    load = pltpu.make_async_copy(far_kernel, kernel, arrival)
+    load.start()
+    size_x, _, size_z, channels = rest.shape
+    size_y = own.shape[1]
+    gy = lax.axis_index("gy")
+    near_y, far_y = gy * size_y, (1 - gy) * size_y
+    for at_y, block, block_z, one, two, one_z, two_z in (
+        (near_y, own, own_z, first, second, first_z, second_z),
+        (far_y, side, side_z, corner, corner_2, corner_z, corner_2z),
+    ):
+        spot_y = pl.ds(2 + at_y, size_y)
+        below, above = below_and_above(one[...], two[...])
+        below_z, above_z = below_and_above(one_z[...], two_z[...])
+        for at_x, main, across in (
+            (2, block[:size_x], block_z[:size_x]),
+            (0, below[:2], below_z[:2]),
+            (2 + size_x, above[:2], above_z[:2]),
+        ):
+            spot = (pl.ds(at_x, main.shape[0]), spot_y)
+            wide[spot + (pl.ds(EDGE, size_z),)] = main.astype(F32)
+            z_edges(wide, spot, across, size_z)
+        level[:size_x, pl.ds(at_y, size_y)] = block[size_x:].astype(F32)
+        level[size_x:, pl.ds(at_y, size_y)] = above[2:].astype(F32)
+    blank = jnp.zeros((size_x + 4, 2) + wide.shape[2:], F32)
+    wide[:, :2] = blank
+    wide[:, 2 + 2 * size_y :] = blank
+    for number in range(5):
+        start = EDGE + number - 2
+        shifted[:, :, :, number * channels : (number + 1) * channels] = wide[
+            :, :, start : start + size_z, :
+        ].astype(BF16)
+    box = (size_x + 2, 2 * size_y, size_z, channels)
+    load.wait()
+    total = jnp.zeros((box[0] * box[1] * box[2], channels), F32)
+    for along_x, along_y, _, count, first_tap in tap_groups():
+        patch = shifted[
+            2 + along_x : 2 + along_x + box[0],
+            2 + along_y : 2 + along_y + box[1],
+            :,
+            : count * channels,
+        ].reshape(-1, count * channels)
+        weights = kernel[first_tap : first_tap + count].reshape(count * channels, channels)
+        total = total + jnp.dot(patch, weights, preferred_element_type=F32)
+    signed = level[...]
+    latent = wide[2:, 2 : 2 + box[1], EDGE : EDGE + size_z]
+    difference = (total.reshape(box) - latent) * (1.0 / (signed * signed))
+    grad[...] = jnp.where(signed > 0.0, difference, 0.0).astype(BF16)
+    held[...] = -difference[:size_x]
+    rest[...] = held[:, pl.ds(near_y, size_y)]
+
+
+def share_kernel(spanned, voxels, *refs):
+    (own, side, first, corner, second, corner_2,
+     own_z, side_z, first_z, corner_z, second_z, corner_2z, grad, grad_z) = refs[:14]
+    mine, later, message, wide, flat, turned, product = refs[14:]
+    rows = mine.shape[0]
+    size_x, all_y, all_z, channels = flat.shape
+    size_y, size_z = all_y // 2, all_z // 2
+    gx, gy, gz = lax.axis_index("gx"), lax.axis_index("gy"), lax.axis_index("gz")
+    blank = jnp.zeros((size_x + 2, 2, wide.shape[2], channels), F32)
+    wide[:, :2] = blank
+    wide[:, 2 + all_y :] = blank
+    for start in (0, EDGE + all_z):
+        wide[:, 2 : 2 + all_y, start : start + EDGE] = jnp.zeros((size_x + 2, all_y, EDGE, channels), F32)
+    for here_y, here_z, block, one, two in (
+        (True, True, own, first, second),
+        (False, True, side, corner, corner_2),
+        (True, False, own_z, first_z, second_z),
+        (False, False, side_z, corner_z, corner_2z),
+    ):
+        at_y = (gy if here_y else 1 - gy) * size_y
+        at_z = (gz if here_z else 1 - gz) * size_z
+        spot_y, spot_z = pl.ds(2 + at_y, size_y), pl.ds(pl.multiple_of(EDGE + at_z, EDGE), size_z)
+        wide[2:, spot_y, spot_z] = block[:size_x].astype(F32)
+        wide[:2, spot_y, spot_z] = below_and_above(one[:2], two[:2])[0].astype(F32)
+    flat[:, :, pl.ds(pl.multiple_of(gz * size_z, size_z), size_z)] = grad[:size_x]
+    flat[:, :, pl.ds(pl.multiple_of((1 - gz) * size_z, size_z), size_z)] = grad_z[:size_x]
+    turned[...] = flat[...].reshape(-1, channels).T
+    for other in range(4):
+        first_row = (((gx ^ other) * 2 + gy) * 2 + gz) * rows
+        first_tap = jnp.minimum(first_row // channels, 62 - spanned)
+        for level in range(5):
+            number = lax.rem(level + 5 - lax.rem(first_tap, 5), 5)
+            group = (first_tap + number) // 5
+            along_x, along_y = group // 5, lax.rem(group, 5)
+            start = EDGE + level - 2
+            patch = wide[pl.ds(along_x, size_x), pl.ds(along_y, all_y), start : start + all_z]
+            result = jnp.dot(
+                turned[...], patch.astype(BF16).reshape(-1, channels), preferred_element_type=F32
+            )
+            product[other, pl.ds(pl.multiple_of(number * channels, channels), channels)] = result.T
+        offset = pl.multiple_of(first_row - first_tap * channels, 16)
+        share = product[other, pl.ds(offset, rows)] * (1.0 / voxels)
+        if other == 0:
+            mine[...] = share
+        elif other == 2:
+            later[...] = share
+        else:
+            half = (other // 2) * rows
+            message[half : half + rows] = share.astype(message.dtype)
+
+
+def feature_kernel(
+    grad, grad_z, kernel, rest, root, features, gamma, block,
+    grad_features, sums, wide, shifted,
+):
+    size_x, size_y, size_z, channels = features.shape
+    voxels = size_x * size_y * size_z
+    gy = lax.axis_index("gy")
+    spot = (pl.ds(0, size_x + 2), pl.ds(2, 2 * size_y))
+    wide[spot + (pl.ds(EDGE, size_z),)] = grad[...].astype(F32)
+    z_edges(wide, spot, grad_z[...], size_z)
+    blank = jnp.zeros((size_x + 2, 2) + wide.shape[2:], F32)
+    wide[:, :2] = blank
+    wide[:, 2 + 2 * size_y :] = blank
+    for number in range(5):
+        start = EDGE - (number - 2)
+        shifted[:, :, :, number * channels : (number + 1) * channels] = wide[
+            :, pl.ds(gy * size_y, size_y + 4), start : start + size_z, :
+        ].astype(BF16)
+    total = jnp.zeros((voxels, channels), F32)
+    for along_x, along_y, _, count, first_tap in tap_groups():
+        patch = shifted[
+            -along_x : -along_x + size_x,
+            2 - along_y : 2 - along_y + size_y,
+            :,
+            : count * channels,
+        ].reshape(-1, count * channels)
+        weights = jnp.concatenate([kernel[first_tap + k] for k in range(count)], axis=1)
+        total = total + lax.dot_general(
+            patch, weights, (((1,), (1,)), ((), ())), preferred_element_type=F32
+        )
+    occupied = jnp.where(block[size_x:].astype(F32).reshape(voxels, channels) > 0.0, 1.0, 0.0)
+    latent_grad = occupied * (total + rest[...].reshape(voxels, channels))
+    inv_root = root[...]
+    feats = features[...].astype(F32).reshape(voxels, channels)
+    weighted = latent_grad * feats * inv_root * inv_root * inv_root
+    coupled = lax.dot_general(
+        weighted, gamma[...], (((1,), (1,)), ((), ())), precision=HIGHEST, preferred_element_type=F32
+    )
+    grad_features[...] = (latent_grad * inv_root - feats * coupled).astype(BF16).reshape(features.shape)
+    factor = 0.5 / math.sqrt(voxels)
+    sums[:channels] = -factor * jnp.dot(
+        (feats * feats).T, weighted, precision=HIGHEST, preferred_element_type=F32
+    )
+    ones = jnp.sum(weighted, axis=0, keepdims=True)
+    sums[channels:] = -factor * jnp.broadcast_to(ones, (8, channels))
+
+
+def call(body, outs, scratch, args, far=()):
+    spaces = [pltpu.HBM if n in far else pltpu.VMEM for n in range(len(args))]
+    args = [pltpu.with_memory_space_constraint(a, space) for a, space in zip(args, spaces)]
+    return pl.pallas_call(
+        body,
+        out_shape=outs,
+        in_specs=[pl.BlockSpec(memory_space=space) for space in spaces],
+        out_specs=[pl.BlockSpec(memory_space=pltpu.VMEM)] * len(outs),
+        scratch_shapes=scratch,
+        compiler_params=pltpu.CompilerParams(vmem_limit_bytes=24 << 20),
+    )(*args)
+
+
+def fast_local(features, scales, occupancy, kernel, gamma, beta):
+    shape = features.shape
+    size_x, size_y, size_z, channels = shape
+    voxels = size_x * size_y * size_z
+    rest_of = shape[1:]
+    latent, across_y, first_x, second_x, root, kept_features, kept_gamma = call(
+        latent_kernel,
+        [
+            pltpu.VMEM(shape, BF16),
+            pltpu.VMEM((2 * size_x,) + rest_of, BF16),
+            pltpu.VMEM((4,) + rest_of, BF16),
+            pltpu.VMEM((4,) + rest_of, BF16),
+            pltpu.VMEM((voxels, channels), F32),
+            pltpu.VMEM(shape, BF16),
+            pltpu.VMEM(gamma.shape, F32),
+        ],
+        [
+            pltpu.VMEM(shape, BF16),
+            pltpu.VMEM((1, channels), F32),
+            pltpu.SMEM(occupancy.shape, jnp.int32),
+            pltpu.SemaphoreType.DMA((5,)),
+        ],
+        (features, scales, occupancy, gamma, beta.reshape(1, channels)),
+        (0, 1, 2, 3, 4),
+    )
+    middle = lambda x: (3 - x if x in (1, 2) else -1,)
+    side = flipped(across_y, "gy")
+    first = exchanged(first_x, "gx", lambda x: (x ^ 1,))
+    second = exchanged(second_x, "gx", middle)
+    upward, downward = side[size_x - 2 : size_x], side[:2]
+    odd = lax.rem(lax.axis_index("gx"), 2) == 1
+    levels = side[size_x : size_x + 2]
+    corner = exchanged(
+        jnp.concatenate([jnp.where(odd, downward, upward), levels]), "gx", lambda x: (x ^ 1,)
+    )
+    corner_2 = exchanged(
+        jnp.concatenate([jnp.where(odd, upward, downward), levels]), "gx", middle
+    )
+    sent = (side, first, corner, second, corner_2)
+    around = (across_y,) + sent + tuple(flipped(part, "gz") for part in (latent,) + sent)
+    wide_y = 2 * size_y + 4
+    wide_z = size_z + 2 * EDGE
+    grad, rest, kept_kernel = call(
+        mean_kernel,
+        [
+            pltpu.VMEM((size_x + 2, 2 * size_y, size_z, channels), BF16),
+            pltpu.VMEM(shape, F32),
+            pltpu.VMEM(kernel.shape, BF16),
+        ],
+        [
+            pltpu.VMEM((size_x + 4, wide_y, wide_z, channels), F32),
+            pltpu.VMEM((size_x + 4, wide_y, size_z, 5 * channels), BF16),
+            pltpu.VMEM((size_x + 2, 2 * size_y, size_z, channels), F32),
+            pltpu.VMEM((size_x, 2 * size_y, size_z, channels), F32),
+            pltpu.SemaphoreType.DMA,
+        ],
+        around + (kernel,),
+        (12,),
+    )
+    grad_z = flipped(grad, "gz")
+    rows = 62 * channels // 16
+    spanned = 5
+    mine, later, message = call(
+        functools.partial(share_kernel, spanned, voxels),
+        [pltpu.VMEM((rows, channels), F32)] * 2 + [pltpu.VMEM((2 * rows, channels), BF16)],
+        [
+            pltpu.VMEM((size_x + 2, wide_y, 2 * size_z + 2 * EDGE, channels), F32),
+            pltpu.VMEM((size_x, 2 * size_y, 2 * size_z, channels), BF16),
+            pltpu.VMEM((channels, 4 * voxels), BF16),
+            pltpu.VMEM((4, spanned * channels, channels), F32),
+        ],
+        around + (grad, grad_z),
+    )
+    halves = exchanged(message, "gx", lambda x: (x ^ 1,))
+    grad_features, sums = call(
+        feature_kernel,
+        [jax.ShapeDtypeStruct(shape, BF16), pltpu.VMEM((channels + 8, channels), F32)],
+        [
+            pltpu.VMEM((size_x + 2, wide_y, wide_z, channels), F32),
+            pltpu.VMEM((size_x + 2, size_y + 4, size_z, 5 * channels), BF16),
+        ],
+        (grad, grad_z, kept_kernel, rest, root, kept_features, kept_gamma, across_y),
+    )
+    sums = sums + flipped(sums, "gz")
+    quarter = exchanged((later + halves[rows:].astype(F32)).astype(BF16), "gx", lambda x: (x ^ 2,))
+    sums = sums + flipped(sums, "gy")
+    sums = sums + exchanged(sums, "gx", lambda x: (x ^ 1,))
+    sums = sums + exchanged(sums, "gx", lambda x: (x ^ 2,))
+    share = mine + halves[:rows].astype(F32) + quarter.astype(F32)
+    return grad_features, share.reshape(-1), sums[:channels], sums[channels]
+
+
+def chosen(features, scales, occupancy, kernel, gamma, beta):
+    sizes = tuple(lax.axis_size(axis) for axis in ("gx", "gy", "gz"))
+    size_x, size_y, size_z, channels = features.shape
+    small = size_x >= 2 and size_y >= 2 and size_z % 16 == 0 and size_x * size_y * size_z <= 1024
+    if sizes == (4, 2, 2) and small and channels == 128:
+        return fast_local(features, scales, occupancy, kernel, gamma, beta)
+    return local(features, scales, occupancy, kernel, gamma, beta)
+
+
 def solution(mesh):
     return jax.shard_map(
-        local,
+        chosen,
         mesh=mesh,
         in_specs=(
             P(("groups", "gx"), "gy", "gz", None),

time: 196 us -> 51.1 us (0.26)
  waiting for transfers between devices: 82.8 us -> 19 us
  blocking collectives: 34.5 us -> 0 us
  local copies, waits for them, and re-layouts: 18.6 us -> 1.15 us
  between operations: 15.6 us -> 0.74 us
  matrix products: 12.9 us -> 0 us
  Pallas kernels: 0 us -> 10.5 us
  starting transfers between devices: 24.6 us -> 18.7 us
  other arithmetic: 6.33 us -> 0.83 us
    unnamed x2 -> x0, waiting for transfers between devices: 75.5 us -> none
    psum x1 -> x0, blocking collectives: 34.5 us -> none  [local(): lax.psum((gamma_local, beta_local), ('gx', 'gy', 'gz'))]
    dot_general x42 -> x0, matrix products: 12.9 us -> none  [the longest x13 3.77 us: kernel_terms(): lax.dot_general(patch, mean_grad, (((0,), (0,)), ((), ())), preferred_ele...]
    ppermute x10 -> x18, waiting for transfers between devices: 7.27 us -> 19 us  [exchanged(): return lax.ppermute(value, names if len(names) > 1 else names[0], pairs)]
    pallas_call x0 -> x4, Pallas kernels: none -> 10.5 us  [call(): pl.pallas_call(body, out_shape=outs, in_specs=[pl.BlockSpec(memory_space=...]
    transpose x15 -> x0, local copies, waits for them, and re-layouts: 9.94 us -> none  [context_transposed(): jnp.transpose(kernel[first_tap:first_tap + count], (0, 2, 1))]
    ppermute x10 -> x18, starting transfers between devices: 24.6 us -> 18.7 us  [exchanged(): return lax.ppermute(value, names if len(names) > 1 else names[0], pairs)]
    unnamed x59 -> x0, local copies, waits for them, and re-layouts: 5.71 us -> none
  transfers between devices with their start and end apart: 11 -> 18, of which waited for: 4 -> 9; matrix products, arithmetic and copies ran while one was open for 11% -> 2% of each run, Pallas kernels for 0% -> 5%
where the time goes in v3:
time: 51.1 us; the launch traced here: 50.9 us
  waiting for transfers between devices  19 us (37%)
  starting transfers between devices  18.7 us (37%)
  Pallas kernels  10.5 us (21%)
  local copies, waits for them, and re-layouts  1.15 us (2%)
  other arithmetic  0.83 us (2%)
  between operations  0.74 us (1%)
    ppermute x18, waiting for transfers between devices, exchanged(): return lax.ppermute(value, names if len(names) > 1 else names[0], pairs)  19 us
    ppermute x18, starting transfers between devices, exchanged(): return lax.ppermute(value, names if len(names) > 1 else names[0], pairs)  18.7 us
    pallas_call x4, Pallas kernels, call(): pl.pallas_call(body, out_shape=outs, in_specs=[pl.BlockSpec(memory_space=...  10.5 us
  transfers between devices with their start and end apart: 18, of which 9 were waited for; matrix products, arithmetic and copies ran while one was open for 2% of the time, Pallas kernels for 5%

profile of v3, /device:TPU:0, one launch (start us, length us, event | category | flops | bytes accessed | tf_op | source)
XLA Modules:
  0.0 50.9 jit_solution(10628203658384097436)
XLA Ops:
  0.6 1.3 %shard_map.93 = (bf16[4,4,16,128]{3,2,1,0:T(8,128)(2,1)S(1)}, bf16[8,4,16,128]{3,2,1,0:T(8,128)(2,1)S(1)}, bf16[4,4,16,128]{3,2,1,0:T(8,128)(2,1)S(1)}, bf16[4,4...) custom-call(bf16[4,4,16,128]{3,2,1,0:T(8,128)(2,1)} %far_features.1,, ...), custom_call_target="tpu_custom_call" | custom-call | tf_op jit(solution)/shard_map/pallas_call | solution.py:433
  1.9 3.0 %collective-permute-start = (bf16[8,4,16,128]{3,2,1,0:T(8,128)(2,1)S(1)}, bf16[8,4,16,128]{3,2,1,0:T(8,128)(2,1)S(1)}, u32[]{:S(2)}, u32[]{:S(2)}) collective-permute-start(bf16[8,4,16,128]{3,2,1,0:T(8,128)(2,1)S(1)} %get-tuple-element.19.own.block.refs_0_), channel_id=1, source_target_pairs={{0,2},{2,0},{1,3},{3,1},{4,6},{6,4},{5,7},{7,5},{8,10},{10,8},{9,1... | collective-permute-start | bytes 393224 | tf_op jit(solution)/shard_map/ppermute | solution.py:196
  4.9 1.6 %collective-permute-start.1 = (bf16[4,4,16,128]{3,2,1,0:T(8,128)(2,1)S(1)}, bf16[4,4,16,128]{3,2,1,0:T(8,128)(2,1)S(1)}, u32[]{:S(2)}, u32[]{:S(2)}) collective-permute-start(bf16[4,4,16,128]{3,2,1,0:T(8,128)(2,1)S(1)} %get-tuple-element.20), channel_id=1, source_target_pairs={{0,4},{4,0},{8,12},{12,8},{1,5},{5,1},{9,13},{13,9},{2,6},{6,2},{1... | collective-permute-start | bytes 196616 | tf_op jit(solution)/shard_map/ppermute | solution.py:196
  6.5 0.7 %collective-permute-start.3 = (bf16[4,4,16,128]{3,2,1,0:T(8,128)(2,1)S(1)}, bf16[4,4,16,128]{3,2,1,0:T(8,128)(2,1)S(1)}, u32[]{:S(2)}, u32[]{:S(2)}) collective-permute-start(bf16[4,4,16,128]{3,2,1,0:T(8,128)(2,1)S(1)} %get-tuple-element.21), channel_id=1, source_target_pairs={{4,8},{8,4},{5,9},{9,5},{6,10},{10,6},{7,11},{11,7},{20,24},{24,20... | collective-permute-start | bytes 196616 | tf_op jit(solution)/shard_map/ppermute | solution.py:196
  7.2 0.1 collective-permute-start.5
  7.3 1.2 %collective-permute-done.side.refs_1_ = bf16[8,4,16,128]{3,2,1,0:T(8,128)(2,1)S(1)} collective-permute-done((bf16[8,4,16,128]{3,2,1,0:T(8,128)(2,1)S(1)}, bf16[8,4,16,128]{3,2,1,0:T(8,128)(2,1)S(1)}, u32[]{:S(2)}, u32[]{:S(2)}) %collective-permute-start) | collective-permute-done | bytes 131104 | tf_op jit(solution)/shard_map/ppermute | solution.py:196
  8.5 0.7 %collective-permute-start.4 = (bf16[4,4,16,128]{3,2,1,0:T(8,128)(2,1)S(1)}, bf16[4,4,16,128]{3,2,1,0:T(8,128)(2,1)S(1)}, u32[]{:S(2)}, u32[]{:S(2)}) collective-permute-start(bf16[4,4,16,128]{3,2,1,0:T(8,128)(2,1)S(1)} %get-tuple-element.37), channel_id=1, source_target_pairs={{4,8},{8,4},{5,9},{9,5},{6,10},{10,6},{7,11},{11,7},{20,24},{24,20... | collective-permute-start | bytes 196616 | tf_op jit(solution)/shard_map/ppermute | solution.py:196
  9.1 4.7 %collective-permute-start.2 = (bf16[4,4,16,128]{3,2,1,0:T(8,128)(2,1)S(1)}, bf16[4,4,16,128]{3,2,1,0:T(8,128)(2,1)S(1)}, u32[]{:S(2)}, u32[]{:S(2)}) collective-permute-start(bf16[4,4,16,128]{3,2,1,0:T(8,128)(2,1)S(1)} %get-tuple-element.38), channel_id=1, source_target_pairs={{0,4},{4,0},{8,12},{12,8},{1,5},{5,1},{9,13},{13,9},{2,6},{6,2},{1... | collective-permute-start | bytes 196616 | tf_op jit(solution)/shard_map/ppermute | solution.py:196
  13.9 0.5 collective-permute-start.7
  14.4 0.1 collective-permute-start.9
  14.4 0.4 collective-permute-start.10
  14.9 1.5 %collective-permute-done.2.corner.refs_3_ = bf16[4,4,16,128]{3,2,1,0:T(8,128)(2,1)S(1)} collective-permute-done((bf16[4,4,16,128]{3,2,1,0:T(8,128)(2,1)S(1)}, bf16[4,4,16,128]{3,2,1,0:T(8,128)(2,1)S(1)}, u32[]{:S(2)}, u32[]{:S(2)}) %collective-permute-start.2) | collective-permute-done | bytes 65568 | tf_op jit(solution)/shard_map/ppermute | solution.py:196
  16.5 1.2 %collective-permute-done.8.corner_z.refs_9_ = bf16[4,4,16,128]{3,2,1,0:T(8,128)(2,1)S(1)} collective-permute-done((bf16[4,4,16,128]{3,2,1,0:T(8,128)(2,1)S(1)}, bf16[4,4,16,128]{3,2,1,0:T(8,128)(2,1)S(1)}, u32[]{:S(2)}, u32[]{:S(2)}) %collective-permute-start.8) | collective-permute-done | bytes 65568 | tf_op jit(solution)/shard_map/ppermute | solution.py:196
  17.7 4.9 %shard_map.94 = (bf16[6,8,16,128]{3,2,1,0:T(8,128)(2,1)S(1)}, f32[4,4,16,128]{3,2,1,0:T(8,128)S(1)}, bf16[62,128,128]{2,1,0:T(8,128)(2,1)S(1)}) custom-call(bf16[8,4,16,128]{3,2,1,0:T(8,128)(2,1)S(1)} %get-tuple-element.19.own.block.refs_0_, bf16[8,4,16,128]{3,2,1,0:T(8,128)(2,1)S(1)} %collective-permute-done.side.refs_1_, ...), custom_call_target="tpu_custom_call" | custom-call | tf_op jit(solution)/shard_map/pallas_call | solution.py:433
  22.6 0.2 collective-permute-start.11
  22.9 1.3 %collective-permute-done.11.grad_z.refs_13_ = bf16[6,8,16,128]{3,2,1,0:T(8,128)(2,1)S(1)} collective-permute-done((bf16[6,8,16,128]{3,2,1,0:T(8,128)(2,1)S(1)}, bf16[6,8,16,128]{3,2,1,0:T(8,128)(2,1)S(1)}, u32[]{:S(2)}, u32[]{:S(2)}) %collective-permute-start.11) | collective-permute-done | bytes 196640 | tf_op jit(solution)/shard_map/ppermute | solution.py:196
  24.2 1.9 %shard_map.96 = (f32[496,128]{1,0:T(8,128)S(1)}, f32[496,128]{1,0:T(8,128)S(1)}, bf16[992,128]{1,0:T(8,128)(2,1)S(1)}) custom-call(bf16[8,4,16,128]{3,2,1,0:T(8,128)(2,1)S(1)} %get-tuple-element.19.own.block.refs_0_, bf16[8,4,16,128]{3,2,1,0:T(8,128)(2,1)S(1)} %collective-permute-done.side.refs_1_, ...), custom_call_target="tpu_custom_call" | custom-call | tf_op jit(solution)/shard_map/pallas_call | solution.py:433
  26.0 1.8 %collective-permute-start.12 = (bf16[992,128]{1,0:T(8,128)(2,1)S(1)}, bf16[992,128]{1,0:T(8,128)(2,1)S(1)}, u32[]{:S(2)}, u32[]{:S(2)}) collective-permute-start(bf16[992,128]{1,0:T(8,128)(2,1)S(1)} %get-tuple-element.31), channel_id=1, source_target_pairs={{0,4},{4,0},{8,12},{12,8},{1,5},{5,1},{9,13},{13,9},{2,6},{6,2},{1... | collective-permute-start | bytes 761864 | tf_op jit(solution)/shard_map/ppermute | solution.py:196
  27.9 2.4 %shard_map.95 = (bf16[4,4,16,128]{3,2,1,0:T(8,128)(2,1)}, f32[136,128]{1,0:T(8,128)S(1)}) custom-call(bf16[6,8,16,128]{3,2,1,0:T(8,128)(2,1)S(1)} %get-tuple-element.23.grad.refs_12_, bf16[6,8,16,128]{3,2,1,0:T(8,128)(2,1)S(1)} %collective-permute-done.11.grad_z.refs_13_, bf16[62,128,128]{2,1,0:T(8,128)(2,1)S(1)} %get-tuple-element.24.kernel, ...), custom_call_target="tpu_custom_call" | custom-call | tf_op jit(solution)/shard_map/pallas_call | solution.py:433
  30.2 0.1 collective-permute-start.14
  30.3 1.2 %collective-permute-done.14 = f32[136,128]{1,0:T(8,128)S(1)} collective-permute-done((f32[136,128]{1,0:T(8,128)S(1)}, f32[136,128]{1,0:T(8,128)S(1)}, u32[]{:S(2)}, u32[]{:S(2)}) %collective-permute-start.14) | collective-permute-done | bytes 69664 | tf_op jit(solution)/shard_map/ppermute | solution.py:196
  31.5 1.5 %collective-permute-start.15 = (f32[136,128]{1,0:T(8,128)S(1)}, f32[136,128]{1,0:T(8,128)S(1)}, u32[]{:S(2)}, u32[]{:S(2)}) collective-permute-start(f32[136,128]{1,0:T(8,128)S(1)} %add.24), channel_id=1, source_target_pairs={{0,2},{2,0},{1,3},{3,1},{4,6},{6,4},{5,7},{7,5},{8,10},{10,8},{9,1... | collective-permute-start | bytes 208904 | tf_op jit(solution)/shard_map/ppermute | solution.py:196
  33.0 2.9 %collective-permute-done.15 = f32[136,128]{1,0:T(8,128)S(1)} collective-permute-done((f32[136,128]{1,0:T(8,128)S(1)}, f32[136,128]{1,0:T(8,128)S(1)}, u32[]{:S(2)}, u32[]{:S(2)}) %collective-permute-start.15) | collective-permute-done | bytes 69664 | tf_op jit(solution)/shard_map/ppermute | solution.py:196
  35.9 0.3 collective-permute-start.16
  36.2 4.1 %collective-permute-done.16 = f32[136,128]{1,0:T(8,128)S(1)} collective-permute-done((f32[136,128]{1,0:T(8,128)S(1)}, f32[136,128]{1,0:T(8,128)S(1)}, u32[]{:S(2)}, u32[]{:S(2)}) %collective-permute-start.16) | collective-permute-done | bytes 69664 | tf_op jit(solution)/shard_map/ppermute | solution.py:196
  40.3 1.5 %collective-permute-start.17 = (f32[136,128]{1,0:T(8,128)S(1)}, f32[136,128]{1,0:T(8,128)S(1)}, u32[]{:S(2)}, u32[]{:S(2)}) collective-permute-start(f32[136,128]{1,0:T(8,128)S(1)} %add.26), channel_id=1, source_target_pairs={{0,8},{4,12},{8,0},{12,4},{1,9},{5,13},{9,1},{13,5},{2,10},{6,14},... | collective-permute-start | bytes 208904 | tf_op jit(solution)/shard_map/ppermute | solution.py:196
  41.8 1.6 %collective-permute-start.13 = (bf16[496,128]{1,0:T(8,128)(2,1)S(1)}, bf16[496,128]{1,0:T(8,128)(2,1)S(1)}, u32[]{:S(2)}, u32[]{:S(2)}) collective-permute-start(bf16[496,128]{1,0:T(8,128)(2,1)S(1)} %add_convert_fusion), channel_id=1, source_target_pairs={{0,8},{4,12},{8,0},{12,4},{1,9},{5,13},{9,1},{13,5},{2,10},{6,14},... | collective-permute-start | bytes 380936 | tf_op jit(solution)/shard_map/ppermute | solution.py:196
  43.4 4.1 %collective-permute-done.17 = f32[136,128]{1,0:T(8,128)S(1)} collective-permute-done((f32[136,128]{1,0:T(8,128)S(1)}, f32[136,128]{1,0:T(8,128)S(1)}, u32[]{:S(2)}, u32[]{:S(2)}) %collective-permute-start.17) | collective-permute-done | bytes 69664 | tf_op jit(solution)/shard_map/ppermute | solution.py:196
  47.5 0.6 %slice.33 = f32[128,128]{1,0:T(8,128)} slice(f32[136,128]{1,0:T(8,128)S(1)} %add.27), slice={[0:128], [0:128]} | slice | bytes 131072 | tf_op jit(solution)/shard_map/slice | solution.py:532
  48.1 0.5 %slice_bitcast_fusion = f32[128]{0:T(128)} fusion(f32[136,128]{1,0:T(8,128)S(1)} %add.27), kind=kLoop, calls=%fused_computation.6 | loop fusion | bytes 1024 | tf_op jit(solution)/shard_map/squeeze | solution.py:532
  48.6 1.6 %collective-permute-done.13 = bf16[496,128]{1,0:T(8,128)(2,1)S(1)} collective-permute-done((bf16[496,128]{1,0:T(8,128)(2,1)S(1)}, bf16[496,128]{1,0:T(8,128)(2,1)S(1)}, u32[]{:S(2)}, u32[]{:S(2)}) %collective-permute-start.13) | collective-permute-done | bytes 127008 | tf_op jit(solution)/shard_map/ppermute | solution.py:196
  50.2 0.7 %add_bitcast_fusion = f32[63488]{0:T(1024)} fusion(bf16[496,128]{1,0:T(8,128)(2,1)S(1)} %collective-permute-done.13, f32[496,128]{1,0:T(8,128)S(1)} %get-tuple-element.30, bf16[992,128]{1,0:T(8,128)(2,1)S(1)} %collective-permute-done.12), kind=kLoop, calls=%fused_computation | loop fusion | flops 253952 | bytes 761856 | tf_op jit(solution)/shard_map/reshape | solution.py:532
  (18 shorter events, 0.2 us)
Async XLA Ops:
  1.9 6.5 %collective-permute-start = (bf16[8,4,16,128]{3,2,1,0:T(8,128)(2,1)S(1)}, bf16[8,4,16,128]{3,2,1,0:T(8,128)(2,1)S(1)}, u32[]{:S(2)}, u32[]{:S(2)}) collective-permute-start(bf16[8,4,16,128]{3,2,1,0:T(8,128)(2,1)S(1)} %get-tuple-element.19.own.block.refs_0_), channel_id=1, source_target_pairs={{0,2},{2,0},{1,3},{3,1},{4,6},{6,4},{5,7},{7,5},{8,10},{10,8},{9,1... | collective-permute-start | bytes 393224 | tf_op jit(solution)/shard_map/ppermute | solution.py:196
  4.9 8.9 %collective-permute-start.1 = (bf16[4,4,16,128]{3,2,1,0:T(8,128)(2,1)S(1)}, bf16[4,4,16,128]{3,2,1,0:T(8,128)(2,1)S(1)}, u32[]{:S(2)}, u32[]{:S(2)}) collective-permute-start(bf16[4,4,16,128]{3,2,1,0:T(8,128)(2,1)S(1)} %get-tuple-element.20), channel_id=1, source_target_pairs={{0,4},{4,0},{8,12},{12,8},{1,5},{5,1},{9,13},{13,9},{2,6},{6,2},{1... | collective-permute-start | bytes 196616 | tf_op jit(solution)/shard_map/ppermute | solution.py:196
  6.5 7.4 %collective-permute-start.3 = (bf16[4,4,16,128]{3,2,1,0:T(8,128)(2,1)S(1)}, bf16[4,4,16,128]{3,2,1,0:T(8,128)(2,1)S(1)}, u32[]{:S(2)}, u32[]{:S(2)}) collective-permute-start(bf16[4,4,16,128]{3,2,1,0:T(8,128)(2,1)S(1)} %get-tuple-element.21), channel_id=1, source_target_pairs={{4,8},{8,4},{5,9},{9,5},{6,10},{10,6},{7,11},{11,7},{20,24},{24,20... | collective-permute-start | bytes 196616 | tf_op jit(solution)/shard_map/ppermute | solution.py:196
  7.2 7.2 %collective-permute-start.5 = (bf16[4,4,16,128]{3,2,1,0:T(8,128)(2,1)S(1)}, bf16[4,4,16,128]{3,2,1,0:T(8,128)(2,1)S(1)}, u32[]{:S(2)}, u32[]{:S(2)}) collective-permute-start(bf16[4,4,16,128]{3,2,1,0:T(8,128)(2,1)S(1)} %get-tuple-element.22), channel_id=1, source_target_pairs={{0,1},{1,0},{2,3},{3,2},{4,5},{5,4},{6,7},{7,6},{8,9},{9,8},{10,11... | collective-permute-start | bytes 196616 | tf_op jit(solution)/shard_map/ppermute | solution.py:196
  8.5 6.0 %collective-permute-start.4 = (bf16[4,4,16,128]{3,2,1,0:T(8,128)(2,1)S(1)}, bf16[4,4,16,128]{3,2,1,0:T(8,128)(2,1)S(1)}, u32[]{:S(2)}, u32[]{:S(2)}) collective-permute-start(bf16[4,4,16,128]{3,2,1,0:T(8,128)(2,1)S(1)} %get-tuple-element.37), channel_id=1, source_target_pairs={{4,8},{8,4},{5,9},{9,5},{6,10},{10,6},{7,11},{11,7},{20,24},{24,20... | collective-permute-start | bytes 196616 | tf_op jit(solution)/shard_map/ppermute | solution.py:196
  9.1 7.3 %collective-permute-start.2 = (bf16[4,4,16,128]{3,2,1,0:T(8,128)(2,1)S(1)}, bf16[4,4,16,128]{3,2,1,0:T(8,128)(2,1)S(1)}, u32[]{:S(2)}, u32[]{:S(2)}) collective-permute-start(bf16[4,4,16,128]{3,2,1,0:T(8,128)(2,1)S(1)} %get-tuple-element.38), channel_id=1, source_target_pairs={{0,4},{4,0},{8,12},{12,8},{1,5},{5,1},{9,13},{13,9},{2,6},{6,2},{1... | collective-permute-start | bytes 196616 | tf_op jit(solution)/shard_map/ppermute | solution.py:196
  13.8 3.8 %collective-permute-start.6 = (bf16[8,4,16,128]{3,2,1,0:T(8,128)(2,1)S(1)}, bf16[8,4,16,128]{3,2,1,0:T(8,128)(2,1)S(1)}, u32[]{:S(2)}, u32[]{:S(2)}) collective-permute-start(bf16[8,4,16,128]{3,2,1,0:T(8,128)(2,1)S(1)} %collective-permute-done.side.refs_1_), channel_id=1, source_target_pairs={{0,1},{1,0},{2,3},{3,2},{4,5},{5,4},{6,7},{7,6},{8,9},{9,8},{10,11... | collective-permute-start | bytes 393224 | tf_op jit(solution)/shard_map/ppermute | solution.py:196
  13.9 2.5 %collective-permute-start.7 = (bf16[4,4,16,128]{3,2,1,0:T(8,128)(2,1)S(1)}, bf16[4,4,16,128]{3,2,1,0:T(8,128)(2,1)S(1)}, u32[]{:S(2)}, u32[]{:S(2)}) collective-permute-start(bf16[4,4,16,128]{3,2,1,0:T(8,128)(2,1)S(1)} %collective-permute-done.1.first.refs_2_), channel_id=1, source_target_pairs={{0,1},{1,0},{2,3},{3,2},{4,5},{5,4},{6,7},{7,6},{8,9},{9,8},{10,11... | collective-permute-start | bytes 196616 | tf_op jit(solution)/shard_map/ppermute | solution.py:196
  14.4 2.1 %collective-permute-start.9 = (bf16[4,4,16,128]{3,2,1,0:T(8,128)(2,1)S(1)}, bf16[4,4,16,128]{3,2,1,0:T(8,128)(2,1)S(1)}, u32[]{:S(2)}, u32[]{:S(2)}) collective-permute-start(bf16[4,4,16,128]{3,2,1,0:T(8,128)(2,1)S(1)} %collective-permute-done.3.second.refs_4_), channel_id=1, source_target_pairs={{0,1},{1,0},{2,3},{3,2},{4,5},{5,4},{6,7},{7,6},{8,9},{9,8},{10,11... | collective-permute-start | bytes 196616 | tf_op jit(solution)/shard_map/ppermute | solution.py:196
  14.4 2.0 %collective-permute-start.10 = (bf16[4,4,16,128]{3,2,1,0:T(8,128)(2,1)S(1)}, bf16[4,4,16,128]{3,2,1,0:T(8,128)(2,1)S(1)}, u32[]{:S(2)}, u32[]{:S(2)}) collective-permute-start(bf16[4,4,16,128]{3,2,1,0:T(8,128)(2,1)S(1)} %collective-permute-done.4.corner_2.refs_5_), channel_id=1, source_target_pairs={{0,1},{1,0},{2,3},{3,2},{4,5},{5,4},{6,7},{7,6},{8,9},{9,8},{10,11... | collective-permute-start | bytes 196616 | tf_op jit(solution)/shard_map/ppermute | solution.py:196
  16.4 1.3 %collective-permute-start.8 = (bf16[4,4,16,128]{3,2,1,0:T(8,128)(2,1)S(1)}, bf16[4,4,16,128]{3,2,1,0:T(8,128)(2,1)S(1)}, u32[]{:S(2)}, u32[]{:S(2)}) collective-permute-start(bf16[4,4,16,128]{3,2,1,0:T(8,128)(2,1)S(1)} %collective-permute-done.2.corner.refs_3_), channel_id=1, source_target_pairs={{0,1},{1,0},{2,3},{3,2},{4,5},{5,4},{6,7},{7,6},{8,9},{9,8},{10,11... | collective-permute-start | bytes 196616 | tf_op jit(solution)/shard_map/ppermute | solution.py:196
  22.6 1.5 %collective-permute-start.11 = (bf16[6,8,16,128]{3,2,1,0:T(8,128)(2,1)S(1)}, bf16[6,8,16,128]{3,2,1,0:T(8,128)(2,1)S(1)}, u32[]{:S(2)}, u32[]{:S(2)}) collective-permute-start(bf16[6,8,16,128]{3,2,1,0:T(8,128)(2,1)S(1)} %get-tuple-element.23.grad.refs_12_), channel_id=1, source_target_pairs={{0,1},{1,0},{2,3},{3,2},{4,5},{5,4},{6,7},{7,6},{8,9},{9,8},{10,11... | collective-permute-start | bytes 589832 | tf_op jit(solution)/shard_map/ppermute | solution.py:196
  26.0 15.8 %collective-permute-start.12 = (bf16[992,128]{1,0:T(8,128)(2,1)S(1)}, bf16[992,128]{1,0:T(8,128)(2,1)S(1)}, u32[]{:S(2)}, u32[]{:S(2)}) collective-permute-start(bf16[992,128]{1,0:T(8,128)(2,1)S(1)} %get-tuple-element.31), channel_id=1, source_target_pairs={{0,4},{4,0},{8,12},{12,8},{1,5},{5,1},{9,13},{13,9},{2,6},{6,2},{1... | collective-permute-start | bytes 761864 | tf_op jit(solution)/shard_map/ppermute | solution.py:196
  30.2 1.3 %collective-permute-start.14 = (f32[136,128]{1,0:T(8,128)S(1)}, f32[136,128]{1,0:T(8,128)S(1)}, u32[]{:S(2)}, u32[]{:S(2)}) collective-permute-start(f32[136,128]{1,0:T(8,128)S(1)} %get-tuple-element.33), channel_id=1, source_target_pairs={{0,1},{1,0},{2,3},{3,2},{4,5},{5,4},{6,7},{7,6},{8,9},{9,8},{10,11... | collective-permute-start | bytes 208904 | tf_op jit(solution)/shard_map/ppermute | solution.py:196
  31.5 4.4 %collective-permute-start.15 = (f32[136,128]{1,0:T(8,128)S(1)}, f32[136,128]{1,0:T(8,128)S(1)}, u32[]{:S(2)}, u32[]{:S(2)}) collective-permute-start(f32[136,128]{1,0:T(8,128)S(1)} %add.24), channel_id=1, source_target_pairs={{0,2},{2,0},{1,3},{3,1},{4,6},{6,4},{5,7},{7,5},{8,10},{10,8},{9,1... | collective-permute-start | bytes 208904 | tf_op jit(solution)/shard_map/ppermute | solution.py:196
  35.9 4.4 %collective-permute-start.16 = (f32[136,128]{1,0:T(8,128)S(1)}, f32[136,128]{1,0:T(8,128)S(1)}, u32[]{:S(2)}, u32[]{:S(2)}) collective-permute-start(f32[136,128]{1,0:T(8,128)S(1)} %add.25), channel_id=1, source_target_pairs={{0,4},{4,0},{8,12},{12,8},{1,5},{5,1},{9,13},{13,9},{2,6},{6,2},{1... | collective-permute-start | bytes 208904 | tf_op jit(solution)/shard_map/ppermute | solution.py:196
  40.3 7.2 %collective-permute-start.17 = (f32[136,128]{1,0:T(8,128)S(1)}, f32[136,128]{1,0:T(8,128)S(1)}, u32[]{:S(2)}, u32[]{:S(2)}) collective-permute-start(f32[136,128]{1,0:T(8,128)S(1)} %add.26), channel_id=1, source_target_pairs={{0,8},{4,12},{8,0},{12,4},{1,9},{5,13},{9,1},{13,5},{2,10},{6,14},... | collective-permute-start | bytes 208904 | tf_op jit(solution)/shard_map/ppermute | solution.py:196
  41.8 8.4 %collective-permute-start.13 = (bf16[496,128]{1,0:T(8,128)(2,1)S(1)}, bf16[496,128]{1,0:T(8,128)(2,1)S(1)}, u32[]{:S(2)}, u32[]{:S(2)}) collective-permute-start(bf16[496,128]{1,0:T(8,128)(2,1)S(1)} %add_convert_fusion), channel_id=1, source_target_pairs={{0,8},{4,12},{8,0},{12,4},{1,9},{5,13},{9,1},{13,5},{2,10},{6,14},... | collective-permute-start | bytes 380936 | tf_op jit(solution)/shard_map/ppermute | solution.py:196

commit v4 on v3

--- a/solution.py
+++ b/solution.py
@@ -262,7 +262,9 @@
 
 
 def below_and_above(first, second):
-    odd = lax.rem(lax.axis_index("gx"), 2) == 1
+    gx = lax.axis_index("gx")
+    odd = lax.rem(gx, 2) == 1
+    second = jnp.where(jnp.logical_or(gx == 1, gx == 2), second, jnp.zeros_like(second))
     return jnp.where(odd, first, second), jnp.where(odd, second, first)
 
 
@@ -311,19 +313,25 @@
         ].astype(BF16)
     box = (size_x + 2, 2 * size_y, size_z, channels)
     load.wait()
-    total = jnp.zeros((box[0] * box[1] * box[2], channels), F32)
-    for along_x, along_y, _, count, first_tap in tap_groups():
+    def product(first_x, layers, first_y, lines, taps, count):
         patch = shifted[
-            2 + along_x : 2 + along_x + box[0],
-            2 + along_y : 2 + along_y + box[1],
-            :,
-            : count * channels,
+            first_x : first_x + layers, first_y : first_y + lines, :, : count * channels
         ].reshape(-1, count * channels)
-        weights = kernel[first_tap : first_tap + count].reshape(count * channels, channels)
-        total = total + jnp.dot(patch, weights, preferred_element_type=F32)
+        columns = [kernel[tap : tap + count].reshape(count * channels, channels) for tap in taps]
+        weights = jnp.concatenate(columns, axis=1) if len(columns) > 1 else columns[0]
+        out = jnp.dot(patch, weights, preferred_element_type=F32)
+        return out.reshape(layers, lines, size_z, len(taps) * channels)
+
+    total = jnp.zeros(box, F32)
+    for along_y in range(5):
+        pair = product(0, box[0] + 1, along_y, box[1], (5 * along_y, 25 + 5 * along_y), 5)
+        total = total + pair[:-1, :, :, :channels] + pair[1:, :, :, channels:]
+    pair = product(2, box[0], 0, box[1] + 1, (50, 55), 5)
+    total = total + pair[:, :-1, :, :channels] + pair[:, 1:, :, channels:]
+    total = total + product(2, box[0], 2, box[1], (60,), 2)
     signed = level[...]
     latent = wide[2:, 2 : 2 + box[1], EDGE : EDGE + size_z]
-    difference = (total.reshape(box) - latent) * (1.0 / (signed * signed))
+    difference = (total - latent) * (1.0 / (signed * signed))
     grad[...] = jnp.where(signed > 0.0, difference, 0.0).astype(BF16)
     held[...] = -difference[:size_x]
     rest[...] = held[:, pl.ds(near_y, size_y)]
@@ -373,16 +381,16 @@
         share = product[other, pl.ds(offset, rows)] * (1.0 / voxels)
         if other == 0:
             mine[...] = share
-        elif other == 2:
+        elif other == 3:
             later[...] = share
         else:
-            half = (other // 2) * rows
+            half = (other - 1) * rows
             message[half : half + rows] = share.astype(message.dtype)
 
 
 def feature_kernel(
     grad, grad_z, kernel, rest, root, features, gamma, block,
-    grad_features, sums, wide, shifted,
+    grad_features, mine, theirs, wide, shifted,
 ):
     size_x, size_y, size_z, channels = features.shape
     voxels = size_x * size_y * size_z
@@ -420,11 +428,27 @@
     )
     grad_features[...] = (latent_grad * inv_root - feats * coupled).astype(BF16).reshape(features.shape)
     factor = 0.5 / math.sqrt(voxels)
-    sums[:channels] = -factor * jnp.dot(
+    sums = -factor * jnp.dot(
         (feats * feats).T, weighted, precision=HIGHEST, preferred_element_type=F32
     )
-    ones = jnp.sum(weighted, axis=0, keepdims=True)
-    sums[channels:] = -factor * jnp.broadcast_to(ones, (8, channels))
+    ones = -factor * jnp.broadcast_to(jnp.sum(weighted, axis=0, keepdims=True), (8, channels))
+    half = channels // 2
+    first_z = lax.axis_index("gz") == 0
+    mine[:half] = jnp.where(first_z, sums[:half], sums[half:])
+    theirs[:half] = jnp.where(first_z, sums[half:], sums[:half])
+    mine[half:] = ones
+    theirs[half:] = ones
+
+
+def join_kernel(mine, theirs, kept, halves, quarter, gamma, beta, share):
+    rows = share.shape[0]
+    share[...] = kept[...] + halves[:rows].astype(F32) + quarter[...].astype(F32)
+    half = gamma.shape[0] // 2
+    first_z = lax.axis_index("gz") == 0
+    own, other = mine[:half], theirs[:half]
+    gamma[:half] = jnp.where(first_z, own, other)
+    gamma[half:] = jnp.where(first_z, other, own)
+    beta[...] = mine[half : half + 1]
 
 
 def call(body, outs, scratch, args, far=()):
@@ -465,18 +489,13 @@
         (features, scales, occupancy, gamma, beta.reshape(1, channels)),
         (0, 1, 2, 3, 4),
     )
-    middle = lambda x: (3 - x if x in (1, 2) else -1,)
+    middle = lambda x, z: (3 - x, z) if x in (1, 2) else (x, 1 - z)
     side = flipped(across_y, "gy")
     first = exchanged(first_x, "gx", lambda x: (x ^ 1,))
-    second = exchanged(second_x, "gx", middle)
-    upward, downward = side[size_x - 2 : size_x], side[:2]
-    odd = lax.rem(lax.axis_index("gx"), 2) == 1
-    levels = side[size_x : size_x + 2]
-    corner = exchanged(
-        jnp.concatenate([jnp.where(odd, downward, upward), levels]), "gx", lambda x: (x ^ 1,)
-    )
+    second = exchanged(second_x, ("gx", "gz"), middle)
+    corner = exchanged(first_x, ("gx", "gy"), lambda x, y: (x ^ 1, 1 - y))
     corner_2 = exchanged(
-        jnp.concatenate([jnp.where(odd, upward, downward), levels]), "gx", middle
+        second_x, ("gx", "gy", "gz"), lambda x, y, z: (3 - x, 1 - y, z) if x in (1, 2) else (x, y, 1 - z)
     )
     sent = (side, first, corner, second, corner_2)
     around = (across_y,) + sent + tuple(flipped(part, "gz") for part in (latent,) + sent)
@@ -514,22 +533,28 @@
         around + (grad, grad_z),
     )
     halves = exchanged(message, "gx", lambda x: (x ^ 1,))
-    grad_features, sums = call(
+    grad_features, sums, others = call(
         feature_kernel,
-        [jax.ShapeDtypeStruct(shape, BF16), pltpu.VMEM((channels + 8, channels), F32)],
+        [jax.ShapeDtypeStruct(shape, BF16)] + [pltpu.VMEM((channels // 2 + 8, channels), F32)] * 2,
         [
             pltpu.VMEM((size_x + 2, wide_y, wide_z, channels), F32),
             pltpu.VMEM((size_x + 2, size_y + 4, size_z, 5 * channels), BF16),
         ],
         (grad, grad_z, kept_kernel, rest, root, kept_features, kept_gamma, across_y),
     )
-    sums = sums + flipped(sums, "gz")
-    quarter = exchanged((later + halves[rows:].astype(F32)).astype(BF16), "gx", lambda x: (x ^ 2,))
+    sums = sums + flipped(others, "gz")
+    quarter = exchanged((later + halves[rows:].astype(F32)).astype(BF16), "gx", lambda x: (3 - x,))
     sums = sums + flipped(sums, "gy")
     sums = sums + exchanged(sums, "gx", lambda x: (x ^ 1,))
     sums = sums + exchanged(sums, "gx", lambda x: (x ^ 2,))
-    share = mine + halves[:rows].astype(F32) + quarter.astype(F32)
-    return grad_features, share.reshape(-1), sums[:channels], sums[channels]
+    struct = jax.ShapeDtypeStruct
+    grad_gamma, grad_beta, share = call(
+        join_kernel,
+        [struct((channels, channels), F32), struct((1, channels), F32), struct((rows, channels), F32)],
+        [],
+        (sums, flipped(sums, "gz"), mine, halves, quarter),
+    )
+    return grad_features, share.reshape(-1), grad_gamma, grad_beta.reshape(channels)
 
 
 def chosen(features, scales, occupancy, kernel, gamma, beta):

time: 51.1 us -> 45.1 us (0.88)
  starting transfers between devices: 18.7 us -> 14.4 us
  local copies, waits for them, and re-layouts: 1.15 us -> 0 us
  other arithmetic: 0.83 us -> 0.06 us
    ppermute x18 -> x19, starting transfers between devices: 18.7 us -> 14.4 us  [exchanged(): return lax.ppermute(value, names if len(names) > 1 else names[0], pairs)]
    reshape x1 -> x0, other arithmetic: 0.73 us -> none  [fast_local(): return (grad_features, share.reshape(-1), sums[:channels], sums[channels])]
    slice x1 -> x0, local copies, waits for them, and re-layouts: 0.63 us -> none  [fast_local(): return (grad_features, share.reshape(-1), sums[:channels], sums[channels])]
    squeeze x1 -> x0, local copies, waits for them, and re-layouts: 0.51 us -> none  [fast_local(): return (grad_features, share.reshape(-1), sums[:channels], sums[channels])]
    ppermute x18 -> x19, waiting for transfers between devices: 19 us -> 19.5 us  [exchanged(): return lax.ppermute(value, names if len(names) > 1 else names[0], pairs)]
    pallas_call x4 -> x5, Pallas kernels: 10.5 us -> 10.3 us  [call(): pl.pallas_call(body, out_shape=outs, in_specs=[pl.BlockSpec(memory_space=...]
  transfers between devices with their start and end apart: 18 -> 19, of which waited for: 9 -> 13; matrix products, arithmetic and copies ran while one was open for 2% -> 0% of each run, Pallas kernels for 5% -> 5%
where the time goes in v4:
time: 45.1 us; the launch traced here: 44.9 us
  waiting for transfers between devices  19.5 us (43%)
  starting transfers between devices  14.4 us (32%)
  Pallas kernels  10.3 us (23%)
  between operations  0.69 us (2%)
    ppermute x19, waiting for transfers between devices, exchanged(): return lax.ppermute(value, names if len(names) > 1 else names[0], pairs)  19.5 us
    ppermute x19, starting transfers between devices, exchanged(): return lax.ppermute(value, names if len(names) > 1 else names[0], pairs)  14.4 us
    pallas_call x5, Pallas kernels, call(): pl.pallas_call(body, out_shape=outs, in_specs=[pl.BlockSpec(memory_space=...  10.3 us
  transfers between devices with their start and end apart: 19, of which 13 were waited for; matrix products, arithmetic and copies ran while one was open for 0% of the time, Pallas kernels for 5%

profile of v4, /device:TPU:0, one launch (start us, length us, event | category | flops | bytes accessed | tf_op | source)
XLA Modules:
  0.0 44.9 jit_solution(11367429333872228831)
XLA Ops:
  0.6 1.3 %shard_map.93 = (bf16[4,4,16,128]{3,2,1,0:T(8,128)(2,1)S(1)}, bf16[8,4,16,128]{3,2,1,0:T(8,128)(2,1)S(1)}, bf16[4,4,16,128]{3,2,1,0:T(8,128)(2,1)S(1)}, bf16[4,4...) custom-call(bf16[4,4,16,128]{3,2,1,0:T(8,128)(2,1)} %far_features.1,, ...), custom_call_target="tpu_custom_call" | custom-call | tf_op jit(solution)/shard_map/pallas_call | solution.py:457
  1.9 3.0 %collective-permute-start = (bf16[8,4,16,128]{3,2,1,0:T(8,128)(2,1)S(1)}, bf16[8,4,16,128]{3,2,1,0:T(8,128)(2,1)S(1)}, u32[]{:S(2)}, u32[]{:S(2)}) collective-permute-start(bf16[8,4,16,128]{3,2,1,0:T(8,128)(2,1)S(1)} %get-tuple-element.23.own.block.refs_0_), channel_id=1, source_target_pairs={{0,2},{2,0},{1,3},{3,1},{4,6},{6,4},{5,7},{7,5},{8,10},{10,8},{9,1... | collective-permute-start | bytes 393224 | tf_op jit(solution)/shard_map/ppermute | solution.py:196
  4.9 1.5 %collective-permute-start.2 = (bf16[4,4,16,128]{3,2,1,0:T(8,128)(2,1)S(1)}, bf16[4,4,16,128]{3,2,1,0:T(8,128)(2,1)S(1)}, u32[]{:S(2)}, u32[]{:S(2)}) collective-permute-start(bf16[4,4,16,128]{3,2,1,0:T(8,128)(2,1)S(1)} %get-tuple-element.24), channel_id=1, source_target_pairs={{0,6},{2,4},{4,2},{6,0},{8,14},{10,12},{12,10},{14,8},{1,7},{3,5},... | collective-permute-start | bytes 196616 | tf_op jit(solution)/shard_map/ppermute | solution.py:196
  6.5 0.1 collective-permute-start.1
  6.6 0.2 collective-permute-start.4
  6.7 0.3 collective-permute-start.3
  7.1 2.0 %collective-permute-done.side.refs_1_ = bf16[8,4,16,128]{3,2,1,0:T(8,128)(2,1)S(1)} collective-permute-done((bf16[8,4,16,128]{3,2,1,0:T(8,128)(2,1)S(1)}, bf16[8,4,16,128]{3,2,1,0:T(8,128)(2,1)S(1)}, u32[]{:S(2)}, u32[]{:S(2)}) %collective-permute-start) | collective-permute-done | bytes 131104 | tf_op jit(solution)/shard_map/ppermute | solution.py:196
  9.1 1.4 %collective-permute-done.2.corner.refs_3_ = bf16[4,4,16,128]{3,2,1,0:T(8,128)(2,1)S(1)} collective-permute-done((bf16[4,4,16,128]{3,2,1,0:T(8,128)(2,1)S(1)}, bf16[4,4,16,128]{3,2,1,0:T(8,128)(2,1)S(1)}, u32[]{:S(2)}, u32[]{:S(2)}) %collective-permute-start.2) | collective-permute-done | bytes 65568 | tf_op jit(solution)/shard_map/ppermute | solution.py:196
  10.4 0.3 collective-permute-done.1.first.refs_2_
  10.7 0.2 collective-permute-start.7
  11.0 0.3 collective-permute-start.10
  11.3 0.2 collective-permute-start.9
  11.5 0.2 collective-permute-done.8.corner_z.refs_9_
  11.7 0.3 collective-permute-done.7.first_z.refs_8_
  12.0 0.2 collective-permute-done.10.corner_2z.refs_11_
  12.2 0.3 collective-permute-done.9.second_z.refs_10_
  12.5 4.0 %shard_map.94 = (bf16[6,8,16,128]{3,2,1,0:T(8,128)(2,1)S(1)}, f32[4,4,16,128]{3,2,1,0:T(8,128)S(1)}, bf16[62,128,128]{2,1,0:T(8,128)(2,1)S(1)}) custom-call(bf16[8,4,16,128]{3,2,1,0:T(8,128)(2,1)S(1)} %get-tuple-element.23.own.block.refs_0_, bf16[8,4,16,128]{3,2,1,0:T(8,128)(2,1)S(1)} %collective-permute-done.side.refs_1_, ...), custom_call_target="tpu_custom_call" | custom-call | tf_op jit(solution)/shard_map/pallas_call | solution.py:457
  16.5 0.3 collective-permute-start.11
  16.8 1.2 %collective-permute-done.11.grad_z.refs_13_ = bf16[6,8,16,128]{3,2,1,0:T(8,128)(2,1)S(1)} collective-permute-done((bf16[6,8,16,128]{3,2,1,0:T(8,128)(2,1)S(1)}, bf16[6,8,16,128]{3,2,1,0:T(8,128)(2,1)S(1)}, u32[]{:S(2)}, u32[]{:S(2)}) %collective-permute-start.11) | collective-permute-done | bytes 196640 | tf_op jit(solution)/shard_map/ppermute | solution.py:196
  18.0 1.9 %shard_map.96 = (f32[496,128]{1,0:T(8,128)S(1)}, f32[496,128]{1,0:T(8,128)S(1)}, bf16[992,128]{1,0:T(8,128)(2,1)S(1)}) custom-call(bf16[8,4,16,128]{3,2,1,0:T(8,128)(2,1)S(1)} %get-tuple-element.23.own.block.refs_0_, bf16[8,4,16,128]{3,2,1,0:T(8,128)(2,1)S(1)} %collective-permute-done.side.refs_1_, ...), custom_call_target="tpu_custom_call" | custom-call | tf_op jit(solution)/shard_map/pallas_call | solution.py:457
  19.9 4.0 %collective-permute-start.17 = (bf16[992,128]{1,0:T(8,128)(2,1)S(1)}, bf16[992,128]{1,0:T(8,128)(2,1)S(1)}, u32[]{:S(2)}, u32[]{:S(2)}) collective-permute-start(bf16[992,128]{1,0:T(8,128)(2,1)S(1)} %get-tuple-element.37), channel_id=1, source_target_pairs={{0,4},{4,0},{8,12},{12,8},{1,5},{5,1},{9,13},{13,9},{2,6},{6,2},{1... | collective-permute-start | bytes 761864 | tf_op jit(solution)/shard_map/ppermute | solution.py:196
  24.0 2.4 %shard_map.95 = (bf16[4,4,16,128]{3,2,1,0:T(8,128)(2,1)}, f32[72,128]{1,0:T(8,128)S(1)}, f32[72,128]{1,0:T(8,128)S(1)}) custom-call(bf16[6,8,16,128]{3,2,1,0:T(8,128)(2,1)S(1)} %get-tuple-element.27.grad.refs_12_, bf16[6,8,16,128]{3,2,1,0:T(8,128)(2,1)S(1)} %collective-permute-done.11.grad_z.refs_13_, bf16[62,128,128]{2,1,0:T(8,128)(2,1)S(1)} %get-tuple-element.28.kernel, ...), custom_call_target="tpu_custom_call" | custom-call | tf_op jit(solution)/shard_map/pallas_call | solution.py:457
  26.4 1.2 %collective-permute-done.12 = f32[72,128]{1,0:T(8,128)S(1)} collective-permute-done((f32[72,128]{1,0:T(8,128)S(1)}, f32[72,128]{1,0:T(8,128)S(1)}, u32[]{:S(2)}, u32[]{:S(2)}) %collective-permute-start.12) | collective-permute-done | bytes 36896 | tf_op jit(solution)/shard_map/ppermute | solution.py:196
  27.6 0.6 %collective-permute-start.13 = (f32[72,128]{1,0:T(8,128)S(1)}, f32[72,128]{1,0:T(8,128)S(1)}, u32[]{:S(2)}, u32[]{:S(2)}) collective-permute-start(f32[72,128]{1,0:T(8,128)S(1)} %add.15), channel_id=1, source_target_pairs={{0,2},{2,0},{1,3},{3,1},{4,6},{6,4},{5,7},{7,5},{8,10},{10,8},{9,1... | collective-permute-start | bytes 110600 | tf_op jit(solution)/shard_map/ppermute | solution.py:196
  28.2 2.3 %collective-permute-done.17.halves = bf16[992,128]{1,0:T(8,128)(2,1)S(1)} collective-permute-done((bf16[992,128]{1,0:T(8,128)(2,1)S(1)}, bf16[992,128]{1,0:T(8,128)(2,1)S(1)}, u32[]{:S(2)}, u32[]{:S(2)}) %collective-permute-start.17) | collective-permute-done | bytes 253984 | tf_op jit(solution)/shard_map/ppermute | solution.py:196
  30.5 2.0 %collective-permute-start.18 = (bf16[496,128]{1,0:T(8,128)(2,1)S(1)}, bf16[496,128]{1,0:T(8,128)(2,1)S(1)}, u32[]{:S(2)}, u32[]{:S(2)}) collective-permute-start(bf16[496,128]{1,0:T(8,128)(2,1)S(1)} %add_convert_fusion), channel_id=1, source_target_pairs={{0,12},{4,8},{8,4},{12,0},{1,13},{5,9},{9,5},{13,1},{2,14},{6,10},... | collective-permute-start | bytes 380936 | tf_op jit(solution)/shard_map/ppermute | solution.py:196
  32.5 0.9 %collective-permute-start.14 = (f32[72,128]{1,0:T(8,128)S(1)}, f32[72,128]{1,0:T(8,128)S(1)}, u32[]{:S(2)}, u32[]{:S(2)}) collective-permute-start(f32[72,128]{1,0:T(8,128)S(1)} %add.16), channel_id=1, source_target_pairs={{0,4},{4,0},{8,12},{12,8},{1,5},{5,1},{9,13},{13,9},{2,6},{6,2},{1... | collective-permute-start | bytes 110600 | tf_op jit(solution)/shard_map/ppermute | solution.py:196
  33.4 4.6 %collective-permute-done.14 = f32[72,128]{1,0:T(8,128)S(1)} collective-permute-done((f32[72,128]{1,0:T(8,128)S(1)}, f32[72,128]{1,0:T(8,128)S(1)}, u32[]{:S(2)}, u32[]{:S(2)}) %collective-permute-start.14) | collective-permute-done | bytes 36896 | tf_op jit(solution)/shard_map/ppermute | solution.py:196
  38.0 0.6 %collective-permute-start.15 = (f32[72,128]{1,0:T(8,128)S(1)}, f32[72,128]{1,0:T(8,128)S(1)}, u32[]{:S(2)}, u32[]{:S(2)}) collective-permute-start(f32[72,128]{1,0:T(8,128)S(1)} %add.17), channel_id=1, source_target_pairs={{0,8},{4,12},{8,0},{12,4},{1,9},{5,13},{9,1},{13,5},{2,10},{6,14},... | collective-permute-start | bytes 110600 | tf_op jit(solution)/shard_map/ppermute | solution.py:196
  38.6 4.3 %collective-permute-done.15 = f32[72,128]{1,0:T(8,128)S(1)} collective-permute-done((f32[72,128]{1,0:T(8,128)S(1)}, f32[72,128]{1,0:T(8,128)S(1)}, u32[]{:S(2)}, u32[]{:S(2)}) %collective-permute-start.15) | collective-permute-done | bytes 36896 | tf_op jit(solution)/shard_map/ppermute | solution.py:196
  43.0 1.2 %collective-permute-done.16.theirs = f32[72,128]{1,0:T(8,128)S(1)} collective-permute-done((f32[72,128]{1,0:T(8,128)S(1)}, f32[72,128]{1,0:T(8,128)S(1)}, u32[]{:S(2)}, u32[]{:S(2)}) %collective-permute-start.16) | collective-permute-done | bytes 36896 | tf_op jit(solution)/shard_map/ppermute | solution.py:196
  44.2 0.8 %shard_map.97 = (f32[128,128]{1,0:T(8,128)}, f32[1,128]{1,0:T(1,128)}, f32[496,128]{1,0:T(8,128)}) custom-call(f32[72,128]{1,0:T(8,128)S(1)} %add.18.mine, f32[72,128]{1,0:T(8,128)S(1)} %collective-permute-done.16.theirs, f32[496,128]{1,0:T(8,128)S(1)} %get-tuple-element.36.kept, bf16[992,128]{1,0:T(8,128)(2,1)S(1)} %collective-permute-done.17.halves, ...), custom_call_target="tpu_custom_call" | custom-call | tf_op jit(solution)/shard_map/pallas_call | solution.py:457
  (16 shorter events, 0.1 us)
Async XLA Ops:
  1.9 7.2 %collective-permute-start = (bf16[8,4,16,128]{3,2,1,0:T(8,128)(2,1)S(1)}, bf16[8,4,16,128]{3,2,1,0:T(8,128)(2,1)S(1)}, u32[]{:S(2)}, u32[]{:S(2)}) collective-permute-start(bf16[8,4,16,128]{3,2,1,0:T(8,128)(2,1)S(1)} %get-tuple-element.23.own.block.refs_0_), channel_id=1, source_target_pairs={{0,2},{2,0},{1,3},{3,1},{4,6},{6,4},{5,7},{7,5},{8,10},{10,8},{9,1... | collective-permute-start | bytes 393224 | tf_op jit(solution)/shard_map/ppermute | solution.py:196
  4.9 1.8 %collective-permute-start.5 = (bf16[4,4,16,128]{3,2,1,0:T(8,128)(2,1)S(1)}, bf16[4,4,16,128]{3,2,1,0:T(8,128)(2,1)S(1)}, u32[]{:S(2)}, u32[]{:S(2)}) collective-permute-start(bf16[4,4,16,128]{3,2,1,0:T(8,128)(2,1)S(1)} %get-tuple-element.26), channel_id=1, source_target_pairs={{0,1},{1,0},{2,3},{3,2},{4,5},{5,4},{6,7},{7,6},{8,9},{9,8},{10,11... | collective-permute-start | bytes 196616 | tf_op jit(solution)/shard_map/ppermute | solution.py:196
  4.9 5.5 %collective-permute-start.2 = (bf16[4,4,16,128]{3,2,1,0:T(8,128)(2,1)S(1)}, bf16[4,4,16,128]{3,2,1,0:T(8,128)(2,1)S(1)}, u32[]{:S(2)}, u32[]{:S(2)}) collective-permute-start(bf16[4,4,16,128]{3,2,1,0:T(8,128)(2,1)S(1)} %get-tuple-element.24), channel_id=1, source_target_pairs={{0,6},{2,4},{4,2},{6,0},{8,14},{10,12},{12,10},{14,8},{1,7},{3,5},... | collective-permute-start | bytes 196616 | tf_op jit(solution)/shard_map/ppermute | solution.py:196
  6.5 4.3 %collective-permute-start.1 = (bf16[4,4,16,128]{3,2,1,0:T(8,128)(2,1)S(1)}, bf16[4,4,16,128]{3,2,1,0:T(8,128)(2,1)S(1)}, u32[]{:S(2)}, u32[]{:S(2)}) collective-permute-start(bf16[4,4,16,128]{3,2,1,0:T(8,128)(2,1)S(1)} %get-tuple-element.24), channel_id=1, source_target_pairs={{0,4},{4,0},{8,12},{12,8},{1,5},{5,1},{9,13},{13,9},{2,6},{6,2},{1... | collective-permute-start | bytes 196616 | tf_op jit(solution)/shard_map/ppermute | solution.py:196
  6.6 4.4 %collective-permute-start.4 = (bf16[4,4,16,128]{3,2,1,0:T(8,128)(2,1)S(1)}, bf16[4,4,16,128]{3,2,1,0:T(8,128)(2,1)S(1)}, u32[]{:S(2)}, u32[]{:S(2)}) collective-permute-start(bf16[4,4,16,128]{3,2,1,0:T(8,128)(2,1)S(1)} %get-tuple-element.25), channel_id=1, source_target_pairs={{0,1},{1,0},{2,3},{3,2},{4,10},{5,11},{6,8},{7,9},{8,6},{9,7},{10,... | collective-permute-start | bytes 196616 | tf_op jit(solution)/shard_map/ppermute | solution.py:196
  6.7 4.5 %collective-permute-start.3 = (bf16[4,4,16,128]{3,2,1,0:T(8,128)(2,1)S(1)}, bf16[4,4,16,128]{3,2,1,0:T(8,128)(2,1)S(1)}, u32[]{:S(2)}, u32[]{:S(2)}) collective-permute-start(bf16[4,4,16,128]{3,2,1,0:T(8,128)(2,1)S(1)} %get-tuple-element.25), channel_id=1, source_target_pairs={{0,1},{1,0},{4,8},{5,9},{8,4},{9,5},{12,13},{13,12},{2,3},{3,2},{6... | collective-permute-start | bytes 196616 | tf_op jit(solution)/shard_map/ppermute | solution.py:196
  9.1 3.4 %collective-permute-start.6 = (bf16[8,4,16,128]{3,2,1,0:T(8,128)(2,1)S(1)}, bf16[8,4,16,128]{3,2,1,0:T(8,128)(2,1)S(1)}, u32[]{:S(2)}, u32[]{:S(2)}) collective-permute-start(bf16[8,4,16,128]{3,2,1,0:T(8,128)(2,1)S(1)} %collective-permute-done.side.refs_1_), channel_id=1, source_target_pairs={{0,1},{1,0},{2,3},{3,2},{4,5},{5,4},{6,7},{7,6},{8,9},{9,8},{10,11... | collective-permute-start | bytes 393224 | tf_op jit(solution)/shard_map/ppermute | solution.py:196
  10.4 1.3 %collective-permute-start.8 = (bf16[4,4,16,128]{3,2,1,0:T(8,128)(2,1)S(1)}, bf16[4,4,16,128]{3,2,1,0:T(8,128)(2,1)S(1)}, u32[]{:S(2)}, u32[]{:S(2)}) collective-permute-start(bf16[4,4,16,128]{3,2,1,0:T(8,128)(2,1)S(1)} %collective-permute-done.2.corner.refs_3_), channel_id=1, source_target_pairs={{0,1},{1,0},{2,3},{3,2},{4,5},{5,4},{6,7},{7,6},{8,9},{9,8},{10,11... | collective-permute-start | bytes 196616 | tf_op jit(solution)/shard_map/ppermute | solution.py:196
  10.7 1.3 %collective-permute-start.7 = (bf16[4,4,16,128]{3,2,1,0:T(8,128)(2,1)S(1)}, bf16[4,4,16,128]{3,2,1,0:T(8,128)(2,1)S(1)}, u32[]{:S(2)}, u32[]{:S(2)}) collective-permute-start(bf16[4,4,16,128]{3,2,1,0:T(8,128)(2,1)S(1)} %collective-permute-done.1.first.refs_2_), channel_id=1, source_target_pairs={{0,1},{1,0},{2,3},{3,2},{4,5},{5,4},{6,7},{7,6},{8,9},{9,8},{10,11... | collective-permute-start | bytes 196616 | tf_op jit(solution)/shard_map/ppermute | solution.py:196
  11.0 1.3 %collective-permute-start.10 = (bf16[4,4,16,128]{3,2,1,0:T(8,128)(2,1)S(1)}, bf16[4,4,16,128]{3,2,1,0:T(8,128)(2,1)S(1)}, u32[]{:S(2)}, u32[]{:S(2)}) collective-permute-start(bf16[4,4,16,128]{3,2,1,0:T(8,128)(2,1)S(1)} %collective-permute-done.4.corner_2.refs_5_), channel_id=1, source_target_pairs={{0,1},{1,0},{2,3},{3,2},{4,5},{5,4},{6,7},{7,6},{8,9},{9,8},{10,11... | collective-permute-start | bytes 196616 | tf_op jit(solution)/shard_map/ppermute | solution.py:196
  11.3 1.3 %collective-permute-start.9 = (bf16[4,4,16,128]{3,2,1,0:T(8,128)(2,1)S(1)}, bf16[4,4,16,128]{3,2,1,0:T(8,128)(2,1)S(1)}, u32[]{:S(2)}, u32[]{:S(2)}) collective-permute-start(bf16[4,4,16,128]{3,2,1,0:T(8,128)(2,1)S(1)} %collective-permute-done.3.second.refs_4_), channel_id=1, source_target_pairs={{0,1},{1,0},{2,3},{3,2},{4,5},{5,4},{6,7},{7,6},{8,9},{9,8},{10,11... | collective-permute-start | bytes 196616 | tf_op jit(solution)/shard_map/ppermute | solution.py:196
  16.5 1.5 %collective-permute-start.11 = (bf16[6,8,16,128]{3,2,1,0:T(8,128)(2,1)S(1)}, bf16[6,8,16,128]{3,2,1,0:T(8,128)(2,1)S(1)}, u32[]{:S(2)}, u32[]{:S(2)}) collective-permute-start(bf16[6,8,16,128]{3,2,1,0:T(8,128)(2,1)S(1)} %get-tuple-element.27.grad.refs_12_), channel_id=1, source_target_pairs={{0,1},{1,0},{2,3},{3,2},{4,5},{5,4},{6,7},{7,6},{8,9},{9,8},{10,11... | collective-permute-start | bytes 589832 | tf_op jit(solution)/shard_map/ppermute | solution.py:196
  19.9 10.5 %collective-permute-start.17 = (bf16[992,128]{1,0:T(8,128)(2,1)S(1)}, bf16[992,128]{1,0:T(8,128)(2,1)S(1)}, u32[]{:S(2)}, u32[]{:S(2)}) collective-permute-start(bf16[992,128]{1,0:T(8,128)(2,1)S(1)} %get-tuple-element.37), channel_id=1, source_target_pairs={{0,4},{4,0},{8,12},{12,8},{1,5},{5,1},{9,13},{13,9},{2,6},{6,2},{1... | collective-permute-start | bytes 761864 | tf_op jit(solution)/shard_map/ppermute | solution.py:196
  26.4 1.2 %collective-permute-start.12 = (f32[72,128]{1,0:T(8,128)S(1)}, f32[72,128]{1,0:T(8,128)S(1)}, u32[]{:S(2)}, u32[]{:S(2)}) collective-permute-start(f32[72,128]{1,0:T(8,128)S(1)} %get-tuple-element.35), channel_id=1, source_target_pairs={{0,1},{1,0},{2,3},{3,2},{4,5},{5,4},{6,7},{7,6},{8,9},{9,8},{10,11... | collective-permute-start | bytes 110600 | tf_op jit(solution)/shard_map/ppermute | solution.py:196
  27.6 4.9 %collective-permute-start.13 = (f32[72,128]{1,0:T(8,128)S(1)}, f32[72,128]{1,0:T(8,128)S(1)}, u32[]{:S(2)}, u32[]{:S(2)}) collective-permute-start(f32[72,128]{1,0:T(8,128)S(1)} %add.15), channel_id=1, source_target_pairs={{0,2},{2,0},{1,3},{3,1},{4,6},{6,4},{5,7},{7,5},{8,10},{10,8},{9,1... | collective-permute-start | bytes 110600 | tf_op jit(solution)/shard_map/ppermute | solution.py:196
  30.5 13.7 %collective-permute-start.18 = (bf16[496,128]{1,0:T(8,128)(2,1)S(1)}, bf16[496,128]{1,0:T(8,128)(2,1)S(1)}, u32[]{:S(2)}, u32[]{:S(2)}) collective-permute-start(bf16[496,128]{1,0:T(8,128)(2,1)S(1)} %add_convert_fusion), channel_id=1, source_target_pairs={{0,12},{4,8},{8,4},{12,0},{1,13},{5,9},{9,5},{13,1},{2,14},{6,10},... | collective-permute-start | bytes 380936 | tf_op jit(solution)/shard_map/ppermute | solution.py:196
  32.5 5.5 %collective-permute-start.14 = (f32[72,128]{1,0:T(8,128)S(1)}, f32[72,128]{1,0:T(8,128)S(1)}, u32[]{:S(2)}, u32[]{:S(2)}) collective-permute-start(f32[72,128]{1,0:T(8,128)S(1)} %add.16), channel_id=1, source_target_pairs={{0,4},{4,0},{8,12},{12,8},{1,5},{5,1},{9,13},{13,9},{2,6},{6,2},{1... | collective-permute-start | bytes 110600 | tf_op jit(solution)/shard_map/ppermute | solution.py:196
  38.0 4.9 %collective-permute-start.15 = (f32[72,128]{1,0:T(8,128)S(1)}, f32[72,128]{1,0:T(8,128)S(1)}, u32[]{:S(2)}, u32[]{:S(2)}) collective-permute-start(f32[72,128]{1,0:T(8,128)S(1)} %add.17), channel_id=1, source_target_pairs={{0,8},{4,12},{8,0},{12,4},{1,9},{5,13},{9,1},{13,5},{2,10},{6,14},... | collective-permute-start | bytes 110600 | tf_op jit(solution)/shard_map/ppermute | solution.py:196
  43.0 1.2 %collective-permute-start.16 = (f32[72,128]{1,0:T(8,128)S(1)}, f32[72,128]{1,0:T(8,128)S(1)}, u32[]{:S(2)}, u32[]{:S(2)}) collective-permute-start(f32[72,128]{1,0:T(8,128)S(1)} %add.18.mine), channel_id=1, source_target_pairs={{0,1},{1,0},{2,3},{3,2},{4,5},{5,4},{6,7},{7,6},{8,9},{9,8},{10,11... | collective-permute-start | bytes 110600 | tf_op jit(solution)/shard_map/ppermute | solution.py:196

commit v5 on v4

--- a/solution.py
+++ b/solution.py
@@ -268,20 +268,31 @@
     return jnp.where(odd, first, second), jnp.where(odd, second, first)
 
 
-def z_edges(wide, spot, across, size_z):
-    first_z = lax.axis_index("gz") == 0
+def z_edges(wide, spot, across, size_z, low=0):
+    first_z = lax.axis_index("gz") == low
     across = across.astype(F32)
     wide[spot + (pl.ds(0, EDGE),)] = jnp.where(first_z, 0.0, across[:, :, size_z - EDGE :])
     wide[spot + (pl.ds(EDGE + size_z, EDGE),)] = jnp.where(first_z, across[:, :, :EDGE], 0.0)
 
 
+def load_kernel(far, near, arrival):
+    taps = far.shape[0]
+    cuts = [n * taps // 4 for n in range(5)]
+    loads = [
+        pltpu.make_async_copy(far.at[low:high], near.at[low:high], arrival.at[n])
+        for n, (low, high) in enumerate(zip(cuts[:-1], cuts[1:]))
+    ]
+    for load in loads:
+        load.start()
+    for load in loads:
+        load.wait()
+
+
 def mean_kernel(
     own, side, first, corner, second, corner_2,
     own_z, side_z, first_z, corner_z, second_z, corner_2z,
-    far_kernel, grad, rest, kernel, wide, shifted, level, held, arrival,
+    kernel, grad, rest, wide, shifted, level, held,
 ):
-    load = pltpu.make_async_copy(far_kernel, kernel, arrival)
-    load.start()
     size_x, _, size_z, channels = rest.shape
     size_y = own.shape[1]
     gy = lax.axis_index("gy")
@@ -312,7 +323,7 @@
             :, :, start : start + size_z, :
         ].astype(BF16)
     box = (size_x + 2, 2 * size_y, size_z, channels)
-    load.wait()
+
     def product(first_x, layers, first_y, lines, taps, count):
         patch = shifted[
             first_x : first_x + layers, first_y : first_y + lines, :, : count * channels
@@ -337,47 +348,78 @@
     rest[...] = held[:, pl.ds(near_y, size_y)]
 
 
-def share_kernel(spanned, voxels, *refs):
-    (own, side, first, corner, second, corner_2,
-     own_z, side_z, first_z, corner_z, second_z, corner_2z, grad, grad_z) = refs[:14]
-    mine, later, message, wide, flat, turned, product = refs[14:]
-    rows = mine.shape[0]
-    size_x, all_y, all_z, channels = flat.shape
-    size_y, size_z = all_y // 2, all_z // 2
+def share_taps(rows, channels, spanned):
     gx, gy, gz = lax.axis_index("gx"), lax.axis_index("gy"), lax.axis_index("gz")
-    blank = jnp.zeros((size_x + 2, 2, wide.shape[2], channels), F32)
-    wide[:, :2] = blank
-    wide[:, 2 + all_y :] = blank
-    for start in (0, EDGE + all_z):
-        wide[:, 2 : 2 + all_y, start : start + EDGE] = jnp.zeros((size_x + 2, all_y, EDGE, channels), F32)
-    for here_y, here_z, block, one, two in (
-        (True, True, own, first, second),
-        (False, True, side, corner, corner_2),
-        (True, False, own_z, first_z, second_z),
-        (False, False, side_z, corner_z, corner_2z),
-    ):
-        at_y = (gy if here_y else 1 - gy) * size_y
-        at_z = (gz if here_z else 1 - gz) * size_z
-        spot_y, spot_z = pl.ds(2 + at_y, size_y), pl.ds(pl.multiple_of(EDGE + at_z, EDGE), size_z)
-        wide[2:, spot_y, spot_z] = block[:size_x].astype(F32)
-        wide[:2, spot_y, spot_z] = below_and_above(one[:2], two[:2])[0].astype(F32)
-    flat[:, :, pl.ds(pl.multiple_of(gz * size_z, size_z), size_z)] = grad[:size_x]
-    flat[:, :, pl.ds(pl.multiple_of((1 - gz) * size_z, size_z), size_z)] = grad_z[:size_x]
-    turned[...] = flat[...].reshape(-1, channels).T
+    taps = []
     for other in range(4):
         first_row = (((gx ^ other) * 2 + gy) * 2 + gz) * rows
         first_tap = jnp.minimum(first_row // channels, 62 - spanned)
-        for level in range(5):
-            number = lax.rem(level + 5 - lax.rem(first_tap, 5), 5)
-            group = (first_tap + number) // 5
-            along_x, along_y = group // 5, lax.rem(group, 5)
-            start = EDGE + level - 2
-            patch = wide[pl.ds(along_x, size_x), pl.ds(along_y, all_y), start : start + all_z]
+        taps.append((first_row - first_tap * channels, first_tap))
+    return taps
+
+
+def products(wide, turned, box, taps):
+    size_x, all_y, size_z, channels = box
+    for level in range(5):
+        start = EDGE + level - 2
+        for pair in ((0, 1), (2, 3)):
+            patches, spots = [], []
+            for other in pair:
+                first_tap = taps[other][1]
+                number = lax.rem(level + 5 - lax.rem(first_tap, 5), 5)
+                group = (first_tap + number) // 5
+                patch = wide[
+                    pl.ds(group // 5, size_x), pl.ds(lax.rem(group, 5), all_y), start : start + size_z
+                ]
+                patches.append(patch.astype(BF16).reshape(-1, channels))
+                spots.append(pl.ds(pl.multiple_of(number * channels, channels), channels))
             result = jnp.dot(
-                turned[...], patch.astype(BF16).reshape(-1, channels), preferred_element_type=F32
+                turned[...], jnp.concatenate(patches, axis=1), preferred_element_type=F32
             )
-            product[other, pl.ds(pl.multiple_of(number * channels, channels), channels)] = result.T
-        offset = pl.multiple_of(first_row - first_tap * channels, 16)
+            for n, other in enumerate(pair):
+                yield other, spots[n], result[:, n * channels : (n + 1) * channels]
+
+
+def partial_kernel(spanned, rows, *refs):
+    (own, side, first, corner, second, corner_2,
+     own_z, side_z, first_z, corner_z, second_z, corner_2z, grad, wide) = refs[:14]
+    partial, across, turned = refs[14:]
+    size_x, _, size_z, channels = own_z.shape
+    all_y = grad.shape[1]
+    size_y = all_y // 2
+    gy = lax.axis_index("gy")
+    for at_y, block, block_z, one, two, one_z, two_z in (
+        (gy * size_y, own, own_z, first, second, first_z, second_z),
+        ((1 - gy) * size_y, side, side_z, corner, corner_2, corner_z, corner_2z),
+    ):
+        below = below_and_above(one[:2], two[:2])[0]
+        below_z = below_and_above(one_z[:2], two_z[:2])[0]
+        for at_x, main, edge in (
+            (2, block_z[:size_x], block[:size_x]),
+            (0, below_z, below),
+        ):
+            spot = (pl.ds(at_x, main.shape[0]), pl.ds(2 + at_y, size_y))
+            across[spot + (pl.ds(EDGE, size_z),)] = main.astype(F32)
+            z_edges(across, spot, edge, size_z, 1)
+    blank = jnp.zeros((size_x + 2, 2) + across.shape[2:], F32)
+    across[:, :2] = blank
+    across[:, 2 + all_y :] = blank
+    turned[...] = grad[:size_x].reshape(-1, channels).T
+    box = (size_x, all_y, size_z, channels)
+    for other, spot, value in products(wide, turned, box, share_taps(rows, channels, spanned)):
+        partial[other, spot] = value
+
+
+def share_kernel(spanned, voxels, partial, across, grad_z, mine, later, message, turned, product):
+    rows, channels = mine.shape
+    size_x = across.shape[0] - 2
+    all_y, size_z = grad_z.shape[1:3]
+    turned[...] = grad_z[:size_x].reshape(-1, channels).T
+    taps = share_taps(rows, channels, spanned)
+    for other, spot, value in products(across, turned, (size_x, all_y, size_z, channels), taps):
+        product[other, spot] = (partial[other, spot] + value).T
+    for other in range(4):
+        offset = pl.multiple_of(taps[other][0], 16)
         share = product[other, pl.ds(offset, rows)] * (1.0 / voxels)
         if other == 0:
             mine[...] = share
@@ -406,18 +448,26 @@
         shifted[:, :, :, number * channels : (number + 1) * channels] = wide[
             :, pl.ds(gy * size_y, size_y + 4), start : start + size_z, :
         ].astype(BF16)
-    total = jnp.zeros((voxels, channels), F32)
-    for along_x, along_y, _, count, first_tap in tap_groups():
+
+    def transposed(first_x, layers, first_y, lines, taps, count):
         patch = shifted[
-            -along_x : -along_x + size_x,
-            2 - along_y : 2 - along_y + size_y,
-            :,
-            : count * channels,
+            first_x : first_x + layers, first_y : first_y + lines, :, : count * channels
         ].reshape(-1, count * channels)
-        weights = jnp.concatenate([kernel[first_tap + k] for k in range(count)], axis=1)
-        total = total + lax.dot_general(
+        rows = [jnp.concatenate([kernel[tap + k] for k in range(count)], axis=1) for tap in taps]
+        weights = jnp.concatenate(rows, axis=0) if len(rows) > 1 else rows[0]
+        out = lax.dot_general(
             patch, weights, (((1,), (1,)), ((), ())), preferred_element_type=F32
         )
+        return out.reshape(layers, lines, size_z, len(taps) * channels)
+
+    total = jnp.zeros((size_x, size_y, size_z, channels), F32)
+    for along_y in range(5):
+        pair = transposed(1, size_x + 1, 4 - along_y, size_y, (5 * along_y, 25 + 5 * along_y), 5)
+        total = total + pair[1:, :, :, :channels] + pair[:-1, :, :, channels:]
+    pair = transposed(0, size_x, 3, size_y + 1, (50, 55), 5)
+    total = total + pair[:, 1:, :, :channels] + pair[:, :-1, :, channels:]
+    total = total + transposed(0, size_x, 2, size_y, (60,), 2)
+    total = total.reshape(voxels, channels)
     occupied = jnp.where(block[size_x:].astype(F32).reshape(voxels, channels) > 0.0, 1.0, 0.0)
     latent_grad = occupied * (total + rest[...].reshape(voxels, channels))
     inv_root = root[...]
@@ -491,46 +541,49 @@
     )
     middle = lambda x, z: (3 - x, z) if x in (1, 2) else (x, 1 - z)
     side = flipped(across_y, "gy")
+    corner = exchanged(first_x, ("gx", "gy"), lambda x, y: (x ^ 1, 1 - y))
     first = exchanged(first_x, "gx", lambda x: (x ^ 1,))
-    second = exchanged(second_x, ("gx", "gz"), middle)
-    corner = exchanged(first_x, ("gx", "gy"), lambda x, y: (x ^ 1, 1 - y))
     corner_2 = exchanged(
         second_x, ("gx", "gy", "gz"), lambda x, y, z: (3 - x, 1 - y, z) if x in (1, 2) else (x, y, 1 - z)
     )
+    second = exchanged(second_x, ("gx", "gz"), middle)
     sent = (side, first, corner, second, corner_2)
     around = (across_y,) + sent + tuple(flipped(part, "gz") for part in (latent,) + sent)
     wide_y = 2 * size_y + 4
     wide_z = size_z + 2 * EDGE
-    grad, rest, kept_kernel = call(
+    kept_kernel, = call(
+        load_kernel, [pltpu.VMEM(kernel.shape, BF16)], [pltpu.SemaphoreType.DMA((4,))], (kernel,), (0,)
+    )
+    grad, rest, wide = call(
         mean_kernel,
         [
             pltpu.VMEM((size_x + 2, 2 * size_y, size_z, channels), BF16),
             pltpu.VMEM(shape, F32),
-            pltpu.VMEM(kernel.shape, BF16),
+            pltpu.VMEM((size_x + 4, wide_y, wide_z, channels), F32),
         ],
         [
-            pltpu.VMEM((size_x + 4, wide_y, wide_z, channels), F32),
             pltpu.VMEM((size_x + 4, wide_y, size_z, 5 * channels), BF16),
             pltpu.VMEM((size_x + 2, 2 * size_y, size_z, channels), F32),
             pltpu.VMEM((size_x, 2 * size_y, size_z, channels), F32),
-            pltpu.SemaphoreType.DMA,
         ],
-        around + (kernel,),
-        (12,),
+        around + (kept_kernel,),
     )
     grad_z = flipped(grad, "gz")
     rows = 62 * channels // 16
     spanned = 5
+    turned = pltpu.VMEM((channels, 2 * voxels), BF16)
+    pieces = (4, spanned * channels, channels)
+    partial, across = call(
+        functools.partial(partial_kernel, spanned, rows),
+        [pltpu.VMEM(pieces, F32), pltpu.VMEM((size_x + 2, wide_y, wide_z, channels), F32)],
+        [turned],
+        around + (grad, wide),
+    )
     mine, later, message = call(
         functools.partial(share_kernel, spanned, voxels),
         [pltpu.VMEM((rows, channels), F32)] * 2 + [pltpu.VMEM((2 * rows, channels), BF16)],
-        [
-            pltpu.VMEM((size_x + 2, wide_y, 2 * size_z + 2 * EDGE, channels), F32),
-            pltpu.VMEM((size_x, 2 * size_y, 2 * size_z, channels), BF16),
-            pltpu.VMEM((channels, 4 * voxels), BF16),
-            pltpu.VMEM((4, spanned * channels, channels), F32),
-        ],
-        around + (grad, grad_z),
+        [turned, pltpu.VMEM(pieces, F32)],
+        (partial, across, grad_z),
     )
     halves = exchanged(message, "gx", lambda x: (x ^ 1,))
     grad_features, sums, others = call(
@@ -567,7 +620,7 @@
 
 
 def solution(mesh):
-    return jax.shard_map(
+    step = jax.shard_map(
         chosen,
         mesh=mesh,
         in_specs=(
@@ -586,3 +639,6 @@
         ),
         check_vma=False,
     )
+    if tuple(mesh.shape[axis] for axis in ("gx", "gy", "gz")) != (4, 2, 2):
+        return step
+    return step

time: 45.1 us -> 43.3 us (0.960)
  waiting for transfers between devices: 19.5 us -> 17.2 us
  starting transfers between devices: 14.4 us -> 15 us
    ppermute x19, waiting for transfers between devices: 19.5 us -> 17.2 us  [exchanged(): return lax.ppermute(value, names if len(names) > 1 else names[0], pairs)]
    ppermute x19, starting transfers between devices: 14.4 us -> 15 us  [exchanged(): return lax.ppermute(value, names if len(names) > 1 else names[0], pairs)]
    pallas_call x5 -> x7, Pallas kernels: 10.3 us -> 10.1 us  [call(): pl.pallas_call(body, out_shape=outs, in_specs=[pl.BlockSpec(memory_space=...]
  transfers between devices with their start and end apart: 19 -> 19, of which waited for: 13 -> 8; matrix products, arithmetic and copies ran while one was open for 0% -> 0% of each run, Pallas kernels for 5% -> 10%
where the time goes in v5:
time: 43.3 us; the launch traced here: 43.1 us
  waiting for transfers between devices  17.2 us (40%)
  starting transfers between devices  15 us (35%)
  Pallas kernels  10.1 us (23%)
  between operations  0.74 us (2%)
    ppermute x19, waiting for transfers between devices, exchanged(): return lax.ppermute(value, names if len(names) > 1 else names[0], pairs)  17.2 us
    ppermute x19, starting transfers between devices, exchanged(): return lax.ppermute(value, names if len(names) > 1 else names[0], pairs)  15 us
    pallas_call x7, Pallas kernels, call(): pl.pallas_call(body, out_shape=outs, in_specs=[pl.BlockSpec(memory_space=...  10.1 us
  transfers between devices with their start and end apart: 19, of which 8 were waited for; matrix products, arithmetic and copies ran while one was open for 0% of the time, Pallas kernels for 10%

profile of v5, /device:TPU:0, one launch (start us, length us, event | category | flops | bytes accessed | tf_op | source)
XLA Modules:
  0.0 43.1 jit_solution(6919584613169348268)
XLA Ops:
  0.6 1.3 %shard_map.93 = (bf16[4,4,16,128]{3,2,1,0:T(8,128)(2,1)S(1)}, bf16[8,4,16,128]{3,2,1,0:T(8,128)(2,1)S(1)}, bf16[4,4,16,128]{3,2,1,0:T(8,128)(2,1)S(1)}, bf16[4,4...) custom-call(bf16[4,4,16,128]{3,2,1,0:T(8,128)(2,1)} %far_features.1,, ...), custom_call_target="tpu_custom_call" | custom-call | tf_op jit(solution)/shard_map/pallas_call | solution.py:507
  1.9 3.0 %collective-permute-start = (bf16[8,4,16,128]{3,2,1,0:T(8,128)(2,1)S(1)}, bf16[8,4,16,128]{3,2,1,0:T(8,128)(2,1)S(1)}, u32[]{:S(2)}, u32[]{:S(2)}) collective-permute-start(bf16[8,4,16,128]{3,2,1,0:T(8,128)(2,1)S(1)} %get-tuple-element.25.own.block.refs_0_), channel_id=1, source_target_pairs={{0,2},{2,0},{1,3},{3,1},{4,6},{6,4},{5,7},{7,5},{8,10},{10,8},{9,1... | collective-permute-start | bytes 393224 | tf_op jit(solution)/shard_map/ppermute | solution.py:196
  4.9 1.6 %collective-permute-start.1 = (bf16[4,4,16,128]{3,2,1,0:T(8,128)(2,1)S(1)}, bf16[4,4,16,128]{3,2,1,0:T(8,128)(2,1)S(1)}, u32[]{:S(2)}, u32[]{:S(2)}) collective-permute-start(bf16[4,4,16,128]{3,2,1,0:T(8,128)(2,1)S(1)} %get-tuple-element.26), channel_id=1, source_target_pairs={{0,4},{4,0},{8,12},{12,8},{1,5},{5,1},{9,13},{13,9},{2,6},{6,2},{1... | collective-permute-start | bytes 196616 | tf_op jit(solution)/shard_map/ppermute | solution.py:196
  6.5 0.0 collective-permute-start.2
  6.5 0.0 collective-permute-start.3
  6.5 0.5 %collective-permute-start.4 = (bf16[4,4,16,128]{3,2,1,0:T(8,128)(2,1)S(1)}, bf16[4,4,16,128]{3,2,1,0:T(8,128)(2,1)S(1)}, u32[]{:S(2)}, u32[]{:S(2)}) collective-permute-start(bf16[4,4,16,128]{3,2,1,0:T(8,128)(2,1)S(1)} %get-tuple-element.27), channel_id=1, source_target_pairs={{0,1},{1,0},{2,3},{3,2},{4,10},{5,11},{6,8},{7,9},{8,6},{9,7},{10,... | collective-permute-start | bytes 196616 | tf_op jit(solution)/shard_map/ppermute | solution.py:196
  7.0 2.7 %collective-permute-done.1.first.refs_2_ = bf16[4,4,16,128]{3,2,1,0:T(8,128)(2,1)S(1)} collective-permute-done((bf16[4,4,16,128]{3,2,1,0:T(8,128)(2,1)S(1)}, bf16[4,4,16,128]{3,2,1,0:T(8,128)(2,1)S(1)}, u32[]{:S(2)}, u32[]{:S(2)}) %collective-permute-start.1) | collective-permute-done | bytes 65568 | tf_op jit(solution)/shard_map/ppermute | solution.py:196
  9.8 0.0 collective-permute-start.5
  9.8 0.0 collective-permute-done.side.refs_1_
  9.8 0.5 %collective-permute-start.6 = (bf16[8,4,16,128]{3,2,1,0:T(8,128)(2,1)S(1)}, bf16[8,4,16,128]{3,2,1,0:T(8,128)(2,1)S(1)}, u32[]{:S(2)}, u32[]{:S(2)}) collective-permute-start(bf16[8,4,16,128]{3,2,1,0:T(8,128)(2,1)S(1)} %collective-permute-done.side.refs_1_), channel_id=1, source_target_pairs={{0,1},{1,0},{2,3},{3,2},{4,5},{5,4},{6,7},{7,6},{8,9},{9,8},{10,11... | collective-permute-start | bytes 393224 | tf_op jit(solution)/shard_map/ppermute | solution.py:196
  10.3 1.4 %collective-permute-done.2.corner.refs_3_ = bf16[4,4,16,128]{3,2,1,0:T(8,128)(2,1)S(1)} collective-permute-done((bf16[4,4,16,128]{3,2,1,0:T(8,128)(2,1)S(1)}, bf16[4,4,16,128]{3,2,1,0:T(8,128)(2,1)S(1)}, u32[]{:S(2)}, u32[]{:S(2)}) %collective-permute-start.2) | collective-permute-done | bytes 65568 | tf_op jit(solution)/shard_map/ppermute | solution.py:196
  11.7 0.5 %collective-permute-start.8 = (bf16[4,4,16,128]{3,2,1,0:T(8,128)(2,1)S(1)}, bf16[4,4,16,128]{3,2,1,0:T(8,128)(2,1)S(1)}, u32[]{:S(2)}, u32[]{:S(2)}) collective-permute-start(bf16[4,4,16,128]{3,2,1,0:T(8,128)(2,1)S(1)} %collective-permute-done.2.corner.refs_3_), channel_id=1, source_target_pairs={{0,1},{1,0},{2,3},{3,2},{4,5},{5,4},{6,7},{7,6},{8,9},{9,8},{10,11... | collective-permute-start | bytes 196616 | tf_op jit(solution)/shard_map/ppermute | solution.py:196
  12.2 0.1 collective-permute-start.9
  12.3 0.4 %collective-permute-start.10 = (bf16[4,4,16,128]{3,2,1,0:T(8,128)(2,1)S(1)}, bf16[4,4,16,128]{3,2,1,0:T(8,128)(2,1)S(1)}, u32[]{:S(2)}, u32[]{:S(2)}) collective-permute-start(bf16[4,4,16,128]{3,2,1,0:T(8,128)(2,1)S(1)} %collective-permute-done.4.corner_2.refs_5_), channel_id=1, source_target_pairs={{0,1},{1,0},{2,3},{3,2},{4,5},{5,4},{6,7},{7,6},{8,9},{9,8},{10,11... | collective-permute-start | bytes 196616 | tf_op jit(solution)/shard_map/ppermute | solution.py:196
  12.7 1.5 %shard_map.94.kernel = bf16[62,128,128]{2,1,0:T(8,128)(2,1)S(1)} custom-call(bf16[62,128,128]{2,1,0:T(8,128)(2,1)} %far.1), custom_call_target="tpu_custom_call" | custom-call | tf_op jit(solution)/shard_map/pallas_call | solution.py:507
  14.3 2.7 %shard_map.95 = (bf16[6,8,16,128]{3,2,1,0:T(8,128)(2,1)S(1)}, f32[4,4,16,128]{3,2,1,0:T(8,128)S(1)}, f32[8,12,32,128]{3,2,1,0:T(8,128)S(1)}) custom-call(bf16[8,4,16,128]{3,2,1,0:T(8,128)(2,1)S(1)} %get-tuple-element.25.own.block.refs_0_, bf16[8,4,16,128]{3,2,1,0:T(8,128)(2,1)S(1)} %collective-permute-done.side.refs_1_, ...), custom_call_target="tpu_custom_call" | custom-call | tf_op jit(solution)/shard_map/pallas_call | solution.py:507
  17.0 0.1 collective-permute-start.11
  17.1 0.9 %shard_map.97 = (f32[4,640,128]{2,1,0:T(8,128)S(1)}, f32[6,12,32,128]{3,2,1,0:T(8,128)S(1)}) custom-call(bf16[8,4,16,128]{3,2,1,0:T(8,128)(2,1)S(1)} %get-tuple-element.25.own.block.refs_0_, bf16[8,4,16,128]{3,2,1,0:T(8,128)(2,1)S(1)} %collective-permute-done.side.refs_1_, bf16[4,4,16,128]{3,2,1,0:T(8,128)(2,1)S(1)} %collective-permute-done.1.first.refs_2_, ...), custom_call_target="tpu_custom_call" | custom-call | tf_op jit(solution)/shard_map/pallas_call | solution.py:507
  18.0 0.5 %collective-permute-done.11.grad_z = bf16[6,8,16,128]{3,2,1,0:T(8,128)(2,1)S(1)} collective-permute-done((bf16[6,8,16,128]{3,2,1,0:T(8,128)(2,1)S(1)}, bf16[6,8,16,128]{3,2,1,0:T(8,128)(2,1)S(1)}, u32[]{:S(2)}, u32[]{:S(2)}) %collective-permute-start.11) | collective-permute-done | bytes 196640 | tf_op jit(solution)/shard_map/ppermute | solution.py:196
  18.5 0.9 %shard_map.98 = (f32[496,128]{1,0:T(8,128)S(1)}, f32[496,128]{1,0:T(8,128)S(1)}, bf16[992,128]{1,0:T(8,128)(2,1)S(1)}) custom-call(f32[4,640,128]{2,1,0:T(8,128)S(1)} %get-tuple-element.38.partial, f32[6,12,32,128]{3,2,1,0:T(8,128)S(1)} %get-tuple-element.39.across, bf16[6,8,16,128]{3,2,1,0:T(8,128)(2,1)S(1)} %collective-permute-done.11.grad_z), custom_call_target="tpu_custom_call" | custom-call | tf_op jit(solution)/shard_map/pallas_call | solution.py:507
  19.4 3.1 %collective-permute-start.17 = (bf16[992,128]{1,0:T(8,128)(2,1)S(1)}, bf16[992,128]{1,0:T(8,128)(2,1)S(1)}, u32[]{:S(2)}, u32[]{:S(2)}) collective-permute-start(bf16[992,128]{1,0:T(8,128)(2,1)S(1)} %get-tuple-element.41), channel_id=1, source_target_pairs={{0,4},{4,0},{8,12},{12,8},{1,5},{5,1},{9,13},{13,9},{2,6},{6,2},{1... | collective-permute-start | bytes 761864 | tf_op jit(solution)/shard_map/ppermute | solution.py:196
  22.5 2.1 %shard_map.96 = (bf16[4,4,16,128]{3,2,1,0:T(8,128)(2,1)}, f32[72,128]{1,0:T(8,128)S(1)}, f32[72,128]{1,0:T(8,128)S(1)}) custom-call(bf16[6,8,16,128]{3,2,1,0:T(8,128)(2,1)S(1)} %get-tuple-element.29.grad.refs_12_, bf16[6,8,16,128]{3,2,1,0:T(8,128)(2,1)S(1)} %collective-permute-done.11.grad_z, bf16[62,128,128]{2,1,0:T(8,128)(2,1)S(1)} %shard_map.94.kernel, ...), custom_call_target="tpu_custom_call" | custom-call | tf_op jit(solution)/shard_map/pallas_call | solution.py:507
  24.6 1.2 %collective-permute-done.12 = f32[72,128]{1,0:T(8,128)S(1)} collective-permute-done((f32[72,128]{1,0:T(8,128)S(1)}, f32[72,128]{1,0:T(8,128)S(1)}, u32[]{:S(2)}, u32[]{:S(2)}) %collective-permute-start.12) | collective-permute-done | bytes 36896 | tf_op jit(solution)/shard_map/ppermute | solution.py:196
  25.8 1.5 %collective-permute-start.13 = (f32[72,128]{1,0:T(8,128)S(1)}, f32[72,128]{1,0:T(8,128)S(1)}, u32[]{:S(2)}, u32[]{:S(2)}) collective-permute-start(f32[72,128]{1,0:T(8,128)S(1)} %add.15), channel_id=1, source_target_pairs={{0,2},{2,0},{1,3},{3,1},{4,6},{6,4},{5,7},{7,5},{8,10},{10,8},{9,1... | collective-permute-start | bytes 110600 | tf_op jit(solution)/shard_map/ppermute | solution.py:196
  27.4 1.6 %collective-permute-done.17.halves = bf16[992,128]{1,0:T(8,128)(2,1)S(1)} collective-permute-done((bf16[992,128]{1,0:T(8,128)(2,1)S(1)}, bf16[992,128]{1,0:T(8,128)(2,1)S(1)}, u32[]{:S(2)}, u32[]{:S(2)}) %collective-permute-start.17) | collective-permute-done | bytes 253984 | tf_op jit(solution)/shard_map/ppermute | solution.py:196
  29.0 1.7 %collective-permute-start.18 = (bf16[496,128]{1,0:T(8,128)(2,1)S(1)}, bf16[496,128]{1,0:T(8,128)(2,1)S(1)}, u32[]{:S(2)}, u32[]{:S(2)}) collective-permute-start(bf16[496,128]{1,0:T(8,128)(2,1)S(1)} %add_convert_fusion), channel_id=1, source_target_pairs={{0,12},{4,8},{8,4},{12,0},{1,13},{5,9},{9,5},{13,1},{2,14},{6,10},... | collective-permute-start | bytes 380936 | tf_op jit(solution)/shard_map/ppermute | solution.py:196
  30.7 0.9 %collective-permute-start.14 = (f32[72,128]{1,0:T(8,128)S(1)}, f32[72,128]{1,0:T(8,128)S(1)}, u32[]{:S(2)}, u32[]{:S(2)}) collective-permute-start(f32[72,128]{1,0:T(8,128)S(1)} %add.16), channel_id=1, source_target_pairs={{0,4},{4,0},{8,12},{12,8},{1,5},{5,1},{9,13},{13,9},{2,6},{6,2},{1... | collective-permute-start | bytes 110600 | tf_op jit(solution)/shard_map/ppermute | solution.py:196
  31.6 4.6 %collective-permute-done.14 = f32[72,128]{1,0:T(8,128)S(1)} collective-permute-done((f32[72,128]{1,0:T(8,128)S(1)}, f32[72,128]{1,0:T(8,128)S(1)}, u32[]{:S(2)}, u32[]{:S(2)}) %collective-permute-start.14) | collective-permute-done | bytes 36896 | tf_op jit(solution)/shard_map/ppermute | solution.py:196
  36.2 0.9 %collective-permute-start.15 = (f32[72,128]{1,0:T(8,128)S(1)}, f32[72,128]{1,0:T(8,128)S(1)}, u32[]{:S(2)}, u32[]{:S(2)}) collective-permute-start(f32[72,128]{1,0:T(8,128)S(1)} %add.17), channel_id=1, source_target_pairs={{0,8},{4,12},{8,0},{12,4},{1,9},{5,13},{9,1},{13,5},{2,10},{6,14},... | collective-permute-start | bytes 110600 | tf_op jit(solution)/shard_map/ppermute | solution.py:196
  37.1 4.0 %collective-permute-done.15 = f32[72,128]{1,0:T(8,128)S(1)} collective-permute-done((f32[72,128]{1,0:T(8,128)S(1)}, f32[72,128]{1,0:T(8,128)S(1)}, u32[]{:S(2)}, u32[]{:S(2)}) %collective-permute-start.15) | collective-permute-done | bytes 36896 | tf_op jit(solution)/shard_map/ppermute | solution.py:196
  41.1 1.2 %collective-permute-done.16.theirs = f32[72,128]{1,0:T(8,128)S(1)} collective-permute-done((f32[72,128]{1,0:T(8,128)S(1)}, f32[72,128]{1,0:T(8,128)S(1)}, u32[]{:S(2)}, u32[]{:S(2)}) %collective-permute-start.16) | collective-permute-done | bytes 36896 | tf_op jit(solution)/shard_map/ppermute | solution.py:196
  42.3 0.8 %shard_map.99 = (f32[128,128]{1,0:T(8,128)}, f32[1,128]{1,0:T(1,128)}, f32[496,128]{1,0:T(8,128)}) custom-call(f32[72,128]{1,0:T(8,128)S(1)} %add.18.mine, f32[72,128]{1,0:T(8,128)S(1)} %collective-permute-done.16.theirs, f32[496,128]{1,0:T(8,128)S(1)} %get-tuple-element.40.kept, bf16[992,128]{1,0:T(8,128)(2,1)S(1)} %collective-permute-done.17.halves, ...), custom_call_target="tpu_custom_call" | custom-call | tf_op jit(solution)/shard_map/pallas_call | solution.py:507
  (18 shorter events, 0.1 us)
Async XLA Ops:
  1.9 7.9 %collective-permute-start = (bf16[8,4,16,128]{3,2,1,0:T(8,128)(2,1)S(1)}, bf16[8,4,16,128]{3,2,1,0:T(8,128)(2,1)S(1)}, u32[]{:S(2)}, u32[]{:S(2)}) collective-permute-start(bf16[8,4,16,128]{3,2,1,0:T(8,128)(2,1)S(1)} %get-tuple-element.25.own.block.refs_0_), channel_id=1, source_target_pairs={{0,2},{2,0},{1,3},{3,1},{4,6},{6,4},{5,7},{7,5},{8,10},{10,8},{9,1... | collective-permute-start | bytes 393224 | tf_op jit(solution)/shard_map/ppermute | solution.py:196
  4.9 4.8 %collective-permute-start.1 = (bf16[4,4,16,128]{3,2,1,0:T(8,128)(2,1)S(1)}, bf16[4,4,16,128]{3,2,1,0:T(8,128)(2,1)S(1)}, u32[]{:S(2)}, u32[]{:S(2)}) collective-permute-start(bf16[4,4,16,128]{3,2,1,0:T(8,128)(2,1)S(1)} %get-tuple-element.26), channel_id=1, source_target_pairs={{0,4},{4,0},{8,12},{12,8},{1,5},{5,1},{9,13},{13,9},{2,6},{6,2},{1... | collective-permute-start | bytes 196616 | tf_op jit(solution)/shard_map/ppermute | solution.py:196
  6.5 5.2 %collective-permute-start.2 = (bf16[4,4,16,128]{3,2,1,0:T(8,128)(2,1)S(1)}, bf16[4,4,16,128]{3,2,1,0:T(8,128)(2,1)S(1)}, u32[]{:S(2)}, u32[]{:S(2)}) collective-permute-start(bf16[4,4,16,128]{3,2,1,0:T(8,128)(2,1)S(1)} %get-tuple-element.26), channel_id=1, source_target_pairs={{0,6},{2,4},{4,2},{6,0},{8,14},{10,12},{12,10},{14,8},{1,7},{3,5},... | collective-permute-start | bytes 196616 | tf_op jit(solution)/shard_map/ppermute | solution.py:196
  6.5 5.2 %collective-permute-start.3 = (bf16[4,4,16,128]{3,2,1,0:T(8,128)(2,1)S(1)}, bf16[4,4,16,128]{3,2,1,0:T(8,128)(2,1)S(1)}, u32[]{:S(2)}, u32[]{:S(2)}) collective-permute-start(bf16[4,4,16,128]{3,2,1,0:T(8,128)(2,1)S(1)} %get-tuple-element.27), channel_id=1, source_target_pairs={{0,1},{1,0},{4,8},{5,9},{8,4},{9,5},{12,13},{13,12},{2,3},{3,2},{6... | collective-permute-start | bytes 196616 | tf_op jit(solution)/shard_map/ppermute | solution.py:196
  6.5 5.7 %collective-permute-start.4 = (bf16[4,4,16,128]{3,2,1,0:T(8,128)(2,1)S(1)}, bf16[4,4,16,128]{3,2,1,0:T(8,128)(2,1)S(1)}, u32[]{:S(2)}, u32[]{:S(2)}) collective-permute-start(bf16[4,4,16,128]{3,2,1,0:T(8,128)(2,1)S(1)} %get-tuple-element.27), channel_id=1, source_target_pairs={{0,1},{1,0},{2,3},{3,2},{4,10},{5,11},{6,8},{7,9},{8,6},{9,7},{10,... | collective-permute-start | bytes 196616 | tf_op jit(solution)/shard_map/ppermute | solution.py:196
  9.8 2.5 %collective-permute-start.5 = (bf16[4,4,16,128]{3,2,1,0:T(8,128)(2,1)S(1)}, bf16[4,4,16,128]{3,2,1,0:T(8,128)(2,1)S(1)}, u32[]{:S(2)}, u32[]{:S(2)}) collective-permute-start(bf16[4,4,16,128]{3,2,1,0:T(8,128)(2,1)S(1)} %get-tuple-element.28), channel_id=1, source_target_pairs={{0,1},{1,0},{2,3},{3,2},{4,5},{5,4},{6,7},{7,6},{8,9},{9,8},{10,11... | collective-permute-start | bytes 196616 | tf_op jit(solution)/shard_map/ppermute | solution.py:196
  9.8 4.5 %collective-permute-start.6 = (bf16[8,4,16,128]{3,2,1,0:T(8,128)(2,1)S(1)}, bf16[8,4,16,128]{3,2,1,0:T(8,128)(2,1)S(1)}, u32[]{:S(2)}, u32[]{:S(2)}) collective-permute-start(bf16[8,4,16,128]{3,2,1,0:T(8,128)(2,1)S(1)} %collective-permute-done.side.refs_1_), channel_id=1, source_target_pairs={{0,1},{1,0},{2,3},{3,2},{4,5},{5,4},{6,7},{7,6},{8,9},{9,8},{10,11... | collective-permute-start | bytes 393224 | tf_op jit(solution)/shard_map/ppermute | solution.py:196
  11.7 2.6 %collective-permute-start.7 = (bf16[4,4,16,128]{3,2,1,0:T(8,128)(2,1)S(1)}, bf16[4,4,16,128]{3,2,1,0:T(8,128)(2,1)S(1)}, u32[]{:S(2)}, u32[]{:S(2)}) collective-permute-start(bf16[4,4,16,128]{3,2,1,0:T(8,128)(2,1)S(1)} %collective-permute-done.1.first.refs_2_), channel_id=1, source_target_pairs={{0,1},{1,0},{2,3},{3,2},{4,5},{5,4},{6,7},{7,6},{8,9},{9,8},{10,11... | collective-permute-start | bytes 196616 | tf_op jit(solution)/shard_map/ppermute | solution.py:196
  11.7 2.6 %collective-permute-start.8 = (bf16[4,4,16,128]{3,2,1,0:T(8,128)(2,1)S(1)}, bf16[4,4,16,128]{3,2,1,0:T(8,128)(2,1)S(1)}, u32[]{:S(2)}, u32[]{:S(2)}) collective-permute-start(bf16[4,4,16,128]{3,2,1,0:T(8,128)(2,1)S(1)} %collective-permute-done.2.corner.refs_3_), channel_id=1, source_target_pairs={{0,1},{1,0},{2,3},{3,2},{4,5},{5,4},{6,7},{7,6},{8,9},{9,8},{10,11... | collective-permute-start | bytes 196616 | tf_op jit(solution)/shard_map/ppermute | solution.py:196
  12.2 2.1 %collective-permute-start.9 = (bf16[4,4,16,128]{3,2,1,0:T(8,128)(2,1)S(1)}, bf16[4,4,16,128]{3,2,1,0:T(8,128)(2,1)S(1)}, u32[]{:S(2)}, u32[]{:S(2)}) collective-permute-start(bf16[4,4,16,128]{3,2,1,0:T(8,128)(2,1)S(1)} %collective-permute-done.3.second.refs_4_), channel_id=1, source_target_pairs={{0,1},{1,0},{2,3},{3,2},{4,5},{5,4},{6,7},{7,6},{8,9},{9,8},{10,11... | collective-permute-start | bytes 196616 | tf_op jit(solution)/shard_map/ppermute | solution.py:196
  12.3 2.0 %collective-permute-start.10 = (bf16[4,4,16,128]{3,2,1,0:T(8,128)(2,1)S(1)}, bf16[4,4,16,128]{3,2,1,0:T(8,128)(2,1)S(1)}, u32[]{:S(2)}, u32[]{:S(2)}) collective-permute-start(bf16[4,4,16,128]{3,2,1,0:T(8,128)(2,1)S(1)} %collective-permute-done.4.corner_2.refs_5_), channel_id=1, source_target_pairs={{0,1},{1,0},{2,3},{3,2},{4,5},{5,4},{6,7},{7,6},{8,9},{9,8},{10,11... | collective-permute-start | bytes 196616 | tf_op jit(solution)/shard_map/ppermute | solution.py:196
  17.0 1.5 %collective-permute-start.11 = (bf16[6,8,16,128]{3,2,1,0:T(8,128)(2,1)S(1)}, bf16[6,8,16,128]{3,2,1,0:T(8,128)(2,1)S(1)}, u32[]{:S(2)}, u32[]{:S(2)}) collective-permute-start(bf16[6,8,16,128]{3,2,1,0:T(8,128)(2,1)S(1)} %get-tuple-element.29.grad.refs_12_), channel_id=1, source_target_pairs={{0,1},{1,0},{2,3},{3,2},{4,5},{5,4},{6,7},{7,6},{8,9},{9,8},{10,11... | collective-permute-start | bytes 589832 | tf_op jit(solution)/shard_map/ppermute | solution.py:196
  19.4 9.6 %collective-permute-start.17 = (bf16[992,128]{1,0:T(8,128)(2,1)S(1)}, bf16[992,128]{1,0:T(8,128)(2,1)S(1)}, u32[]{:S(2)}, u32[]{:S(2)}) collective-permute-start(bf16[992,128]{1,0:T(8,128)(2,1)S(1)} %get-tuple-element.41), channel_id=1, source_target_pairs={{0,4},{4,0},{8,12},{12,8},{1,5},{5,1},{9,13},{13,9},{2,6},{6,2},{1... | collective-permute-start | bytes 761864 | tf_op jit(solution)/shard_map/ppermute | solution.py:196
  24.6 1.2 %collective-permute-start.12 = (f32[72,128]{1,0:T(8,128)S(1)}, f32[72,128]{1,0:T(8,128)S(1)}, u32[]{:S(2)}, u32[]{:S(2)}) collective-permute-start(f32[72,128]{1,0:T(8,128)S(1)} %get-tuple-element.36), channel_id=1, source_target_pairs={{0,1},{1,0},{2,3},{3,2},{4,5},{5,4},{6,7},{7,6},{8,9},{9,8},{10,11... | collective-permute-start | bytes 110600 | tf_op jit(solution)/shard_map/ppermute | solution.py:196
  25.8 4.9 %collective-permute-start.13 = (f32[72,128]{1,0:T(8,128)S(1)}, f32[72,128]{1,0:T(8,128)S(1)}, u32[]{:S(2)}, u32[]{:S(2)}) collective-permute-start(f32[72,128]{1,0:T(8,128)S(1)} %add.15), channel_id=1, source_target_pairs={{0,2},{2,0},{1,3},{3,1},{4,6},{6,4},{5,7},{7,5},{8,10},{10,8},{9,1... | collective-permute-start | bytes 110600 | tf_op jit(solution)/shard_map/ppermute | solution.py:196
  29.0 13.3 %collective-permute-start.18 = (bf16[496,128]{1,0:T(8,128)(2,1)S(1)}, bf16[496,128]{1,0:T(8,128)(2,1)S(1)}, u32[]{:S(2)}, u32[]{:S(2)}) collective-permute-start(bf16[496,128]{1,0:T(8,128)(2,1)S(1)} %add_convert_fusion), channel_id=1, source_target_pairs={{0,12},{4,8},{8,4},{12,0},{1,13},{5,9},{9,5},{13,1},{2,14},{6,10},... | collective-permute-start | bytes 380936 | tf_op jit(solution)/shard_map/ppermute | solution.py:196
  30.7 5.5 %collective-permute-start.14 = (f32[72,128]{1,0:T(8,128)S(1)}, f32[72,128]{1,0:T(8,128)S(1)}, u32[]{:S(2)}, u32[]{:S(2)}) collective-permute-start(f32[72,128]{1,0:T(8,128)S(1)} %add.16), channel_id=1, source_target_pairs={{0,4},{4,0},{8,12},{12,8},{1,5},{5,1},{9,13},{13,9},{2,6},{6,2},{1... | collective-permute-start | bytes 110600 | tf_op jit(solution)/shard_map/ppermute | solution.py:196
  36.2 4.9 %collective-permute-start.15 = (f32[72,128]{1,0:T(8,128)S(1)}, f32[72,128]{1,0:T(8,128)S(1)}, u32[]{:S(2)}, u32[]{:S(2)}) collective-permute-start(f32[72,128]{1,0:T(8,128)S(1)} %add.17), channel_id=1, source_target_pairs={{0,8},{4,12},{8,0},{12,4},{1,9},{5,13},{9,1},{13,5},{2,10},{6,14},... | collective-permute-start | bytes 110600 | tf_op jit(solution)/shard_map/ppermute | solution.py:196
  41.1 1.2 %collective-permute-start.16 = (f32[72,128]{1,0:T(8,128)S(1)}, f32[72,128]{1,0:T(8,128)S(1)}, u32[]{:S(2)}, u32[]{:S(2)}) collective-permute-start(f32[72,128]{1,0:T(8,128)S(1)} %add.18.mine), channel_id=1, source_target_pairs={{0,1},{1,0},{2,3},{3,2},{4,5},{5,4},{6,7},{7,6},{8,9},{9,8},{10,11... | collective-permute-start | bytes 110600 | tf_op jit(solution)/shard_map/ppermute | solution.py:196

commit v6 on v5

--- a/solution.py
+++ b/solution.py
@@ -410,7 +410,7 @@
         partial[other, spot] = value
 
 
-def share_kernel(spanned, voxels, partial, across, grad_z, mine, later, message, turned, product):
+def share_kernel(spanned, voxels, partial, across, grad_z, mine, later, ahead, direct, turned, product):
     rows, channels = mine.shape
     size_x = across.shape[0] - 2
     all_y, size_z = grad_z.shape[1:3]
@@ -425,9 +425,10 @@
             mine[...] = share
         elif other == 3:
             later[...] = share
+        elif other == 2:
+            ahead[...] = share.astype(ahead.dtype)
         else:
-            half = (other - 1) * rows
-            message[half : half + rows] = share.astype(message.dtype)
+            direct[...] = share.astype(direct.dtype)
 
 
 def feature_kernel(
@@ -490,9 +491,8 @@
     theirs[half:] = ones
 
 
-def join_kernel(mine, theirs, kept, halves, quarter, gamma, beta, share):
-    rows = share.shape[0]
-    share[...] = kept[...] + halves[:rows].astype(F32) + quarter[...].astype(F32)
+def join_kernel(mine, theirs, kept, direct, quarter, gamma, beta, share):
+    share[...] = kept[...] + direct[...].astype(F32) + quarter[...].astype(F32)
     half = gamma.shape[0] // 2
     first_z = lax.axis_index("gz") == 0
     own, other = mine[:half], theirs[:half]
@@ -548,7 +548,9 @@
     )
     second = exchanged(second_x, ("gx", "gz"), middle)
     sent = (side, first, corner, second, corner_2)
-    around = (across_y,) + sent + tuple(flipped(part, "gz") for part in (latent,) + sent)
+    around = (across_y,) + sent + tuple(
+        flipped(part, "gz") for part in (latent, side[:size_x]) + tuple(part[:2] for part in sent[1:])
+    )
     wide_y = 2 * size_y + 4
     wide_z = size_z + 2 * EDGE
     kept_kernel, = call(
@@ -579,13 +581,14 @@
         [turned],
         around + (grad, wide),
     )
-    mine, later, message = call(
+    mine, later, ahead, direct = call(
         functools.partial(share_kernel, spanned, voxels),
-        [pltpu.VMEM((rows, channels), F32)] * 2 + [pltpu.VMEM((2 * rows, channels), BF16)],
+        [pltpu.VMEM((rows, channels), F32)] * 2 + [pltpu.VMEM((rows, channels), BF16)] * 2,
         [turned, pltpu.VMEM(pieces, F32)],
         (partial, across, grad_z),
     )
-    halves = exchanged(message, "gx", lambda x: (x ^ 1,))
+    ahead = exchanged(ahead, "gx", lambda x: (x ^ 1,))
+    direct = exchanged(direct, "gx", lambda x: (x ^ 1,))
     grad_features, sums, others = call(
         feature_kernel,
         [jax.ShapeDtypeStruct(shape, BF16)] + [pltpu.VMEM((channels // 2 + 8, channels), F32)] * 2,
@@ -596,16 +599,18 @@
         (grad, grad_z, kept_kernel, rest, root, kept_features, kept_gamma, across_y),
     )
     sums = sums + flipped(others, "gz")
-    quarter = exchanged((later + halves[rows:].astype(F32)).astype(BF16), "gx", lambda x: (3 - x,))
+    quarter = exchanged((later + ahead.astype(F32)).astype(BF16), "gx", lambda x: (3 - x,))
     sums = sums + flipped(sums, "gy")
-    sums = sums + exchanged(sums, "gx", lambda x: (x ^ 1,))
-    sums = sums + exchanged(sums, "gx", lambda x: (x ^ 2,))
+    near = exchanged(sums, "gx", lambda x: (x ^ 1,))
+    second_near = exchanged(sums, "gx", lambda x: (x ^ 2,))
+    mirrored = exchanged(sums, "gx", lambda x: (3 - x,))
+    sums = (sums + near) + (second_near + mirrored)
     struct = jax.ShapeDtypeStruct
     grad_gamma, grad_beta, share = call(
         join_kernel,
         [struct((channels, channels), F32), struct((1, channels), F32), struct((rows, channels), F32)],
         [],
-        (sums, flipped(sums, "gz"), mine, halves, quarter),
+        (sums, flipped(sums, "gz"), mine, direct, quarter),
     )
     return grad_features, share.reshape(-1), grad_gamma, grad_beta.reshape(channels)
 

time: 43.3 us -> 41.2 us (0.952)
  waiting for transfers between devices: 17.2 us -> 13.8 us
  starting transfers between devices: 15 us -> 16.3 us
    ppermute x19 -> x21, waiting for transfers between devices: 17.2 us -> 13.8 us  [exchanged(): return lax.ppermute(value, names if len(names) > 1 else names[0], pairs)]
    ppermute x19 -> x21, starting transfers between devices: 15 us -> 16.3 us  [exchanged(): return lax.ppermute(value, names if len(names) > 1 else names[0], pairs)]
  transfers between devices with their start and end apart: 19 -> 21, of which waited for: 8 -> 10; matrix products, arithmetic and copies ran while one was open for 0% -> 0% of each run, Pallas kernels for 10% -> 11%
where the time goes in v6:
time: 41.2 us; the launch traced here: 41 us
  starting transfers between devices  16.3 us (40%)
  waiting for transfers between devices  13.8 us (33%)
  Pallas kernels  10.1 us (25%)
  between operations  0.76 us (2%)
    ppermute x21, starting transfers between devices, exchanged(): return lax.ppermute(value, names if len(names) > 1 else names[0], pairs)  16.3 us
    ppermute x21, waiting for transfers between devices, exchanged(): return lax.ppermute(value, names if len(names) > 1 else names[0], pairs)  13.8 us
    pallas_call x7, Pallas kernels, call(): pl.pallas_call(body, out_shape=outs, in_specs=[pl.BlockSpec(memory_space=...  10.1 us
  transfers between devices with their start and end apart: 21, of which 10 were waited for; matrix products, arithmetic and copies ran while one was open for 0% of the time, Pallas kernels for 11%

profile of v6, /device:TPU:0, one launch (start us, length us, event | category | flops | bytes accessed | tf_op | source)
XLA Modules:
  0.0 41.0 jit_solution(438085923302513361)
XLA Ops:
  0.6 1.3 %shard_map.93 = (bf16[4,4,16,128]{3,2,1,0:T(8,128)(2,1)S(1)}, bf16[8,4,16,128]{3,2,1,0:T(8,128)(2,1)S(1)}, bf16[4,4,16,128]{3,2,1,0:T(8,128)(2,1)S(1)}, bf16[4,4...) custom-call(bf16[4,4,16,128]{3,2,1,0:T(8,128)(2,1)} %far_features.1,, ...), custom_call_target="tpu_custom_call" | custom-call | tf_op jit(solution)/shard_map/pallas_call | solution.py:507
  1.9 3.0 %collective-permute-start = (bf16[8,4,16,128]{3,2,1,0:T(8,128)(2,1)S(1)}, bf16[8,4,16,128]{3,2,1,0:T(8,128)(2,1)S(1)}, u32[]{:S(2)}, u32[]{:S(2)}) collective-permute-start(bf16[8,4,16,128]{3,2,1,0:T(8,128)(2,1)S(1)} %get-tuple-element.26.own.block.refs_0_), channel_id=1, source_target_pairs={{0,2},{2,0},{1,3},{3,1},{4,6},{6,4},{5,7},{7,5},{8,10},{10,8},{9,1... | collective-permute-start | bytes 393224 | tf_op jit(solution)/shard_map/ppermute | solution.py:196
  4.9 1.6 %collective-permute-start.1 = (bf16[4,4,16,128]{3,2,1,0:T(8,128)(2,1)S(1)}, bf16[4,4,16,128]{3,2,1,0:T(8,128)(2,1)S(1)}, u32[]{:S(2)}, u32[]{:S(2)}) collective-permute-start(bf16[4,4,16,128]{3,2,1,0:T(8,128)(2,1)S(1)} %get-tuple-element.27), channel_id=1, source_target_pairs={{0,4},{4,0},{8,12},{12,8},{1,5},{5,1},{9,13},{13,9},{2,6},{6,2},{1... | collective-permute-start | bytes 196616 | tf_op jit(solution)/shard_map/ppermute | solution.py:196
  6.5 0.5 %collective-permute-start.4 = (bf16[4,4,16,128]{3,2,1,0:T(8,128)(2,1)S(1)}, bf16[4,4,16,128]{3,2,1,0:T(8,128)(2,1)S(1)}, u32[]{:S(2)}, u32[]{:S(2)}) collective-permute-start(bf16[4,4,16,128]{3,2,1,0:T(8,128)(2,1)S(1)} %get-tuple-element.28), channel_id=1, source_target_pairs={{0,1},{1,0},{2,3},{3,2},{4,10},{5,11},{6,8},{7,9},{8,6},{9,7},{10,... | collective-permute-start | bytes 196616 | tf_op jit(solution)/shard_map/ppermute | solution.py:196
  7.0 1.4 %collective-permute-done.side.refs_1_ = bf16[8,4,16,128]{3,2,1,0:T(8,128)(2,1)S(1)} collective-permute-done((bf16[8,4,16,128]{3,2,1,0:T(8,128)(2,1)S(1)}, bf16[8,4,16,128]{3,2,1,0:T(8,128)(2,1)S(1)}, u32[]{:S(2)}, u32[]{:S(2)}) %collective-permute-start) | collective-permute-done | bytes 131104 | tf_op jit(solution)/shard_map/ppermute | solution.py:196
  8.4 1.3 %collective-permute-done.1.first.refs_2_ = bf16[4,4,16,128]{3,2,1,0:T(8,128)(2,1)S(1)} collective-permute-done((bf16[4,4,16,128]{3,2,1,0:T(8,128)(2,1)S(1)}, bf16[4,4,16,128]{3,2,1,0:T(8,128)(2,1)S(1)}, u32[]{:S(2)}, u32[]{:S(2)}) %collective-permute-start.1) | collective-permute-done | bytes 65568 | tf_op jit(solution)/shard_map/ppermute | solution.py:196
  9.8 1.9 %collective-permute-done.2.corner.refs_3_ = bf16[4,4,16,128]{3,2,1,0:T(8,128)(2,1)S(1)} collective-permute-done((bf16[4,4,16,128]{3,2,1,0:T(8,128)(2,1)S(1)}, bf16[4,4,16,128]{3,2,1,0:T(8,128)(2,1)S(1)}, u32[]{:S(2)}, u32[]{:S(2)}) %collective-permute-start.2) | collective-permute-done | bytes 65568 | tf_op jit(solution)/shard_map/ppermute | solution.py:196
  11.7 0.5 %collective-permute-start.8 = (bf16[2,4,16,128]{3,2,1,0:T(8,128)(2,1)S(1)}, bf16[2,4,16,128]{3,2,1,0:T(8,128)(2,1)S(1)}, u32[]{:S(2)}, u32[]{:S(2)}) collective-permute-start(bf16[2,4,16,128]{3,2,1,0:T(8,128)(2,1)S(1)} %slice.22), channel_id=1, source_target_pairs={{0,1},{1,0},{2,3},{3,2},{4,5},{5,4},{6,7},{7,6},{8,9},{9,8},{10,11... | collective-permute-start | bytes 98312 | tf_op jit(solution)/shard_map/ppermute | solution.py:196
  12.2 0.1 collective-permute-start.9
  12.3 0.4 collective-permute-start.10
  12.7 1.5 %shard_map.94.kernel = bf16[62,128,128]{2,1,0:T(8,128)(2,1)S(1)} custom-call(bf16[62,128,128]{2,1,0:T(8,128)(2,1)} %far.1), custom_call_target="tpu_custom_call" | custom-call | tf_op jit(solution)/shard_map/pallas_call | solution.py:507
  14.3 2.7 %shard_map.95 = (bf16[6,8,16,128]{3,2,1,0:T(8,128)(2,1)S(1)}, f32[4,4,16,128]{3,2,1,0:T(8,128)S(1)}, f32[8,12,32,128]{3,2,1,0:T(8,128)S(1)}) custom-call(bf16[8,4,16,128]{3,2,1,0:T(8,128)(2,1)S(1)} %get-tuple-element.26.own.block.refs_0_, bf16[8,4,16,128]{3,2,1,0:T(8,128)(2,1)S(1)} %collective-permute-done.side.refs_1_, ...), custom_call_target="tpu_custom_call" | custom-call | tf_op jit(solution)/shard_map/pallas_call | solution.py:507
  17.0 0.2 collective-permute-start.11
  17.2 0.9 %shard_map.97 = (f32[4,640,128]{2,1,0:T(8,128)S(1)}, f32[6,12,32,128]{3,2,1,0:T(8,128)S(1)}) custom-call(bf16[8,4,16,128]{3,2,1,0:T(8,128)(2,1)S(1)} %get-tuple-element.26.own.block.refs_0_, bf16[8,4,16,128]{3,2,1,0:T(8,128)(2,1)S(1)} %collective-permute-done.side.refs_1_, bf16[4,4,16,128]{3,2,1,0:T(8,128)(2,1)S(1)} %collective-permute-done.1.first.refs_2_, ...), custom_call_target="tpu_custom_call" | custom-call | tf_op jit(solution)/shard_map/pallas_call | solution.py:507
  18.1 0.4 %collective-permute-done.11.grad_z = bf16[6,8,16,128]{3,2,1,0:T(8,128)(2,1)S(1)} collective-permute-done((bf16[6,8,16,128]{3,2,1,0:T(8,128)(2,1)S(1)}, bf16[6,8,16,128]{3,2,1,0:T(8,128)(2,1)S(1)}, u32[]{:S(2)}, u32[]{:S(2)}) %collective-permute-start.11) | collective-permute-done | bytes 196640 | tf_op jit(solution)/shard_map/ppermute | solution.py:196
  18.5 0.9 %shard_map.98 = (f32[496,128]{1,0:T(8,128)S(1)}, f32[496,128]{1,0:T(8,128)S(1)}, bf16[496,128]{1,0:T(8,128)(2,1)S(1)}, bf16[496,128]{1,0:T(8,128)(2,1)S(1)}) custom-call(f32[4,640,128]{2,1,0:T(8,128)S(1)} %get-tuple-element.39.partial, f32[6,12,32,128]{3,2,1,0:T(8,128)S(1)} %get-tuple-element.40.across, ...), custom_call_target="tpu_custom_call" | custom-call | tf_op jit(solution)/shard_map/pallas_call | solution.py:507
  19.5 3.1 %collective-permute-start.19 = (bf16[496,128]{1,0:T(8,128)(2,1)S(1)}, bf16[496,128]{1,0:T(8,128)(2,1)S(1)}, u32[]{:S(2)}, u32[]{:S(2)}) collective-permute-start(bf16[496,128]{1,0:T(8,128)(2,1)S(1)} %get-tuple-element.44), channel_id=1, source_target_pairs={{0,4},{4,0},{8,12},{12,8},{1,5},{5,1},{9,13},{13,9},{2,6},{6,2},{1... | collective-permute-start | bytes 380936 | tf_op jit(solution)/shard_map/ppermute | solution.py:196
  22.6 2.1 %shard_map.96 = (bf16[4,4,16,128]{3,2,1,0:T(8,128)(2,1)}, f32[72,128]{1,0:T(8,128)S(1)}, f32[72,128]{1,0:T(8,128)S(1)}) custom-call(bf16[6,8,16,128]{3,2,1,0:T(8,128)(2,1)S(1)} %get-tuple-element.30.grad.refs_12_, bf16[6,8,16,128]{3,2,1,0:T(8,128)(2,1)S(1)} %collective-permute-done.11.grad_z, bf16[62,128,128]{2,1,0:T(8,128)(2,1)S(1)} %shard_map.94.kernel, ...), custom_call_target="tpu_custom_call" | custom-call | tf_op jit(solution)/shard_map/pallas_call | solution.py:507
  24.7 1.2 %collective-permute-done.12 = f32[72,128]{1,0:T(8,128)S(1)} collective-permute-done((f32[72,128]{1,0:T(8,128)S(1)}, f32[72,128]{1,0:T(8,128)S(1)}, u32[]{:S(2)}, u32[]{:S(2)}) %collective-permute-start.12) | collective-permute-done | bytes 36896 | tf_op jit(solution)/shard_map/ppermute | solution.py:196
  25.9 1.5 %collective-permute-start.13 = (f32[72,128]{1,0:T(8,128)S(1)}, f32[72,128]{1,0:T(8,128)S(1)}, u32[]{:S(2)}, u32[]{:S(2)}) collective-permute-start(f32[72,128]{1,0:T(8,128)S(1)} %add.18), channel_id=1, source_target_pairs={{0,2},{2,0},{1,3},{3,1},{4,6},{6,4},{5,7},{7,5},{8,10},{10,8},{9,1... | collective-permute-start | bytes 110600 | tf_op jit(solution)/shard_map/ppermute | solution.py:196
  27.4 0.0 collective-permute-start.18
  27.4 2.4 %collective-permute-done.13 = f32[72,128]{1,0:T(8,128)S(1)} collective-permute-done((f32[72,128]{1,0:T(8,128)S(1)}, f32[72,128]{1,0:T(8,128)S(1)}, u32[]{:S(2)}, u32[]{:S(2)}) %collective-permute-start.13) | collective-permute-done | bytes 36896 | tf_op jit(solution)/shard_map/ppermute | solution.py:196
  29.9 0.2 collective-permute-start.15
  30.0 2.2 %collective-permute-start.16 = (f32[72,128]{1,0:T(8,128)S(1)}, f32[72,128]{1,0:T(8,128)S(1)}, u32[]{:S(2)}, u32[]{:S(2)}) collective-permute-start(f32[72,128]{1,0:T(8,128)S(1)} %add.19), channel_id=1, source_target_pairs={{0,12},{4,8},{8,4},{12,0},{1,13},{5,9},{9,5},{13,1},{2,14},{6,10},... | collective-permute-start | bytes 110600 | tf_op jit(solution)/shard_map/ppermute | solution.py:196
  32.2 1.1 %collective-permute-start.14 = (f32[72,128]{1,0:T(8,128)S(1)}, f32[72,128]{1,0:T(8,128)S(1)}, u32[]{:S(2)}, u32[]{:S(2)}) collective-permute-start(f32[72,128]{1,0:T(8,128)S(1)} %add.19), channel_id=1, source_target_pairs={{0,4},{4,0},{8,12},{12,8},{1,5},{5,1},{9,13},{13,9},{2,6},{6,2},{1... | collective-permute-start | bytes 110600 | tf_op jit(solution)/shard_map/ppermute | solution.py:196
  33.4 1.7 %collective-permute-start.20 = (bf16[496,128]{1,0:T(8,128)(2,1)S(1)}, bf16[496,128]{1,0:T(8,128)(2,1)S(1)}, u32[]{:S(2)}, u32[]{:S(2)}) collective-permute-start(bf16[496,128]{1,0:T(8,128)(2,1)S(1)} %add_convert_fusion), channel_id=1, source_target_pairs={{0,12},{4,8},{8,4},{12,0},{1,13},{5,9},{9,5},{13,1},{2,14},{6,10},... | collective-permute-start | bytes 380936 | tf_op jit(solution)/shard_map/ppermute | solution.py:196
  35.1 0.8 %collective-permute-done.16 = f32[72,128]{1,0:T(8,128)S(1)} collective-permute-done((f32[72,128]{1,0:T(8,128)S(1)}, f32[72,128]{1,0:T(8,128)S(1)}, u32[]{:S(2)}, u32[]{:S(2)}) %collective-permute-start.16) | collective-permute-done | bytes 36896 | tf_op jit(solution)/shard_map/ppermute | solution.py:196
  35.9 1.2 %collective-permute-done.14 = f32[72,128]{1,0:T(8,128)S(1)} collective-permute-done((f32[72,128]{1,0:T(8,128)S(1)}, f32[72,128]{1,0:T(8,128)S(1)}, u32[]{:S(2)}, u32[]{:S(2)}) %collective-permute-start.14) | collective-permute-done | bytes 36896 | tf_op jit(solution)/shard_map/ppermute | solution.py:196
  37.1 0.1 collective-permute-start.17
  37.2 1.2 %collective-permute-done.17.theirs = f32[72,128]{1,0:T(8,128)S(1)} collective-permute-done((f32[72,128]{1,0:T(8,128)S(1)}, f32[72,128]{1,0:T(8,128)S(1)}, u32[]{:S(2)}, u32[]{:S(2)}) %collective-permute-start.17) | collective-permute-done | bytes 36896 | tf_op jit(solution)/shard_map/ppermute | solution.py:196
  38.4 1.9 %collective-permute-done.20.quarter = bf16[496,128]{1,0:T(8,128)(2,1)S(1)} collective-permute-done((bf16[496,128]{1,0:T(8,128)(2,1)S(1)}, bf16[496,128]{1,0:T(8,128)(2,1)S(1)}, u32[]{:S(2)}, u32[]{:S(2)}) %collective-permute-start.20) | collective-permute-done | bytes 127008 | tf_op jit(solution)/shard_map/ppermute | solution.py:196
  40.3 0.8 %shard_map.99 = (f32[128,128]{1,0:T(8,128)}, f32[1,128]{1,0:T(1,128)}, f32[496,128]{1,0:T(8,128)}) custom-call(f32[72,128]{1,0:T(8,128)S(1)} %add_add_fusion.mine, f32[72,128]{1,0:T(8,128)S(1)} %collective-permute-done.17.theirs, f32[496,128]{1,0:T(8,128)S(1)} %get-tuple-element.41.kept, bf16[496,128]{1,0:T(8,128)(2,1)S(1)} %collective-permute-done.18.direct, ...), custom_call_target="tpu_custom_call" | custom-call | tf_op jit(solution)/shard_map/pallas_call | solution.py:507
  (26 shorter events, 0.1 us)
Async XLA Ops:
  1.9 6.5 %collective-permute-start = (bf16[8,4,16,128]{3,2,1,0:T(8,128)(2,1)S(1)}, bf16[8,4,16,128]{3,2,1,0:T(8,128)(2,1)S(1)}, u32[]{:S(2)}, u32[]{:S(2)}) collective-permute-start(bf16[8,4,16,128]{3,2,1,0:T(8,128)(2,1)S(1)} %get-tuple-element.26.own.block.refs_0_), channel_id=1, source_target_pairs={{0,2},{2,0},{1,3},{3,1},{4,6},{6,4},{5,7},{7,5},{8,10},{10,8},{9,1... | collective-permute-start | bytes 393224 | tf_op jit(solution)/shard_map/ppermute | solution.py:196
  4.9 4.8 %collective-permute-start.1 = (bf16[4,4,16,128]{3,2,1,0:T(8,128)(2,1)S(1)}, bf16[4,4,16,128]{3,2,1,0:T(8,128)(2,1)S(1)}, u32[]{:S(2)}, u32[]{:S(2)}) collective-permute-start(bf16[4,4,16,128]{3,2,1,0:T(8,128)(2,1)S(1)} %get-tuple-element.27), channel_id=1, source_target_pairs={{0,4},{4,0},{8,12},{12,8},{1,5},{5,1},{9,13},{13,9},{2,6},{6,2},{1... | collective-permute-start | bytes 196616 | tf_op jit(solution)/shard_map/ppermute | solution.py:196
  6.5 5.2 %collective-permute-start.2 = (bf16[4,4,16,128]{3,2,1,0:T(8,128)(2,1)S(1)}, bf16[4,4,16,128]{3,2,1,0:T(8,128)(2,1)S(1)}, u32[]{:S(2)}, u32[]{:S(2)}) collective-permute-start(bf16[4,4,16,128]{3,2,1,0:T(8,128)(2,1)S(1)} %get-tuple-element.27), channel_id=1, source_target_pairs={{0,6},{2,4},{4,2},{6,0},{8,14},{10,12},{12,10},{14,8},{1,7},{3,5},... | collective-permute-start | bytes 196616 | tf_op jit(solution)/shard_map/ppermute | solution.py:196
  6.5 5.2 %collective-permute-start.3 = (bf16[4,4,16,128]{3,2,1,0:T(8,128)(2,1)S(1)}, bf16[4,4,16,128]{3,2,1,0:T(8,128)(2,1)S(1)}, u32[]{:S(2)}, u32[]{:S(2)}) collective-permute-start(bf16[4,4,16,128]{3,2,1,0:T(8,128)(2,1)S(1)} %get-tuple-element.28), channel_id=1, source_target_pairs={{0,1},{1,0},{4,8},{5,9},{8,4},{9,5},{12,13},{13,12},{2,3},{3,2},{6... | collective-permute-start | bytes 196616 | tf_op jit(solution)/shard_map/ppermute | solution.py:196
  6.5 5.7 %collective-permute-start.4 = (bf16[4,4,16,128]{3,2,1,0:T(8,128)(2,1)S(1)}, bf16[4,4,16,128]{3,2,1,0:T(8,128)(2,1)S(1)}, u32[]{:S(2)}, u32[]{:S(2)}) collective-permute-start(bf16[4,4,16,128]{3,2,1,0:T(8,128)(2,1)S(1)} %get-tuple-element.28), channel_id=1, source_target_pairs={{0,1},{1,0},{2,3},{3,2},{4,10},{5,11},{6,8},{7,9},{8,6},{9,7},{10,... | collective-permute-start | bytes 196616 | tf_op jit(solution)/shard_map/ppermute | solution.py:196
  8.4 3.9 %collective-permute-start.5 = (bf16[4,4,16,128]{3,2,1,0:T(8,128)(2,1)S(1)}, bf16[4,4,16,128]{3,2,1,0:T(8,128)(2,1)S(1)}, u32[]{:S(2)}, u32[]{:S(2)}) collective-permute-start(bf16[4,4,16,128]{3,2,1,0:T(8,128)(2,1)S(1)} %get-tuple-element.29), channel_id=1, source_target_pairs={{0,1},{1,0},{2,3},{3,2},{4,5},{5,4},{6,7},{7,6},{8,9},{9,8},{10,11... | collective-permute-start | bytes 196616 | tf_op jit(solution)/shard_map/ppermute | solution.py:196
  9.8 4.5 %collective-permute-start.6 = (bf16[4,4,16,128]{3,2,1,0:T(8,128)(2,1)S(1)}, bf16[4,4,16,128]{3,2,1,0:T(8,128)(2,1)S(1)}, u32[]{:S(2)}, u32[]{:S(2)}) collective-permute-start(bf16[4,4,16,128]{3,2,1,0:T(8,128)(2,1)S(1)} %slice.20), channel_id=1, source_target_pairs={{0,1},{1,0},{2,3},{3,2},{4,5},{5,4},{6,7},{7,6},{8,9},{9,8},{10,11... | collective-permute-start | bytes 196616 | tf_op jit(solution)/shard_map/ppermute | solution.py:196
  11.7 2.6 %collective-permute-start.7 = (bf16[2,4,16,128]{3,2,1,0:T(8,128)(2,1)S(1)}, bf16[2,4,16,128]{3,2,1,0:T(8,128)(2,1)S(1)}, u32[]{:S(2)}, u32[]{:S(2)}) collective-permute-start(bf16[2,4,16,128]{3,2,1,0:T(8,128)(2,1)S(1)} %slice.21), channel_id=1, source_target_pairs={{0,1},{1,0},{2,3},{3,2},{4,5},{5,4},{6,7},{7,6},{8,9},{9,8},{10,11... | collective-permute-start | bytes 98312 | tf_op jit(solution)/shard_map/ppermute | solution.py:196
  11.7 2.6 %collective-permute-start.8 = (bf16[2,4,16,128]{3,2,1,0:T(8,128)(2,1)S(1)}, bf16[2,4,16,128]{3,2,1,0:T(8,128)(2,1)S(1)}, u32[]{:S(2)}, u32[]{:S(2)}) collective-permute-start(bf16[2,4,16,128]{3,2,1,0:T(8,128)(2,1)S(1)} %slice.22), channel_id=1, source_target_pairs={{0,1},{1,0},{2,3},{3,2},{4,5},{5,4},{6,7},{7,6},{8,9},{9,8},{10,11... | collective-permute-start | bytes 98312 | tf_op jit(solution)/shard_map/ppermute | solution.py:196
  12.2 2.1 %collective-permute-start.9 = (bf16[2,4,16,128]{3,2,1,0:T(8,128)(2,1)S(1)}, bf16[2,4,16,128]{3,2,1,0:T(8,128)(2,1)S(1)}, u32[]{:S(2)}, u32[]{:S(2)}) collective-permute-start(bf16[2,4,16,128]{3,2,1,0:T(8,128)(2,1)S(1)} %slice.23), channel_id=1, source_target_pairs={{0,1},{1,0},{2,3},{3,2},{4,5},{5,4},{6,7},{7,6},{8,9},{9,8},{10,11... | collective-permute-start | bytes 98312 | tf_op jit(solution)/shard_map/ppermute | solution.py:196
  12.3 2.0 %collective-permute-start.10 = (bf16[2,4,16,128]{3,2,1,0:T(8,128)(2,1)S(1)}, bf16[2,4,16,128]{3,2,1,0:T(8,128)(2,1)S(1)}, u32[]{:S(2)}, u32[]{:S(2)}) collective-permute-start(bf16[2,4,16,128]{3,2,1,0:T(8,128)(2,1)S(1)} %slice.24), channel_id=1, source_target_pairs={{0,1},{1,0},{2,3},{3,2},{4,5},{5,4},{6,7},{7,6},{8,9},{9,8},{10,11... | collective-permute-start | bytes 98312 | tf_op jit(solution)/shard_map/ppermute | solution.py:196
  17.0 1.5 %collective-permute-start.11 = (bf16[6,8,16,128]{3,2,1,0:T(8,128)(2,1)S(1)}, bf16[6,8,16,128]{3,2,1,0:T(8,128)(2,1)S(1)}, u32[]{:S(2)}, u32[]{:S(2)}) collective-permute-start(bf16[6,8,16,128]{3,2,1,0:T(8,128)(2,1)S(1)} %get-tuple-element.30.grad.refs_12_), channel_id=1, source_target_pairs={{0,1},{1,0},{2,3},{3,2},{4,5},{5,4},{6,7},{7,6},{8,9},{9,8},{10,11... | collective-permute-start | bytes 589832 | tf_op jit(solution)/shard_map/ppermute | solution.py:196
  19.5 13.9 %collective-permute-start.19 = (bf16[496,128]{1,0:T(8,128)(2,1)S(1)}, bf16[496,128]{1,0:T(8,128)(2,1)S(1)}, u32[]{:S(2)}, u32[]{:S(2)}) collective-permute-start(bf16[496,128]{1,0:T(8,128)(2,1)S(1)} %get-tuple-element.44), channel_id=1, source_target_pairs={{0,4},{4,0},{8,12},{12,8},{1,5},{5,1},{9,13},{13,9},{2,6},{6,2},{1... | collective-permute-start | bytes 380936 | tf_op jit(solution)/shard_map/ppermute | solution.py:196
  24.7 1.2 %collective-permute-start.12 = (f32[72,128]{1,0:T(8,128)S(1)}, f32[72,128]{1,0:T(8,128)S(1)}, u32[]{:S(2)}, u32[]{:S(2)}) collective-permute-start(f32[72,128]{1,0:T(8,128)S(1)} %get-tuple-element.37), channel_id=1, source_target_pairs={{0,1},{1,0},{2,3},{3,2},{4,5},{5,4},{6,7},{7,6},{8,9},{9,8},{10,11... | collective-permute-start | bytes 110600 | tf_op jit(solution)/shard_map/ppermute | solution.py:196
  25.9 4.0 %collective-permute-start.13 = (f32[72,128]{1,0:T(8,128)S(1)}, f32[72,128]{1,0:T(8,128)S(1)}, u32[]{:S(2)}, u32[]{:S(2)}) collective-permute-start(f32[72,128]{1,0:T(8,128)S(1)} %add.18), channel_id=1, source_target_pairs={{0,2},{2,0},{1,3},{3,1},{4,6},{6,4},{5,7},{7,5},{8,10},{10,8},{9,1... | collective-permute-start | bytes 110600 | tf_op jit(solution)/shard_map/ppermute | solution.py:196
  27.4 9.7 %collective-permute-start.18 = (bf16[496,128]{1,0:T(8,128)(2,1)S(1)}, bf16[496,128]{1,0:T(8,128)(2,1)S(1)}, u32[]{:S(2)}, u32[]{:S(2)}) collective-permute-start(bf16[496,128]{1,0:T(8,128)(2,1)S(1)} %get-tuple-element.42), channel_id=1, source_target_pairs={{0,4},{4,0},{8,12},{12,8},{1,5},{5,1},{9,13},{13,9},{2,6},{6,2},{1... | collective-permute-start | bytes 380936 | tf_op jit(solution)/shard_map/ppermute | solution.py:196
  29.9 5.2 %collective-permute-start.15 = (f32[72,128]{1,0:T(8,128)S(1)}, f32[72,128]{1,0:T(8,128)S(1)}, u32[]{:S(2)}, u32[]{:S(2)}) collective-permute-start(f32[72,128]{1,0:T(8,128)S(1)} %add.19), channel_id=1, source_target_pairs={{0,8},{4,12},{8,0},{12,4},{1,9},{5,13},{9,1},{13,5},{2,10},{6,14},... | collective-permute-start | bytes 110600 | tf_op jit(solution)/shard_map/ppermute | solution.py:196
  30.0 5.9 %collective-permute-start.16 = (f32[72,128]{1,0:T(8,128)S(1)}, f32[72,128]{1,0:T(8,128)S(1)}, u32[]{:S(2)}, u32[]{:S(2)}) collective-permute-start(f32[72,128]{1,0:T(8,128)S(1)} %add.19), channel_id=1, source_target_pairs={{0,12},{4,8},{8,4},{12,0},{1,13},{5,9},{9,5},{13,1},{2,14},{6,10},... | collective-permute-start | bytes 110600 | tf_op jit(solution)/shard_map/ppermute | solution.py:196
  32.2 4.8 %collective-permute-start.14 = (f32[72,128]{1,0:T(8,128)S(1)}, f32[72,128]{1,0:T(8,128)S(1)}, u32[]{:S(2)}, u32[]{:S(2)}) collective-permute-start(f32[72,128]{1,0:T(8,128)S(1)} %add.19), channel_id=1, source_target_pairs={{0,4},{4,0},{8,12},{12,8},{1,5},{5,1},{9,13},{13,9},{2,6},{6,2},{1... | collective-permute-start | bytes 110600 | tf_op jit(solution)/shard_map/ppermute | solution.py:196
  33.4 6.9 %collective-permute-start.20 = (bf16[496,128]{1,0:T(8,128)(2,1)S(1)}, bf16[496,128]{1,0:T(8,128)(2,1)S(1)}, u32[]{:S(2)}, u32[]{:S(2)}) collective-permute-start(bf16[496,128]{1,0:T(8,128)(2,1)S(1)} %add_convert_fusion), channel_id=1, source_target_pairs={{0,12},{4,8},{8,4},{12,0},{1,13},{5,9},{9,5},{13,1},{2,14},{6,10},... | collective-permute-start | bytes 380936 | tf_op jit(solution)/shard_map/ppermute | solution.py:196
  37.1 1.3 %collective-permute-start.17 = (f32[72,128]{1,0:T(8,128)S(1)}, f32[72,128]{1,0:T(8,128)S(1)}, u32[]{:S(2)}, u32[]{:S(2)}) collective-permute-start(f32[72,128]{1,0:T(8,128)S(1)} %add_add_fusion.mine), channel_id=1, source_target_pairs={{0,1},{1,0},{2,3},{3,2},{4,5},{5,4},{6,7},{7,6},{8,9},{9,8},{10,11... | collective-permute-start | bytes 110600 | tf_op jit(solution)/shard_map/ppermute | solution.py:196
